TPU v7x, 256 devices: a whole 4x4x8 slice. The times are simulated.
256 devices in a mesh: samp: 8 (over x, z_hi), feat: 32 (over y, z_lo, core).
Axes of the slice: x: 4, y: 4, z: 8 (z_hi: 2, z_lo: 4; z = z_hi * 4 + z_lo), core: 2. Of those that a mesh axis runs over, the one named last changes fastest.
Arguments:
- embeddings: bfloat16 [8192, 1024], P('samp'), may hold values from -6 to 6
- frequencies: bfloat16 [1024, 8192], P(None, 'feat'), may hold values from -0.1875 to 0.1875
- phases: float32 [8192], P('feat'), may hold values from -3.140625 to 3.140625
- treat_freq: float32 [8192], P('feat'), may hold values from -3.140625 to 3.140625
- treatment: int32 [8192], P('samp'), may hold values from 0 to 1
- flips: int32 [8192], P('samp'), may hold values from 0 to 1
- panel: int32 [1], replicated, may hold values from 0 to 15
Outputs:
- schur: float32 [8192, 8192], P('samp', 'feat')
- panel_factor: float32 [8192, 512], P('samp')
- moment_scaled: float32 [8192], P('feat')
All inputs are finite; a program needn't handle non-finite values.
Results may differ from a plain program's by a relative error of at most 0.0032.
Values may be sent and summed in bfloat16 or wider, within the bound.
No kernel may reach another device: no remote copies, remote signals or barrier semaphores. Data moves between devices by JAX's collectives and lax.ppermute only.
A program may use at most 128 MiB of HBM per device.

v0:
```python
import jax
import jax.numpy as jnp
from jax import lax
from jax.sharding import PartitionSpec as P

PANEL = 512


ridge = 0.1
root_two = 1.4142135623730951


def broadcast(shard, axis, root):
    mine = lax.axis_index(axis) == root
    return lax.psum(jnp.where(mine, shard, jnp.zeros_like(shard)), axis)


def cosine_map(project, phases, treat_freq, treated):
    return root_two * jnp.cos(project + phases[None, :] + treated[:, None] * treat_freq[None, :])


def inner_rows(left, right):
    return lax.dot_general(
        left, right, (((0,), (0,)), ((), ())), preferred_element_type=jnp.float32
    )


def per_device(embeddings, frequencies, phases, treat_freq, treatment, flips, panel):
    project = jnp.dot(embeddings, frequencies, preferred_element_type=jnp.float32)
    treated = treatment.astype(jnp.float32)
    flipped = flips.astype(jnp.float32)
    counter = treated + flipped - 2.0 * treated * flipped
    observed = cosine_map(project, phases, treat_freq, treated)
    counterfactual = cosine_map(project, phases, treat_freq, counter)
    feature_obs = observed.astype(jnp.bfloat16)
    samp_size = lax.axis_size("samp")
    feat_size = lax.axis_size("feat")
    sample_count = embeddings.shape[0] * samp_size
    col_width = feature_obs.shape[1]
    feat_total = col_width * feat_size
    row_height = feat_total // samp_size
    samp_index = lax.axis_index("samp")
    feat_index = lax.axis_index("feat")
    moment_part = jnp.sum(counterfactual - observed, axis=0)
    moment_sum = lax.psum(moment_part, "samp") / sample_count
    first_col = panel[0] * PANEL
    panel_devs = PANEL // col_width
    first_dev = first_col // col_width
    gram_part = inner_rows(lax.all_gather(feature_obs, "feat", axis=1, tiled=True), feature_obs)
    gram_raw = lax.psum_scatter(gram_part, "samp", scatter_dimension=0, tiled=True)
    row_ids = samp_index * row_height + lax.broadcasted_iota(jnp.int32, (row_height, col_width), 0)
    col_ids = feat_index * col_width + lax.broadcasted_iota(jnp.int32, (row_height, col_width), 1)
    gram_own = gram_raw / sample_count + ridge * (row_ids == col_ids).astype(jnp.float32)
    col_parts = []
    moment_parts = []
    for member in range(panel_devs):
        got_cols, got_moment = (
            broadcast(gram_own, "feat", first_dev + member),
            broadcast(moment_sum, "feat", first_dev + member),
        )
        col_parts.append(got_cols)
        moment_parts.append(got_moment)
    panel_cols = jnp.concatenate(col_parts, axis=1)
    moment_panel = jnp.concatenate(moment_parts, axis=0)
    source_samp = first_col // row_height
    offset_row = first_col % row_height
    pivot_local = lax.dynamic_slice_in_dim(panel_cols, offset_row, PANEL, 0)
    cross_local = lax.dynamic_slice_in_dim(gram_own, offset_row, PANEL, 0)
    pivot, cross = (
        broadcast(pivot_local, "samp", source_samp),
        broadcast(cross_local, "samp", source_samp),
    )
    lower = jnp.linalg.cholesky(pivot)
    factor_t = lax.linalg.triangular_solve(lower, panel_cols.T, left_side=True, lower=True)
    panel_factor = factor_t.T
    cross_t = lax.linalg.triangular_solve(lower, cross, left_side=True, lower=True)
    schur = gram_own - jnp.dot(panel_factor, cross_t, precision=lax.Precision.HIGHEST)
    solved = lax.linalg.triangular_solve(lower, moment_panel[:, None], left_side=True, lower=True)[
        :, 0
    ]
    reduced = moment_sum - jnp.dot(cross_t.T, solved, precision=lax.Precision.HIGHEST)
    moment_scaled = jnp.sqrt(jnp.float32(sample_count)) * reduced
    return (schur, panel_factor, moment_scaled)


def solution(mesh):
    return jax.shard_map(
        per_device,
        mesh=mesh,
        in_specs=(
            P("samp", None),
            P(None, "feat"),
            P("feat"),
            P("feat"),
            P("samp"),
            P("samp"),
            P(),
        ),
        out_specs=(P("samp", "feat"), P("samp", None), P("feat")),
        check_vma=False,
    )
```

profile of v0, /device:TPU:1, one launch (start us, length us, event | category | flops | bytes accessed | tf_op | source)
XLA Modules:
  0.0 977.3 jit_solution(12588586258870872119)
XLA Ops:
  8.8 9.7 subtract_reduce_fusion
  18.5 127.9 %all-gather.2.cloned.1.call-done = bf16[1024,8192]{1,0:T(8,128)(2,1)} async-done(((bf16[1024,256]{1,0:T(8,128)(2,1)}), bf16[1024,8192]{1,0:T(8,128)(2,1)}) %all-gather.2.cloned.1.call-update) | async-done | bytes 16777232 | tf_op jit(solution)/shard_map/all_gather | solution.py:49
  146.4 13.7 %fusion.87 = f32[8192,256]{0,1:T(8,128)} fusion(bf16[1024,8192]{1,0:T(8,128)(2,1)} %all-gather.2.cloned.1.call-done, bf16[1024,256]{1,0:T(8,128)(2,1)} %get-tuple-element.37), kind=kOutput, calls=%fused_computation.148 | convolution fusion | flops 4294967296 | bytes 25690112 | tf_op jit(solution)/shard_map/dot_general | solution.py:23
  160.8 183.6 %reduce-scatter.2.cloned.1.call-done = f32[1024,256]{0,1:T(8,128)} async-done(((f32[8192,256]{0,1:T(8,128)}), f32[1024,256]{0,1:T(8,128)}) %reduce-scatter.2.cloned.1.call-update) | async-done | bytes 1048592 | tf_op jit(solution)/shard_map/reduce_scatter | solution.py:50
  344.5 2.4 broadcast_select_fusion
  349.3 277.2 %all-reduce.7.cloned.1.call-done = (f32[1024,256]{0,1:T(8,128)}, f32[1024,256]{0,1:T(8,128)}) async-done(((f32[1024,256]{0,1:T(8,128)}, f32[1024,256]{0,1:T(8,128)}), (f32[1024,256]{0,1:T(8,128)}, f32[1024,256]{0,1:T(8,128)})) %all-reduce.7.cloned.1.call-update) | async-done | bytes 2097168 | tf_op jit(solution)/shard_map/psum | solution.py:15
  626.4 1.4 constant_dynamic-update-slice_fusion.1
  630.7 26.3 %psum.53 = f32[256]{0:T(256)S(1)} all-reduce(f32[256]{0:T(256)S(1)} %get-tuple-element.36), channel_id=1, replica_groups=mesh['samp'=8,'feat'=32] {'samp'}, use_global_device_ids=true, to_apply=%region_14.15 | all-reduce | flops 256 | bytes 2048 | tf_op jit(solution)/shard_map/psum | solution.py:45
  657.0 79.7 %all-reduce.1 = (f32[256]{0:T(256)S(1)}, f32[256]{0:T(256)S(1)}) all-reduce(f32[256]{0:T(256)S(1)} %get-tuple-element.45, f32[256]{0:T(256)S(1)} %get-tuple-element.44), channel_id=1, replica_groups=mesh['samp'=8,'feat'=32] {'feat'}, use_global_device_ids=true, to_apply=%region_15.16 | all-reduce | flops 512 | bytes 4096 | tf_op jit(solution)/shard_map/psum | solution.py:15
  737.2 54.4 %all-reduce.9.cloned.1.call-done = (f32[512,512]{0,1:T(8,128)}, f32[512,256]{0,1:T(8,128)}) async-done(((f32[512,512]{0,1:T(8,128)}, f32[512,256]{0,1:T(8,128)}), (f32[512,512]{0,1:T(8,128)}, f32[512,256]{0,1:T(8,128)})) %all-reduce.9.cloned.1.call-update) | async-done | bytes 1572880 | tf_op jit(solution)/shard_map/psum | solution.py:15
  791.6 2.6 copy.11
  794.2 1.4 fusion.19
  796.7 11.7 %cholesky.103 = f32[128,128]{1,0:T(8,128)S(1)} custom-call(f32[128,128]{1,0:T(8,128)S(1)} %cholesky.263), custom_call_target="Cholesky" | custom-call | tf_op jit(solution)/shard_map/jit(cholesky)/cholesky | solution.py:73
  808.4 9.8 %custom-call.34 = f32[1,128,128]{1,2,0:T(8,128)S(1)} custom-call(f32[1,128,128]{2,1,0:T(8,128)S(1)} %get-tuple-element.43), custom_call_target="InvertDiagBlocksLowerTriangular" | custom-call | tf_op jit(solution)/shard_map/jit(cholesky)/cholesky | solution.py:73
  820.8 11.7 %cholesky.215 = f32[128,128]{1,0:T(8,128)S(1)} custom-call(f32[128,128]{1,0:T(8,128)S(1)} %cholesky.267), custom_call_target="Cholesky" | custom-call | tf_op jit(solution)/shard_map/jit(cholesky)/cholesky | solution.py:73
  834.6 10.8 %custom-call.35 = f32[1,128,128]{1,2,0:T(8,128)} custom-call(f32[1,128,128]{2,1,0:T(8,128)S(1)} %get-tuple-element.41), custom_call_target="InvertDiagBlocksLowerTriangular" | custom-call | tf_op jit(solution)/shard_map/jit(cholesky)/cholesky | solution.py:73
  848.4 1.5 convolution_subtract_fusion.6
  849.9 11.7 %cholesky.236 = f32[128,128]{1,0:T(8,128)S(1)} custom-call(f32[128,128]{1,0:T(8,128)S(1)} %cholesky.272), custom_call_target="Cholesky" | custom-call | tf_op jit(solution)/shard_map/jit(cholesky)/cholesky | solution.py:73
  861.8 9.8 %custom-call.36 = f32[1,128,128]{1,2,0:T(8,128)S(1)} custom-call(f32[1,128,128]{2,1,0:T(8,128)S(1)} %get-tuple-element.39), custom_call_target="InvertDiagBlocksLowerTriangular" | custom-call | tf_op jit(solution)/shard_map/jit(cholesky)/cholesky | solution.py:73
  873.2 11.9 %cholesky.253 = f32[128,128]{1,0:T(8,128)S(1)} custom-call(f32[128,128]{1,0:T(8,128)S(1)} %convolution_subtract_fusion.8), custom_call_target="Cholesky" | custom-call | tf_op jit(solution)/shard_map/jit(cholesky)/cholesky | solution.py:73
  891.4 14.1 %while.1 = (s32[]{:T(128)}, f32[512,512]{0,1:T(8,128)}, s32[4,2]{0,1:T(2,128)S(1)}, f32[4,128,128]{2,1,0:T(8,128)}, s32[]{:T(128)}) while((s32[]{:T(128)}, f32[512,512]{0,1:T(8,128)}, s32[4,2]{0,1:T(2,128)S(1)}, f32[4,128,128]{2,1,0:T(8,128)}, s32[]{:T(128)}) %tuple.32), condition=%wide.while_cond, body=%wide.while_body.sunk | while | flops 2 | bytes 393829 | solution.py:74
  892.0 2.2 dynamic-slice.7
  895.6 2.2 dynamic-slice.7
  899.1 2.2 dynamic-slice.7
  902.6 2.2 dynamic-slice.7
  905.5 40.2 %custom-call.37 = f32[4,128,128]{1,2,0:T(8,128)S(1)} custom-call(f32[4,128,128]{2,1,0:T(8,128)} %get-tuple-element.10), custom_call_target="InvertDiagBlocksLowerTriangular" | custom-call | tf_op jit(solution)/shard_map/triangular_solve | solution.py:74
  951.1 1.3 convolution_subtract_fusion.7
  952.7 1.6 convolution_subtract_fusion.5
  954.6 1.7 convolution_subtract_fusion.4
  961.8 1.6 fusion.9
  963.4 2.0 convolution_subtract_fusion
  966.4 2.9 copy.22
  (103 shorter events, 40.4 us)
Async XLA Ops:
  7.2 1.6 copy-start
  7.2 139.2 %all-gather.2.cloned.1.call-start = ((), (), s32[]{:S(2)}) async-start(), calls=%async_computation.1 | async-start | bytes 17301504 | tf_op jit(solution)/shard_map/all_gather | solution.py:49
  18.5 326.0 %reduce-scatter.2.cloned.1.call-start = ((), (), s32[]{:S(2)}) async-start(), calls=%async_computation.2 | async-start | bytes 9437184 | tf_op jit(solution)/shard_map/reduce_scatter | solution.py:50
  160.1 466.3 %all-reduce.7.cloned.1.call-start = ((), (), s32[]{:S(2)}) async-start(), calls=%async_computation.3 | async-start | bytes 4194304 | tf_op jit(solution)/shard_map/psum | solution.py:15
  346.9 1.3 copy-start.3
  348.1 443.5 %all-reduce.9.cloned.1.call-start = ((), (), s32[]{:S(2)}) async-start(), calls=%async_computation.4 | async-start | bytes 3145728 | tf_op jit(solution)/shard_map/psum | solution.py:15
  626.4 1.5 copy-start.8
  628.1 1.3 copy-start.1
  791.6 2.6 copy-start.6
  795.7 1.0 copy-start.7
  848.4 43.0 %copy-start.9 = (s32[4]{0:T(128)S(1)}, s32[4]{0:T(128)}, u32[]{:S(2)}) copy-start(s32[4]{0:T(128)} %iota_multiply_fusion) | copy-start | bytes 52
  905.5 49.1 %copy-start.5 = (f32[512,512]{0,1:T(8,128)S(1)}, f32[512,512]{0,1:T(8,128)}, u32[]{:S(2)}) copy-start(f32[512,512]{0,1:T(8,128)} %get-tuple-element.104) | copy-start | bytes 3145732
  945.8 10.9 %copy-start.2 = (f32[1024,512]{0,1:T(8,128)S(1)}, f32[1024,512]{0,1:T(8,128)}, u32[]{:S(2)}) copy-start(f32[1024,512]{0,1:T(8,128)} %copy-done.1) | copy-start | bytes 6291460
  961.8 1.6 copy-start.4
Sparse Core Ops, SparseCore 0:
  18.6 127.7 all-gather.1
  160.2 184.2 reduce-scatter.1
  348.2 278.1 all-reduce.6
  630.8 160.7 all-reduce.8
where the time goes:
time: 985 us; the launch traced here: 977 us
  waiting for transfers between devices  643 us (65%)
  other arithmetic  134 us (14%)
  blocking collectives  106 us (11%)
  matrix products  48.4 us (5%)
  local copies, waits for them, and re-layouts  28.5 us (3%)
  between operations  17.5 us (2%)
    psum x2, waiting for transfers between devices, broadcast(): return lax.psum(jnp.where(mine, shard, jnp.zeros_like(shard)), axis)  332 us
    reduce_scatter x1, waiting for transfers between devices, per_device(): lax.psum_scatter(gram_part, 'samp', scatter_dimension=0, tiled=True)  184 us
    all_gather x1, waiting for transfers between devices, per_device(): lax.all_gather(feature_obs, 'feat', axis=1, tiled=True)  128 us
    another operation x14, other arithmetic, per_device(): lower = jnp.linalg.cholesky(pivot)  80.7 us
    psum x1, blocking collectives, broadcast(): return lax.psum(jnp.where(mine, shard, jnp.zeros_like(shard)), axis)  79.7 us
    another operation x3, other arithmetic, per_device(): lax.linalg.triangular_solve(lower, panel_cols.T, left_side=True, lower=True)  41.9 us
    psum x1, blocking collectives, per_device(): moment_sum = lax.psum(moment_part, 'samp') / sample_count  26.3 us
  transfers between devices with their start and end apart: 4, of which 4 were waited for; matrix products, arithmetic and copies ran while one was open for 0% of the time, Pallas kernels for 0%

commit v1 on v0

v1 whole, which is shorter than its diff:
```python
import jax
import jax.numpy as jnp
from jax import lax
from jax.experimental import pallas as pl
from jax.experimental.pallas import tpu as pltpu
from jax.sharding import Mesh
from jax.sharding import PartitionSpec as P

PANEL = 512
ridge = 0.1
f32 = jnp.float32
bf16 = jnp.bfloat16
HIGHEST = lax.Precision.HIGHEST

SAMP = ("x", "zh")
FEAT = ("y", "zl", "core")

SINE = (
    -8.885765875337938,
    58.46599556065702,
    -115.4071939365197,
    108.47536728137668,
    -59.39695452559278,
    20.275610646954046,
)


def cosine(x):
    turns = x * 0.15915494309189535
    s = jnp.abs(turns - jnp.round(turns)) - 0.25
    u = s * s
    p = SINE[5]
    for c in SINE[4::-1]:
        p = p * u + c
    return s * p


def dot(left, right, dims, **kw):
    return lax.dot_general(left, right, (dims, ((), ())), preferred_element_type=f32, **kw)


def gram_body(zh_ref, all_ref, near_ref, far_ref, own_ref, panel_ref, pivot_ref):
    step = pl.program_id(0)
    imps = near_ref.shape[1]
    width = near_ref.shape[2]
    blocks = all_ref.shape[2]
    row_blocks = blocks - PANEL // width

    @pl.when(step == 0)
    def _():
        own_ref[...] = jnp.zeros_like(own_ref)
        panel_ref[...] = jnp.zeros_like(panel_ref)
        pivot_ref[...] = jnp.zeros_like(pivot_ref)

    mine = jnp.where(step % 2 == zh_ref[0], near_ref[0], far_ref[0])
    block = [all_ref[:, 0, b].reshape(imps, width) for b in range(blocks)]
    elim = jnp.concatenate(block[row_blocks:], axis=1)
    mine_t = mine.T
    elim_t = elim.T
    for b in range(blocks):
        at = slice(b * width, (b + 1) * width)
        own_ref[:, at] += dot(mine_t, block[b], ((1,), (0,)))
        if b < row_blocks:
            panel_ref[:, at] += dot(elim_t, block[b], ((1,), (0,)))
    pivot_ref[...] += dot(elim_t, elim, ((1,), (0,)))


def gram_sums(zh, gathered, near, far):
    feat, samp, blocks, piece, width = gathered.shape
    imps = near.shape[1]
    rows = blocks * width - PANEL
    return pl.pallas_call(
        gram_body,
        out_shape=(
            jax.ShapeDtypeStruct((width, blocks * width), f32),
            jax.ShapeDtypeStruct((PANEL, rows), f32),
            jax.ShapeDtypeStruct((PANEL, PANEL), f32),
        ),
        grid_spec=pltpu.PrefetchScalarGridSpec(
            num_scalar_prefetch=1,
            grid=(samp,),
            in_specs=[
                pl.BlockSpec(
                    (feat, 1, blocks, piece, width),
                    lambda i, zh_ref: (0, i, 0, 0, 0),
                ),
                pl.BlockSpec((1, imps, width), lambda i, zh_ref: (i // 2, 0, 0)),
                pl.BlockSpec((1, imps, width), lambda i, zh_ref: (i // 2, 0, 0)),
            ],
            out_specs=[
                pl.BlockSpec((width, blocks * width), lambda i, zh_ref: (0, 0)),
                pl.BlockSpec((PANEL, rows), lambda i, zh_ref: (0, 0)),
                pl.BlockSpec((PANEL, PANEL), lambda i, zh_ref: (0, 0)),
            ],
        ),
        compiler_params=pltpu.CompilerParams(vmem_limit_bytes=50 << 20),
        name="gram_sums",
    )(zh, gathered, near, far)


def invert_body(a_ref, out_ref, work, diag):
    n = a_ref.shape[0]
    nb = 128
    work[:, :n] = a_ref[...]
    row = lax.broadcasted_iota(jnp.int32, (n, n), 0)
    col = lax.broadcasted_iota(jnp.int32, (n, n), 1)
    work[:, n:] = (row == col).astype(f32)
    sub = lax.broadcasted_iota(jnp.int32, (8, nb), 0)
    lane = lax.broadcasted_iota(jnp.int32, (8, nb), 1)
    eye = (
        lax.broadcasted_iota(jnp.int32, (nb, nb), 0) == lax.broadcasted_iota(jnp.int32, (nb, nb), 1)
    ).astype(f32)
    for lo in range(0, n, nb):
        hi = lo + nb
        diag[:, :nb] = work[lo:hi, lo:hi]
        diag[:, nb:] = eye
        for q in range(0, nb, 8):
            ra = diag[q : q + 8, :nb]
            rb = diag[q : q + 8, nb:]
            cols = [jnp.broadcast_to(ra[:, q + c : q + c + 1], (8, nb)) for c in range(8)]
            pivots = jnp.ones((8, nb), f32)
            for c in range(8):
                d = jnp.broadcast_to(cols[c][c : c + 1, :], (8, nb))
                pivots = jnp.where(sub == c, d, pivots)
                if c < 7:
                    mult = jnp.where(sub > c, cols[c] / d, 0.0)
                    for e in range(c + 1, 8):
                        cols[e] = cols[e] - mult * jnp.broadcast_to(cols[e][c : c + 1, :], (8, nb))
                    ra = ra - mult * jnp.broadcast_to(ra[c : c + 1, :], (8, nb))
                    rb = rb - mult * jnp.broadcast_to(rb[c : c + 1, :], (8, nb))
            scale = lax.rsqrt(pivots)
            ra = ra * scale
            rb = rb * scale
            diag[q : q + 8, nb:] = rb
            if q + 8 < nb:
                low = jnp.where(lane >= q + 8, ra, 0.0)
                update = dot(low, jnp.concatenate([low, rb], 1), ((0,), (0,)), precision=HIGHEST)
                diag[q + 8 :, :] = diag[q + 8 :, :] - update[q + 8 :, :]
        upper = dot(diag[:, nb:], work[lo:hi, hi : n + hi], ((1,), (0,)), precision=HIGHEST)
        rest = n - hi
        out_ref[lo:hi, :hi] = upper[:, rest:]
        if rest:
            work[hi:, hi : n + hi] = work[hi:, hi : n + hi] - dot(
                upper[:, :rest], upper, ((0,), (0,)), precision=HIGHEST
            )
            out_ref[lo:hi, hi:] = jnp.zeros((nb, rest), f32)


def inverse_factor(pivot):
    n = pivot.shape[0]
    return pl.pallas_call(
        invert_body,
        out_shape=jax.ShapeDtypeStruct((n, n), f32),
        scratch_shapes=[pltpu.VMEM((n, 2 * n), f32), pltpu.VMEM((128, 256), f32)],
        compiler_params=pltpu.CompilerParams(vmem_limit_bytes=32 << 20),
        name="inverse_factor",
    )(pivot)


def finish_body(count, at_ref, own_ref, panel_ref, inv_ref, m_ref, mk_ref, schur_ref, factor_ref, red_ref):
    row0, col0, first = at_ref[0], at_ref[1], at_ref[2]
    scale = 1.0 / count
    rows = panel_ref.shape[1]
    width = own_ref.shape[0]

    def diagonal(shape, r0, c0):
        r = r0 + lax.broadcasted_iota(jnp.int32, shape, 0)
        c = c0 + lax.broadcasted_iota(jnp.int32, shape, 1)
        return jnp.where(r == c, ridge, 0.0)

    inv = inv_ref[...]
    panel = panel_ref[...].T * scale + diagonal((rows, PANEL), row0, first)
    factor = dot(panel, inv, ((1,), (1,)), precision=HIGHEST)
    factor_ref[...] = factor
    cross = own_ref[:, rows:] * scale + diagonal((width, PANEL), col0, first)
    cross = dot(cross, inv, ((1,), (1,)), precision=HIGHEST)
    gram = own_ref[:, :rows].T * scale + diagonal((rows, width), row0, col0)
    schur_ref[...] = gram - dot(factor, cross, ((1,), (1,)), precision=HIGHEST)
    solved = dot(mk_ref[...], inv, ((1,), (1,)), precision=HIGHEST)
    reduced = m_ref[...] - dot(solved, cross, ((1,), (1,)), precision=HIGHEST)
    red_ref[...] = reduced * (count**0.5)


def finish(count, at, own, panel, inv, m, mk):
    width = own.shape[0]
    rows = panel.shape[1]
    vmem = pl.BlockSpec(memory_space=pltpu.VMEM)
    return pl.pallas_call(
        lambda *refs: finish_body(count, *refs),
        out_shape=(
            jax.ShapeDtypeStruct((rows, width), f32),
            jax.ShapeDtypeStruct((rows, PANEL), f32),
            jax.ShapeDtypeStruct((1, width), f32),
        ),
        in_specs=[pl.BlockSpec(memory_space=pltpu.SMEM)] + [vmem] * 5,
        out_specs=[vmem] * 3,
        compiler_params=pltpu.CompilerParams(vmem_limit_bytes=50 << 20),
        name="finish",
    )(at, own, panel, inv, m, mk)


def per_device(embeddings, frequencies, phases, treat_freq, treatment, flips, panel):
    imps = embeddings.shape[0]
    width = frequencies.shape[1]
    samp = lax.axis_size(SAMP)
    feat = lax.axis_size(FEAT)
    samp_index = lax.axis_index(SAMP)
    feat_index = lax.axis_index(FEAT)
    count = imps * samp
    rows = width * feat // samp
    piece = imps // feat
    elim = PANEL // width

    project = jnp.dot(embeddings, frequencies, preferred_element_type=f32)
    treated = treatment.astype(f32)
    flipped = flips.astype(f32)
    counter = treated + flipped - 2.0 * treated * flipped
    base = project + phases[None, :]
    observed = cosine(base + treated[:, None] * treat_freq[None, :])
    counterfactual = cosine(base + counter[:, None] * treat_freq[None, :])
    moment_part = jnp.sum(counterfactual - observed, axis=0)
    feature = observed.astype(bf16)

    swapped = lax.ppermute(feature, "zh", [(0, 1), (1, 0)])
    near = lax.all_gather(feature, "x")
    far = lax.all_gather(swapped, "x")

    shares = lax.all_to_all(
        feature.reshape(feat, piece, width), FEAT, split_axis=0, concat_axis=0, tiled=True
    )
    first_dev = panel[0] * elim
    picked = lax.dynamic_slice_in_dim(shares, first_dev, elim, 0)
    send = jnp.concatenate(
        [
            shares.reshape(samp, feat // samp, piece, width),
            jnp.broadcast_to(picked[None], (samp, elim, piece, width)),
        ],
        axis=1,
    )
    share = lax.all_to_all(send, SAMP, split_axis=0, concat_axis=0, tiled=True)
    gathered = lax.all_gather(share, FEAT)

    share, moment_part = lax.optimization_barrier((share, moment_part))
    moment = lax.psum(moment_part, SAMP) / count
    moments = lax.all_gather(lax.all_gather(moment, ("zl", "core")), "y").reshape(-1)
    moment_panel = lax.dynamic_slice_in_dim(moments, panel[0] * PANEL, PANEL, 0)

    zh = lax.axis_index("zh").astype(jnp.int32)[None]
    own, panel_sum, pivot_sum = gram_sums(zh, gathered, near, far)
    pivot = pivot_sum / count + ridge * jnp.eye(PANEL, dtype=f32)
    inv = inverse_factor(pivot)
    at = jnp.stack([samp_index * rows, feat_index * width, panel[0] * PANEL]).astype(jnp.int32)
    schur, factor, reduced = finish(
        count, at, own, panel_sum, inv, moment[None], moment_panel[None]
    )
    return (schur, factor, reduced[0])


def solution(mesh):
    fine = Mesh(mesh.devices.reshape(4, 2, 4, 4, 2), ("x", "zh", "y", "zl", "core"))
    return jax.shard_map(
        per_device,
        mesh=fine,
        in_specs=(P(SAMP, None), P(None, FEAT), P(FEAT), P(FEAT), P(SAMP), P(SAMP), P()),
        out_specs=(P(SAMP, FEAT), P(SAMP, None), P(FEAT)),
        check_vma=False,
    )
```

time: 985 us -> 319 us (0.32)
  waiting for transfers between devices: 643 us -> 124 us
  other arithmetic: 134 us -> 1.82 us
  Pallas kernels: 0 us -> 72.6 us
  matrix products: 48.4 us -> 3.84 us
  blocking collectives: 106 us -> 76.6 us
  local copies, waits for them, and re-layouts: 28.5 us -> 0.94 us
  starting transfers between devices: 0.16 us -> 24.8 us
    psum x2 -> x0, waiting for transfers between devices: 332 us -> none  [broadcast(): return lax.psum(jnp.where(mine, shard, jnp.zeros_like(shard)), axis)]
    reduce_scatter x1 -> x0, waiting for transfers between devices: 184 us -> none  [per_device(): lax.psum_scatter(gram_part, 'samp', scatter_dimension=0, tiled=True)]
    another operation x17 -> x1, other arithmetic: 123 us -> 0.08 us  [per_device(): jnp.stack([samp_index * rows, feat_index * width, panel[0] * PANEL])]
    psum x2 -> x1, blocking collectives: 106 us -> 20.7 us  [per_device(): moment = lax.psum(moment_part, SAMP) / count]
    pallas_call x0 -> x3, Pallas kernels: none -> 72.6 us  [the longest x1 37.2 us: inverse_factor(): pl.pallas_call(invert_body, out_shape=jax.ShapeDtypeStruct((n, n), f32),...]
    all_gather x1 -> x3, waiting for transfers between devices: 128 us -> 94.1 us  [the longest x1 94.1 us: per_device(): gathered = lax.all_gather(share, FEAT)]
    all_to_all x0 -> x1, blocking collectives: none -> 30.2 us  [per_device(): share = lax.all_to_all(send, SAMP, split_axis=0, concat_axis=0, tiled=True)]
    all_gather x0 -> x2, blocking collectives: none -> 25.6 us  [the longest x1 16.6 us: per_device(): lax.all_gather(moment, ('zl', 'core'))]
  transfers between devices with their start and end apart: 4 -> 5, of which waited for: 4 -> 3; matrix products, arithmetic and copies ran while one was open for 0% -> 0% of each run, Pallas kernels for 0% -> 0%
where the time goes in v1:
time: 319 us
  waiting for transfers between devices  124 us (39%)
  blocking collectives  76.6 us (24%)
  Pallas kernels  72.6 us (23%)
  starting transfers between devices  24.8 us (8%)
  between operations  14.5 us (5%)
  matrix products  3.84 us (1%)
    all_gather x1, waiting for transfers between devices, per_device(): gathered = lax.all_gather(share, FEAT)  94.1 us
    pallas_call x1, Pallas kernels, inverse_factor(): pl.pallas_call(invert_body, out_shape=jax.ShapeDtypeStruct((n, n), f32),...  37.2 us
    all_to_all x1, blocking collectives, per_device(): share = lax.all_to_all(send, SAMP, split_axis=0, concat_axis=0, tiled=True)  30.2 us
    pallas_call x1, Pallas kernels, gram_sums(): pl.pallas_call(gram_body, out_shape=(jax.ShapeDtypeStruct((width, blocks...  24.9 us
    psum x1, blocking collectives, per_device(): moment = lax.psum(moment_part, SAMP) / count  20.7 us
    all_to_all x1, starting transfers between devices, per_device(): lax.all_to_all(feature.reshape(feat, piece, width), FEAT, split_axis=0, c...  16.9 us
    all_gather x1, blocking collectives, per_device(): lax.all_gather(moment, ('zl', 'core'))  16.6 us
    all_to_all x1, waiting for transfers between devices, per_device(): lax.all_to_all(feature.reshape(feat, piece, width), FEAT, split_axis=0, c...  16.1 us
  transfers between devices with their start and end apart: 5, of which 3 were waited for; matrix products, arithmetic and copies ran while one was open for 0% of the time, Pallas kernels for 0%

profile of v1, /device:TPU:1, one launch (start us, length us, event | category | flops | bytes accessed | tf_op | source)
XLA Modules:
  0.0 318.7 jit_solution(7020047763913257693)
XLA Ops:
  7.2 0.0 copy-start
  7.2 0.0 all-gather.12.cloned.1.call-start
  7.2 0.8 convert_element_type.10
  8.1 0.7 multiply_subtract_fusion
  8.8 0.0 copy-done
  8.8 3.8 %subtract_reduce_fusion = (f32[256]{0:T(256)S(1)}, bf16[1024,256]{1,0:T(8,128)(2,1)}) fusion(f32[1024]{0:T(1024)S(1)} %multiply_subtract_fusion, f32[256]{0:T(256)} %param.10, f32[1024]{0:T(1024)S(1)} %convert_element_type.10, f32[256]{0:T(256)} %param.9, bf16[1024,1024]{1,0:T(8,128)(2,1)S(1)} %copy-done, bf16[1024,256]{1,0:T(8,128)(2,1)} %param.8), kind=kOutput, calls=%fused_computation.7 | convolution fusion | flops 547880704 | bytes 3156992 | tf_op jit(solution)/shard_map/dot_general | solution.py:214
  12.6 0.0 all-gather.12.cloned.1.call-update
  12.6 0.0 all-gather.14.cloned.1.call-start
  12.7 7.8 %collective-permute-start = (bf16[1024,256]{1,0:T(8,128)(2,1)}, bf16[1024,256]{1,0:T(8,128)(2,1)S(1)}, u32[]{:S(2)}, u32[]{:S(2)}) collective-permute-start(bf16[1024,256]{1,0:T(8,128)(2,1)} %get-tuple-element.18), channel_id=1, source_target_pairs={{0,32},{32,0},{1,33},{33,1},{2,34},{34,2},{3,35},{35,3},{4,36},{36... | collective-permute-start | bytes 1572872 | tf_op jit(solution)/shard_map/ppermute | solution.py:224
  20.5 13.4 %collective-permute-done = bf16[1024,256]{1,0:T(8,128)(2,1)S(1)} collective-permute-done((bf16[1024,256]{1,0:T(8,128)(2,1)}, bf16[1024,256]{1,0:T(8,128)(2,1)S(1)}, u32[]{:S(2)}, u32[]{:S(2)}) %collective-permute-start) | collective-permute-done | bytes 524320 | tf_op jit(solution)/shard_map/ppermute | solution.py:224
  33.9 0.0 copy-start.1
  33.9 0.8 copy-done.1
  34.7 0.0 all-gather.14.cloned.1.call-update
  34.8 16.9 %all-to-all-start = ((bf16[32,32,256]{2,1,0:T(8,128)(2,1)}), bf16[32,32,256]{2,1,0:T(8,128)(2,1)S(1)}, u32[]{:S(2)}, u32[]{:S(2)}) async-start(bf16[32,32,256]{2,1,0:T(8,128)(2,1)} %bitcast.26), calls=%async_computation | async-start | bytes 1048576 | tf_op jit(solution)/shard_map/all_to_all | solution.py:228
  51.6 0.0 all-gather.10.cloned.1.call-start
  52.3 16.1 %all-to-all-done = bf16[32,32,256]{2,1,0:T(8,128)(2,1)S(1)} async-done(((bf16[32,32,256]{2,1,0:T(8,128)(2,1)}), bf16[32,32,256]{2,1,0:T(8,128)(2,1)S(1)}, u32[]{:S(2)}, u32[]{:S(2)}) %all-to-all-start) | async-done | bytes 524320 | tf_op jit(solution)/shard_map/all_to_all | solution.py:228
  68.5 0.1 pad_maximum_fusion
  68.6 30.2 %all_to_all.10 = bf16[8,6,32,256]{3,2,1,0:T(8,128)(2,1)} all-to-all(bf16[8,6,32,256]{3,2,1,0:T(8,128)(2,1)S(1)} %pad_maximum_fusion), channel_id=1, replica_groups=mesh['x'=4,'zh'=2,'y'=4,'zl'=4,'core'=2] {'x','zh'}, dimensions={0} | all-to-all | bytes 1572864 | tf_op jit(solution)/shard_map/all_to_all | solution.py:240
  98.8 0.0 all-gather.10.cloned.1.call-update
  98.8 0.1 pad_add_fusion.refs_0_
  98.9 20.7 %psum.7 = f32[256]{0:T(256)S(1)} all-reduce(f32[256]{0:T(256)S(1)} %get-tuple-element.13), channel_id=1, replica_groups=mesh['x'=4,'zh'=2,'y'=4,'zl'=4,'core'=2] {'x','zh'}, use_global_device_ids=true, to_apply=%region_1.2 | all-reduce | flops 256 | bytes 2048 | tf_op jit(solution)/shard_map/psum | solution.py:244
  119.6 16.6 %all-gather.5 = f32[8,1,256]{2,1,0:T(1,128)S(1)} all-gather(f32[1,1,256]{2,1,0:T(1,128)S(1)} %bitcast.21), channel_id=5, replica_groups=mesh['x'=4,'zh'=2,'y'=4,'zl'=4,'core'=2] {'zl','core'}, dimensions={0}, use_global_device_ids=true | all-gather | bytes 9216 | tf_op jit(solution)/shard_map/all_gather | solution.py:245
  136.3 9.0 %all-gather.4 = f32[32,256]{1,0:T(8,128)S(1)} all-gather(f32[8,256]{1,0:T(8,128)S(1)} %bitcast.31), channel_id=6, replica_groups=mesh['x'=4,'zh'=2,'y'=4,'zl'=4,'core'=2] {'y'}, dimensions={0}, use_global_device_ids=true | all-gather | bytes 40960 | tf_op jit(solution)/shard_map/all_gather | solution.py:245
  145.3 0.1 dynamic_slice.7
  145.4 0.0 all-gather.12.cloned.1.call-done
  145.4 0.0 all-gather.14.cloned.1.call-done
  145.4 94.1 %all-gather.10.cloned.1.call-done = bf16[256,6,32,256]{3,2,1,0:T(8,128)(2,1)} async-done(((bf16[8,6,32,256]{3,2,1,0:T(8,128)(2,1)}), bf16[256,6,32,256]{3,2,1,0:T(8,128)(2,1)}) %all-gather.10.cloned.1.call-update) | async-done | bytes 25165840 | tf_op jit(solution)/shard_map/all_gather | solution.py:241
  239.4 24.9 %gram_sums.1 = (f32[256,1536]{1,0:T(8,128)S(1)}, f32[512,1024]{1,0:T(8,128)}, f32[512,512]{1,0:T(8,128)S(1)}) custom-call(s32[1]{0:T(128)} %bitcast.2.zh_ref, bf16[32,8,6,32,256]{4,3,2,1,0:T(8,128)(2,1)} %bitcast.24, bf16[4,1024,256]{2,1,0:T(8,128)(2,1)} %bitcast.27, bf16[4,1024,256]{2,1,0:T(8,128)(2,1)} %bitcast.28), custom_call_target="tpu_custom_call" | custom-call | tf_op jit(solution)/shard_map/gram_sums/pallas_call | solution.py:72
  264.3 0.1 select_add_fusion.a_ref
  264.5 37.2 %inverse_factor.1.refs_3_ = f32[512,512]{1,0:T(8,128)S(1)} custom-call(f32[512,512]{1,0:T(8,128)S(1)} %select_add_fusion.a_ref), custom_call_target="tpu_custom_call" | custom-call | tf_op jit(solution)/shard_map/inverse_factor/pallas_call | solution.py:151
  301.7 10.5 %finish.1 = (f32[1024,256]{1,0:T(8,128)}, f32[1024,512]{1,0:T(8,128)}, f32[1,256]{1,0:T(1,128)}) custom-call(s32[3]{0:T(128)S(1)} %pad_add_fusion.refs_0_, f32[256,1536]{1,0:T(8,128)S(1)} %get-tuple-element.10.refs_1_, f32[512,1024]{1,0:T(8,128)} %get-tuple-element.11.refs_2_, f32[512,512]{1,0:T(8,128)S(1)} %inverse_factor.1.refs_3_, f32[1,256]{1,0:T(1,128)S(1)} %bitcast.22, ...), custom_call_target="tpu_custom_call" | custom-call | tf_op jit(solution)/shard_map/finish/pallas_call | solution.py:188
  (5 shorter events, 0.0 us)
Async XLA Ops:
  7.2 1.6 copy-start
  7.2 138.2 %all-gather.12.cloned.1.call-start = ((), (), s32[]{:S(2)}) async-start(), calls=%async_computation.3 | async-start | bytes 2621440 | tf_op jit(solution)/shard_map/all_gather | solution.py:225
  12.6 132.7 %all-gather.14.cloned.1.call-start = ((), (), s32[]{:S(2)}) async-start(), calls=%async_computation.4 | async-start | bytes 2621440 | tf_op jit(solution)/shard_map/all_gather | solution.py:226
  12.7 21.2 %collective-permute-start = (bf16[1024,256]{1,0:T(8,128)(2,1)}, bf16[1024,256]{1,0:T(8,128)(2,1)S(1)}, u32[]{:S(2)}, u32[]{:S(2)}) collective-permute-start(bf16[1024,256]{1,0:T(8,128)(2,1)} %get-tuple-element.18), channel_id=1, source_target_pairs={{0,32},{32,0},{1,33},{33,1},{2,34},{34,2},{3,35},{35,3},{4,36},{36... | collective-permute-start | bytes 1572872 | tf_op jit(solution)/shard_map/ppermute | solution.py:224
  33.9 0.8 copy-start.1
  34.8 33.7 %all-to-all-start = ((bf16[32,32,256]{2,1,0:T(8,128)(2,1)}), bf16[32,32,256]{2,1,0:T(8,128)(2,1)S(1)}, u32[]{:S(2)}, u32[]{:S(2)}) async-start(bf16[32,32,256]{2,1,0:T(8,128)(2,1)} %bitcast.26), calls=%async_computation | async-start | bytes 1048576 | tf_op jit(solution)/shard_map/all_to_all | solution.py:228
  51.6 187.8 %all-gather.10.cloned.1.call-start = ((), (), s32[]{:S(2)}) async-start(), calls=%async_computation.2 | async-start | bytes 25952256 | tf_op jit(solution)/shard_map/all_gather | solution.py:241
Sparse Core Ops, SparseCore 0:
  12.8 37.1 all-gather.11
  52.3 38.3 all-gather.13
  98.9 140.4 all-gather.9

commit v2 on v1

v2 whole, which is shorter than its diff:
```python
import jax
import jax.numpy as jnp
from jax import lax
from jax.experimental import pallas as pl
from jax.experimental.pallas import tpu as pltpu
from jax.sharding import Mesh
from jax.sharding import PartitionSpec as P

PANEL = 512
ridge = 0.1
f32 = jnp.float32
bf16 = jnp.bfloat16
HIGHEST = lax.Precision.HIGHEST

SAMP = ("x", "zh")
FEAT = ("y", "zl", "core")

SINE = (
    -8.885765875337938,
    58.46599556065702,
    -115.4071939365197,
    108.47536728137668,
    -59.39695452559278,
    20.275610646954046,
)


def cosine(x):
    turns = x * 0.15915494309189535
    s = jnp.abs(turns - jnp.round(turns)) - 0.25
    u = s * s
    p = SINE[5]
    for c in SINE[4::-1]:
        p = p * u + c
    return s * p


def dot(left, right, dims, **kw):
    return lax.dot_general(left, right, (dims, ((), ())), preferred_element_type=f32, **kw)


def split(a):
    high = a.astype(bf16)
    return high, (a - high.astype(f32)).astype(bf16)


def dot3(left, right, dims):
    lh, ll = left
    rh, rl = right
    return dot(lh, rh, dims) + (dot(lh, rl, dims) + dot(ll, rh, dims))


NT = ((1,), (1,))


def gram_body(
    count, at_ref, all_ref, near_ref, far_ref, inv_ref, schur_ref, factor_ref, red_ref, own, panel, mom
):
    step = pl.program_id(0)
    imps = near_ref.shape[1]
    width = near_ref.shape[2]
    feat = all_ref.shape[0]
    piece = imps // feat
    rows = panel.shape[1]
    row_blocks = rows // width
    blocks = row_blocks + PANEL // width

    @pl.when(step == 0)
    def _():
        own[...] = jnp.zeros_like(own)
        panel[...] = jnp.zeros_like(panel)
        mom[...] = jnp.zeros_like(mom)

    mine = jnp.where(step % 2 == at_ref[3], near_ref[0], far_ref[0])
    block = [
        all_ref[:, 0, b * piece : (b + 1) * piece, :].reshape(imps, width) for b in range(blocks)
    ]
    mine_t = mine.T
    elim_t = jnp.concatenate(block[row_blocks:], axis=1).T
    for b in range(blocks):
        at = slice(b * width, (b + 1) * width)
        own[:, at] += dot(mine_t, block[b], ((1,), (0,)))
        if b < row_blocks:
            panel[:, at] += dot(elim_t, block[b], ((1,), (0,)))
    mom[...] += jnp.sum(all_ref[:, 0, blocks * piece :, :].astype(f32), axis=1)

    @pl.when(step == pl.num_programs(0) - 1)
    def _():
        row0, col0, first = at_ref[0], at_ref[1], at_ref[2]
        scale = 1.0 / count

        def diagonal(shape, r0, c0):
            r = r0 + lax.broadcasted_iota(jnp.int32, shape, 0)
            c = c0 + lax.broadcasted_iota(jnp.int32, shape, 1)
            return jnp.where(r == c, ridge, 0.0)

        inv = split(inv_ref[...])
        cross = own[:, rows:] * scale + diagonal((width, PANEL), col0, first)
        cross = dot3(split(cross), inv, NT)
        cross_parts = split(cross)
        for lo in range(0, rows, width):
            at = slice(lo, lo + width)
            cols = panel[:, at].T * scale + diagonal((width, PANEL), row0 + lo, first)
            factor = dot3(split(cols), inv, NT)
            factor_ref[at, :] = factor
            gram = own[:, at].T * scale + diagonal((width, width), row0 + lo, col0)
            schur_ref[at, :] = gram - dot3(split(factor), cross_parts, NT)
        own_dev = at_ref[4]
        first_dev = at_ref[5]
        picked = [mom[pl.ds(first_dev + k, 1), :] * scale for k in range(PANEL // width)]
        elim = jnp.broadcast_to(jnp.concatenate(picked, axis=1), (8, PANEL))
        solved = dot(elim, inv_ref[...], NT, precision=HIGHEST)
        part = dot(solved, cross, NT, precision=HIGHEST)
        reduced = mom[pl.ds(own_dev, 1), :] * scale - part[:1]
        red_ref[...] = reduced * (count**0.5)


def gram_schur(count, at, gathered, near, far, inv):
    feat, samp, held, width = gathered.shape
    imps = near.shape[1]
    rows = width * feat // samp
    fixed = lambda i, at_ref: (0, 0)
    return pl.pallas_call(
        lambda *refs: gram_body(count, *refs),
        out_shape=(
            jax.ShapeDtypeStruct((rows, width), f32),
            jax.ShapeDtypeStruct((rows, PANEL), f32),
            jax.ShapeDtypeStruct((1, width), f32),
        ),
        grid_spec=pltpu.PrefetchScalarGridSpec(
            num_scalar_prefetch=1,
            grid=(samp,),
            in_specs=[
                pl.BlockSpec((feat, 1, held, width), lambda i, at_ref: (0, i, 0, 0)),
                pl.BlockSpec((1, imps, width), lambda i, at_ref: (i // 2, 0, 0)),
                pl.BlockSpec((1, imps, width), lambda i, at_ref: ((i // 2 - at_ref[6]) & 3, 0, 0)),
                pl.BlockSpec((PANEL, PANEL), fixed),
            ],
            out_specs=[
                pl.BlockSpec((rows, width), fixed),
                pl.BlockSpec((rows, PANEL), fixed),
                pl.BlockSpec((1, width), fixed),
            ],
            scratch_shapes=[
                pltpu.VMEM((width, rows + PANEL), f32),
                pltpu.VMEM((PANEL, rows), f32),
                pltpu.VMEM((feat, width), f32),
            ],
        ),
        compiler_params=pltpu.CompilerParams(vmem_limit_bytes=50 << 20),
        name="gram_schur",
    )(at, gathered, near, far, inv)


def invert_body(a_ref, out_ref, work, diag):
    n = a_ref.shape[0]
    nb = 128
    work[:, :n] = a_ref[...]
    row = lax.broadcasted_iota(jnp.int32, (n, n), 0)
    col = lax.broadcasted_iota(jnp.int32, (n, n), 1)
    work[:, n:] = (row == col).astype(f32)
    sub = lax.broadcasted_iota(jnp.int32, (8, nb), 0)
    lane = lax.broadcasted_iota(jnp.int32, (8, nb), 1)
    eye = (
        lax.broadcasted_iota(jnp.int32, (nb, nb), 0) == lax.broadcasted_iota(jnp.int32, (nb, nb), 1)
    ).astype(f32)
    for lo in range(0, n, nb):
        hi = lo + nb
        diag[:, :nb] = work[lo:hi, lo:hi]
        diag[:, nb:] = eye
        for q in range(0, nb, 8):
            ra = diag[q : q + 8, :nb]
            rb = diag[q : q + 8, nb:]
            cols = [jnp.broadcast_to(ra[:, q + c : q + c + 1], (8, nb)) for c in range(8)]
            pivots = jnp.ones((8, nb), f32)
            for c in range(8):
                d = jnp.broadcast_to(cols[c][c : c + 1, :], (8, nb))
                pivots = jnp.where(sub == c, d, pivots)
                if c < 7:
                    mult = jnp.where(sub > c, cols[c] / d, 0.0)
                    for e in range(c + 1, 8):
                        cols[e] = cols[e] - mult * jnp.broadcast_to(cols[e][c : c + 1, :], (8, nb))
                    ra = ra - mult * jnp.broadcast_to(ra[c : c + 1, :], (8, nb))
                    rb = rb - mult * jnp.broadcast_to(rb[c : c + 1, :], (8, nb))
            scale = lax.rsqrt(pivots)
            ra = ra * scale
            rb = rb * scale
            diag[q : q + 8, nb:] = rb
            if q + 8 < nb:
                low = jnp.where(lane >= q + 8, ra, 0.0)
                update = dot(low, jnp.concatenate([low, rb], 1), ((0,), (0,)), precision=HIGHEST)
                diag[q + 8 :, :] = diag[q + 8 :, :] - update[q + 8 :, :]
        upper = dot(diag[:, nb:], work[lo:hi, hi : n + hi], ((1,), (0,)), precision=HIGHEST)
        rest = n - hi
        out_ref[lo:hi, :hi] = upper[:, rest:]
        if rest:
            work[hi:, hi : n + hi] = work[hi:, hi : n + hi] - dot(
                upper[:, :rest], upper, ((0,), (0,)), precision=HIGHEST
            )
            out_ref[lo:hi, hi:] = jnp.zeros((nb, rest), f32)


def inverse_factor(pivot):
    n = pivot.shape[0]
    return pl.pallas_call(
        invert_body,
        out_shape=jax.ShapeDtypeStruct((n, n), f32),
        scratch_shapes=[pltpu.VMEM((n, 2 * n), f32), pltpu.VMEM((128, 256), f32)],
        compiler_params=pltpu.CompilerParams(vmem_limit_bytes=32 << 20),
        name="inverse_factor",
    )(pivot)


def per_device(embeddings, frequencies, phases, treat_freq, treatment, flips, panel):
    imps = embeddings.shape[0]
    width = frequencies.shape[1]
    samp = lax.axis_size(SAMP)
    feat = lax.axis_size(FEAT)
    samp_index = lax.axis_index(SAMP)
    feat_index = lax.axis_index(FEAT)
    count = imps * samp
    rows = width * feat // samp
    piece = imps // feat
    elim = PANEL // width

    project = jnp.dot(embeddings, frequencies, preferred_element_type=f32)
    treated = treatment.astype(f32)
    flipped = flips.astype(f32)
    counter = treated + flipped - 2.0 * treated * flipped
    base = project + phases[None, :]
    observed = cosine(base + treated[:, None] * treat_freq[None, :])
    counterfactual = cosine(base + counter[:, None] * treat_freq[None, :])
    moment_part = jnp.sum(counterfactual - observed, axis=0)
    feature = observed.astype(bf16)

    near = lax.all_gather(feature, "x")

    shares = lax.all_to_all(
        feature.reshape(feat, piece, width), FEAT, split_axis=0, concat_axis=0, tiled=True
    )
    first_dev = panel[0] * elim
    picked = lax.dynamic_slice_in_dim(shares, first_dev, elim, 0)
    high = lax.reduce_precision(moment_part, 8, 7)
    middle = lax.reduce_precision(moment_part - high, 8, 7)
    low = moment_part - high - middle
    moment_rows = jnp.pad(jnp.stack([high, middle, low]), ((0, 13), (0, 0))).astype(bf16)
    held = jnp.concatenate([picked.reshape(elim * piece, width), moment_rows], axis=0)
    send = jnp.concatenate(
        [
            shares.reshape(samp, feat // samp * piece, width),
            jnp.broadcast_to(held[None], (samp,) + held.shape),
        ],
        axis=1,
    )
    share = lax.all_to_all(send, SAMP, split_axis=0, concat_axis=0, tiled=True)
    gathered = lax.all_gather(share, FEAT)

    later, share = lax.optimization_barrier((feature, share))
    swapped = lax.ppermute(later, "zh", [(0, 1), (1, 0)])
    xs = lax.axis_size("x")
    far = jnp.stack(
        [swapped]
        + [lax.ppermute(swapped, "x", [(i, (i - r) % xs) for i in range(xs)]) for r in range(1, xs)]
    )

    skip = feat // samp * piece
    parts = [
        share[:, skip + k * piece : skip + (k + 1) * piece, :].reshape(samp * piece, width)
        for k in range(elim)
    ]
    mine = jnp.concatenate(parts, axis=1)
    partial = dot(mine, mine, ((0,), (0,)))
    slabs = lax.all_to_all(
        partial.reshape(feat, PANEL // feat, PANEL), FEAT, split_axis=0, concat_axis=0, tiled=True
    )
    slab = jnp.sum(slabs, axis=0)
    pivot = lax.all_to_all(
        jnp.broadcast_to(slab[None], slabs.shape), FEAT, split_axis=0, concat_axis=0, tiled=True
    ).reshape(PANEL, PANEL)
    inv = inverse_factor(pivot / count + ridge * jnp.eye(PANEL, dtype=f32))

    at = jnp.stack(
        [
            samp_index * rows,
            feat_index * width,
            panel[0] * PANEL,
            lax.axis_index("zh"),
            feat_index,
            first_dev,
            lax.axis_index("x"),
        ]
    ).astype(jnp.int32)
    schur, factor, reduced = gram_schur(count, at, gathered, near, far, inv)
    return (schur, factor, reduced[0])


def solution(mesh):
    fine = Mesh(mesh.devices.reshape(4, 2, 4, 4, 2), ("x", "zh", "y", "zl", "core"))
    return jax.shard_map(
        per_device,
        mesh=fine,
        in_specs=(P(SAMP, None), P(None, FEAT), P(FEAT), P(FEAT), P(SAMP), P(SAMP), P()),
        out_specs=(P(SAMP, FEAT), P(SAMP, None), P(FEAT)),
        check_vma=False,
    )
```

time: 319 us -> 323 us (1.013)
  starting transfers between devices: 24.8 us -> 16.8 us
  waiting for transfers between devices: 124 us -> 132 us
  Pallas kernels: 72.6 us -> 65.3 us
    ppermute x1 -> x4, waiting for transfers between devices: 13.4 us -> 91.7 us  [the longest x1 67.4 us: per_device(): swapped = lax.ppermute(later, 'zh', [(0, 1), (1, 0)])]
    all_gather x1, waiting for transfers between devices: 94.1 us -> 24.5 us  [per_device(): gathered = lax.all_gather(share, FEAT)]
    all_to_all x0 -> x1, blocking collectives: none -> 45.9 us  [per_device(): lax.all_to_all(partial.reshape(feat, PANEL // feat, PANEL), FEAT, split_a...]
    all_gather x2 -> x0, blocking collectives: 25.6 us -> none  [the longest x1 16.6 us: per_device(): lax.all_gather(moment, ('zl', 'core'))]
    psum x1 -> x0, blocking collectives: 20.7 us -> none  [per_device(): moment = lax.psum(moment_part, SAMP) / count]
    pallas_call x2 -> x1, Pallas kernels: 35.4 us -> 28.1 us  [gram_schur(): pl.pallas_call(lambda *refs: gram_body(count, *refs), out_shape=(jax.Shap...]
    all_to_all x1, starting transfers between devices: 16.9 us -> 10.2 us  [per_device(): lax.all_to_all(feature.reshape(feat, piece, width), FEAT, split_axis=0, c...]
    ppermute x1 -> x4, starting transfers between devices: 7.83 us -> 2.77 us  [the longest x3 2.68 us: per_device(): lax.ppermute(swapped, 'x', [(i, (i - r) % xs) for i in range(xs)])]
  transfers between devices with their start and end apart: 5 -> 8, of which waited for: 3 -> 5; matrix products, arithmetic and copies ran while one was open for 0% -> 2% of each run, Pallas kernels for 0% -> 12%
where the time goes in v2:
time: 323 us; the launch traced here: 320 us
  waiting for transfers between devices  132 us (41%)
  blocking collectives  77.6 us (24%)
  Pallas kernels  65.3 us (20%)
  starting transfers between devices  16.8 us (5%)
  between operations  14.8 us (5%)
  other arithmetic  4.98 us (2%)
  matrix products  4.17 us (1%)
  local copies, waits for them, and re-layouts  3.81 us (1%)
    ppermute x1, waiting for transfers between devices, per_device(): swapped = lax.ppermute(later, 'zh', [(0, 1), (1, 0)])  67.4 us
    all_to_all x1, blocking collectives, per_device(): lax.all_to_all(partial.reshape(feat, PANEL // feat, PANEL), FEAT, split_a...  45.9 us
    pallas_call x1, Pallas kernels, inverse_factor(): pl.pallas_call(invert_body, out_shape=jax.ShapeDtypeStruct((n, n), f32),...  37.2 us
    all_to_all x1, blocking collectives, per_device(): share = lax.all_to_all(send, SAMP, split_axis=0, concat_axis=0, tiled=True)  31.7 us
    pallas_call x1, Pallas kernels, gram_schur(): pl.pallas_call(lambda *refs: gram_body(count, *refs), out_shape=(jax.Shap...  28.1 us
    all_gather x1, waiting for transfers between devices, per_device(): gathered = lax.all_gather(share, FEAT)  24.5 us
    ppermute x3, waiting for transfers between devices, per_device(): lax.ppermute(swapped, 'x', [(i, (i - r) % xs) for i in range(xs)])  24.3 us
    all_to_all x1, waiting for transfers between devices, per_device(): lax.all_to_all(feature.reshape(feat, piece, width), FEAT, split_axis=0, c...  16.1 us
  transfers between devices with their start and end apart: 8, of which 5 were waited for; matrix products, arithmetic and copies ran while one was open for 2% of the time, Pallas kernels for 12%

profile of v2, /device:TPU:1, one launch (start us, length us, event | category | flops | bytes accessed | tf_op | source)
XLA Modules:
  0.0 319.8 jit_solution(17928388637996107753)
XLA Ops:
  7.2 0.0 all-gather.7.cloned.1.call-start
  7.2 0.8 convert_element_type.13
  8.1 0.7 multiply_subtract_fusion
  8.8 3.8 %fusion.21 = (bf16[1024,256]{1,0:T(8,128)(2,1)}, f32[256]{0:T(256)S(1)}) fusion(f32[256]{0:T(256)} %param.10, f32[1024]{0:T(1024)S(1)} %convert_element_type.13, f32[1024]{0:T(1024)S(1)} %multiply_subtract_fusion, f32[256]{0:T(256)} %param.9, bf16[1024,1024]{1,0:T(8,128)(2,1)S(1)} %copy-done, bf16[1024,256]{1,0:T(8,128)(2,1)} %param.8), kind=kOutput, calls=%fused_computation.45 | convolution fusion | flops 547880704 | bytes 3156992 | tf_op jit(solution)/shard_map/dot_general | solution.py:226
  12.6 0.0 all-gather.7.cloned.1.call-update
  12.6 10.2 %all-to-all-start = ((bf16[32,32,256]{2,1,0:T(8,128)(2,1)}), bf16[32,32,256]{2,1,0:T(8,128)(2,1)S(1)}, u32[]{:S(2)}, u32[]{:S(2)}) async-start(bf16[32,32,256]{2,1,0:T(8,128)(2,1)} %bitcast.28), calls=%async_computation | async-start | bytes 1048576 | tf_op jit(solution)/shard_map/all_to_all | solution.py:238
  22.9 0.0 all-gather.5.cloned.1.call-start
  23.6 16.1 %all-to-all-done = bf16[32,32,256]{2,1,0:T(8,128)(2,1)S(1)} async-done(((bf16[32,32,256]{2,1,0:T(8,128)(2,1)}), bf16[32,32,256]{2,1,0:T(8,128)(2,1)S(1)}, u32[]{:S(2)}, u32[]{:S(2)}) %all-to-all-start) | async-done | bytes 524320 | tf_op jit(solution)/shard_map/all_to_all | solution.py:238
  39.7 0.1 pad_maximum_fusion.1
  39.8 31.7 %all_to_all.20 = bf16[8,208,256]{2,1,0:T(8,128)(2,1)} all-to-all(bf16[8,208,256]{2,1,0:T(8,128)(2,1)S(1)} %pad_maximum_fusion.1), channel_id=1, replica_groups=mesh['x'=4,'zh'=2,'y'=4,'zl'=4,'core'=2] {'x','zh'}, dimensions={0} | all-to-all | bytes 1703936 | tf_op jit(solution)/shard_map/all_to_all | solution.py:255
  71.5 0.0 all-gather.5.cloned.1.call-update
  71.5 1.0 fusion.22
  72.5 0.3 fusion.10
  72.8 45.9 %all_to_all.21 = f32[32,16,512]{2,1,0:T(8,128)S(1)} all-to-all(f32[32,16,512]{2,1,0:T(8,128)S(1)} %bitcast.26), channel_id=1, replica_groups=mesh['x'=4,'zh'=2,'y'=4,'zl'=4,'core'=2] {'y','zl','core'}, dimensions={0} | all-to-all | bytes 2097152 | tf_op jit(solution)/shard_map/all_to_all | solution.py:273
  118.7 0.1 reduce_sum.22
  118.8 1.1 broadcast_in_dim.5
  119.9 3.7 %all-to-all-start.3 = ((f32[32,16,512]{2,1,0:T(8,128)}), f32[32,16,512]{2,1,0:T(8,128)S(1)}, u32[]{:S(2)}, u32[]{:S(2)}) async-start(f32[32,16,512]{2,1,0:T(8,128)} %broadcast_in_dim.5), calls=%async_computation.3 | async-start | bytes 2097152 | tf_op jit(solution)/shard_map/all_to_all | solution.py:277
  123.6 0.1 collective-permute-start
  123.7 67.4 %collective-permute-done = bf16[1024,256]{1,0:T(8,128)(2,1)} collective-permute-done((bf16[1024,256]{1,0:T(8,128)(2,1)}, bf16[1024,256]{1,0:T(8,128)(2,1)}, u32[]{:S(2)}, u32[]{:S(2)}) %collective-permute-start) | collective-permute-done | bytes 524320 | tf_op jit(solution)/shard_map/ppermute | solution.py:259
  191.2 1.1 collective-permute-start.2
  192.2 1.6 collective-permute-start.1
  193.8 0.1 stack.47.refs_0_
  193.9 23.9 %collective-permute-done.3 = bf16[1024,256]{1,0:T(8,128)(2,1)} collective-permute-done((bf16[1024,256]{1,0:T(8,128)(2,1)}, bf16[1024,256]{1,0:T(8,128)(2,1)}, u32[]{:S(2)}, u32[]{:S(2)}) %collective-permute-start.3) | collective-permute-done | bytes 524320 | tf_op jit(solution)/shard_map/ppermute | solution.py:263
  217.8 0.3 collective-permute-done.1
  218.2 3.1 pad_maximum_fusion.refs_3_
  221.3 0.1 broadcast_multiply_fusion
  221.4 0.1 bitcast_add_fusion.a_ref
  221.5 37.2 %inverse_factor.1.refs_4_ = f32[512,512]{1,0:T(8,128)S(1)} custom-call(f32[512,512]{1,0:T(8,128)S(1)} %bitcast_add_fusion.a_ref), custom_call_target="tpu_custom_call" | custom-call | tf_op jit(solution)/shard_map/inverse_factor/pallas_call | solution.py:205
  258.7 0.0 all-gather.7.cloned.1.call-done
  258.8 24.5 %all-gather.5.cloned.1.call-done = bf16[256,208,256]{2,1,0:T(8,128)(2,1)} async-done(((bf16[8,208,256]{2,1,0:T(8,128)(2,1)}), bf16[256,208,256]{2,1,0:T(8,128)(2,1)}) %all-gather.5.cloned.1.call-update) | async-done | bytes 27262992 | tf_op jit(solution)/shard_map/all_gather | solution.py:256
  283.3 1.6 copy-done.1
  284.9 28.1 %gram_schur.1 = (f32[1024,256]{1,0:T(8,128)}, f32[1024,512]{1,0:T(8,128)}, f32[1,256]{1,0:T(1,128)}) custom-call(s32[7]{0:T(128)S(1)} %stack.47.refs_0_, bf16[32,8,208,256]{3,2,1,0:T(8,128)(2,1)} %bitcast.25, bf16[4,1024,256]{2,1,0:T(8,128)(2,1)S(1)} %bitcast.24, bf16[4,1024,256]{2,1,0:T(8,128)(2,1)} %pad_maximum_fusion.refs_3_, ...), custom_call_target="tpu_custom_call" | custom-call | tf_op jit(solution)/shard_map/gram_schur/pallas_call | solution.py:123
  (11 shorter events, 0.1 us)
Async XLA Ops:
  7.2 1.6 copy-start
  7.2 251.6 %all-gather.7.cloned.1.call-start = ((), (), s32[]{:S(2)}) async-start(), calls=%async_computation.5 | async-start | bytes 2621440 | tf_op jit(solution)/shard_map/all_gather | solution.py:236
  12.6 27.0 %all-to-all-start = ((bf16[32,32,256]{2,1,0:T(8,128)(2,1)}), bf16[32,32,256]{2,1,0:T(8,128)(2,1)S(1)}, u32[]{:S(2)}, u32[]{:S(2)}) async-start(bf16[32,32,256]{2,1,0:T(8,128)(2,1)} %bitcast.28), calls=%async_computation | async-start | bytes 1048576 | tf_op jit(solution)/shard_map/all_to_all | solution.py:238
  22.9 260.4 %all-gather.5.cloned.1.call-start = ((), (), s32[]{:S(2)}) async-start(), calls=%async_computation.4 | async-start | bytes 28114944 | tf_op jit(solution)/shard_map/all_gather | solution.py:256
  119.9 101.4 %all-to-all-start.3 = ((f32[32,16,512]{2,1,0:T(8,128)}), f32[32,16,512]{2,1,0:T(8,128)S(1)}, u32[]{:S(2)}, u32[]{:S(2)}) async-start(f32[32,16,512]{2,1,0:T(8,128)} %broadcast_in_dim.5), calls=%async_computation.3 | async-start | bytes 2097152 | tf_op jit(solution)/shard_map/all_to_all | solution.py:277
  123.6 67.5 %collective-permute-start = (bf16[1024,256]{1,0:T(8,128)(2,1)}, bf16[1024,256]{1,0:T(8,128)(2,1)}, u32[]{:S(2)}, u32[]{:S(2)}) collective-permute-start(bf16[1024,256]{1,0:T(8,128)(2,1)} %get-tuple-element.8), channel_id=1, source_target_pairs={{0,32},{32,0},{1,33},{33,1},{2,34},{34,2},{3,35},{35,3},{4,36},{36... | collective-permute-start | bytes 1572872 | tf_op jit(solution)/shard_map/ppermute | solution.py:259
  191.2 26.7 %collective-permute-start.3 = (bf16[1024,256]{1,0:T(8,128)(2,1)}, bf16[1024,256]{1,0:T(8,128)(2,1)}, u32[]{:S(2)}, u32[]{:S(2)}) collective-permute-start(bf16[1024,256]{1,0:T(8,128)(2,1)} %collective-permute-done), channel_id=1, source_target_pairs={{0,64},{64,128},{128,192},{192,0},{1,65},{65,129},{129,193},{193,1... | collective-permute-start | bytes 1572872 | tf_op jit(solution)/shard_map/ppermute | solution.py:263
  191.2 26.7 %collective-permute-start.2 = (bf16[1024,256]{1,0:T(8,128)(2,1)}, bf16[1024,256]{1,0:T(8,128)(2,1)}, u32[]{:S(2)}, u32[]{:S(2)}) collective-permute-start(bf16[1024,256]{1,0:T(8,128)(2,1)} %collective-permute-done), channel_id=1, source_target_pairs={{0,128},{64,192},{128,0},{192,64},{1,129},{65,193},{129,1},{193,65... | collective-permute-start | bytes 1572872 | tf_op jit(solution)/shard_map/ppermute | solution.py:263
  192.2 26.0 %collective-permute-start.1 = (bf16[1024,256]{1,0:T(8,128)(2,1)}, bf16[1024,256]{1,0:T(8,128)(2,1)}, u32[]{:S(2)}, u32[]{:S(2)}) collective-permute-start(bf16[1024,256]{1,0:T(8,128)(2,1)} %collective-permute-done), channel_id=1, source_target_pairs={{0,192},{64,0},{128,64},{192,128},{1,193},{65,1},{129,65},{193,129... | collective-permute-start | bytes 1572872 | tf_op jit(solution)/shard_map/ppermute | solution.py:263
  283.3 1.6 copy-start.1
Sparse Core Ops, SparseCore 0:
  12.8 37.1 all-gather.6
  71.6 211.6 all-gather.4

commit v3 on v2

v3 whole, which is shorter than its diff:
```python
import jax
import jax.numpy as jnp
from jax import lax
from jax.experimental import pallas as pl
from jax.experimental.pallas import tpu as pltpu
from jax.sharding import Mesh
from jax.sharding import PartitionSpec as P

PANEL = 512
ridge = 0.1
f32 = jnp.float32
bf16 = jnp.bfloat16
HIGHEST = lax.Precision.HIGHEST

SAMP = ("x", "zh")
FEAT = ("y", "zl", "core")

SINE = (
    -8.885765875337938,
    58.46599556065702,
    -115.4071939365197,
    108.47536728137668,
    -59.39695452559278,
    20.275610646954046,
)


def cosine(x):
    turns = x * 0.15915494309189535
    s = jnp.abs(turns - jnp.round(turns)) - 0.25
    u = s * s
    p = SINE[5]
    for c in SINE[4::-1]:
        p = p * u + c
    return s * p


def dot(left, right, dims, **kw):
    return lax.dot_general(left, right, (dims, ((), ())), preferred_element_type=f32, **kw)


def split(a):
    high = a.astype(bf16)
    return high, (a - high.astype(f32)).astype(bf16)


def dot3(left, right, dims):
    lh, ll = left
    rh, rl = right
    return dot(lh, rh, dims) + (dot(lh, rl, dims) + dot(ll, rh, dims))


NT = ((1,), (1,))


def invert(a, out_ref, work, diag):
    n = a.shape[0]
    nb = 128
    work[:, :n] = a
    row = lax.broadcasted_iota(jnp.int32, (n, n), 0)
    col = lax.broadcasted_iota(jnp.int32, (n, n), 1)
    work[:, n:] = (row == col).astype(f32)
    sub = lax.broadcasted_iota(jnp.int32, (8, nb), 0)
    lane = lax.broadcasted_iota(jnp.int32, (8, nb), 1)
    eye = (
        lax.broadcasted_iota(jnp.int32, (nb, nb), 0) == lax.broadcasted_iota(jnp.int32, (nb, nb), 1)
    ).astype(f32)
    for lo in range(0, n, nb):
        hi = lo + nb
        diag[:, :nb] = work[lo:hi, lo:hi]
        diag[:, nb:] = eye
        for q in range(0, nb, 8):
            ra = diag[q : q + 8, :nb]
            rb = diag[q : q + 8, nb:]
            cols = [jnp.broadcast_to(ra[:, q + c : q + c + 1], (8, nb)) for c in range(8)]
            pivots = jnp.ones((8, nb), f32)
            for c in range(8):
                d = jnp.broadcast_to(cols[c][c : c + 1, :], (8, nb))
                pivots = jnp.where(sub == c, d, pivots)
                if c < 7:
                    mult = jnp.where(sub > c, cols[c] / d, 0.0)
                    for e in range(c + 1, 8):
                        cols[e] = cols[e] - mult * jnp.broadcast_to(cols[e][c : c + 1, :], (8, nb))
                    ra = ra - mult * jnp.broadcast_to(ra[c : c + 1, :], (8, nb))
                    rb = rb - mult * jnp.broadcast_to(rb[c : c + 1, :], (8, nb))
            scale = lax.rsqrt(pivots)
            ra = ra * scale
            rb = rb * scale
            diag[q : q + 8, nb:] = rb
            if q + 8 < nb:
                low = jnp.where(lane >= q + 8, ra, 0.0)
                update = dot(low, jnp.concatenate([low, rb], 1), ((0,), (0,)), precision=HIGHEST)
                diag[q + 8 :, :] = diag[q + 8 :, :] - update[q + 8 :, :]
        upper = dot(diag[:, nb:], work[lo:hi, hi : n + hi], ((1,), (0,)), precision=HIGHEST)
        rest = n - hi
        out_ref[lo:hi, :hi] = upper[:, rest:]
        if rest:
            work[hi:, hi : n + hi] = work[hi:, hi : n + hi] - dot(
                upper[:, :rest], upper, ((0,), (0,)), precision=HIGHEST
            )
            out_ref[lo:hi, hi:] = jnp.zeros((nb, rest), f32)


def gram_body(
    count, at_ref, all_ref, near_ref, far_ref, schur_ref, factor_ref, red_ref,
    own, panel, pivot, mom, inv_ref, work, diag
):
    step = pl.program_id(0)
    imps = near_ref.shape[1]
    width = near_ref.shape[2]
    feat = all_ref.shape[0]
    piece = imps // feat
    rows = panel.shape[1]
    row_blocks = rows // width
    blocks = row_blocks + PANEL // width

    @pl.when(step == 0)
    def _():
        own[...] = jnp.zeros_like(own)
        panel[...] = jnp.zeros_like(panel)
        pivot[...] = jnp.zeros_like(pivot)
        mom[...] = jnp.zeros_like(mom)

    mine = jnp.where(step % 2 == at_ref[3], near_ref[0], far_ref[0])
    block = [
        all_ref[:, 0, b * piece : (b + 1) * piece, :].reshape(imps, width) for b in range(blocks)
    ]
    mine_t = mine.T
    elim = jnp.concatenate(block[row_blocks:], axis=1)
    elim_t = elim.T
    for b in range(blocks):
        at = slice(b * width, (b + 1) * width)
        own[:, at] += dot(mine_t, block[b], ((1,), (0,)))
        if b < row_blocks:
            panel[:, at] += dot(elim_t, block[b], ((1,), (0,)))
    pivot[...] += dot(elim_t, elim, ((1,), (0,)))
    mom[...] += jnp.sum(all_ref[:, 0, blocks * piece :, :].astype(f32), axis=1)

    @pl.when(step == pl.num_programs(0) - 1)
    def _():
        row0, col0, first = at_ref[0], at_ref[1], at_ref[2]
        scale = 1.0 / count

        def diagonal(shape, r0, c0):
            r = r0 + lax.broadcasted_iota(jnp.int32, shape, 0)
            c = c0 + lax.broadcasted_iota(jnp.int32, shape, 1)
            return jnp.where(r == c, ridge, 0.0)

        invert(pivot[...] * scale + diagonal((PANEL, PANEL), 0, 0), inv_ref, work, diag)
        inv = split(inv_ref[...])
        cross = own[:, rows:] * scale + diagonal((width, PANEL), col0, first)
        cross = dot3(split(cross), inv, NT)
        cross_parts = split(cross)
        for lo in range(0, rows, width):
            at = slice(lo, lo + width)
            cols = panel[:, at].T * scale + diagonal((width, PANEL), row0 + lo, first)
            factor = dot3(split(cols), inv, NT)
            factor_ref[at, :] = factor
            gram = own[:, at].T * scale + diagonal((width, width), row0 + lo, col0)
            schur_ref[at, :] = gram - dot3(split(factor), cross_parts, NT)
        own_dev = at_ref[4]
        first_dev = at_ref[5]
        picked = [mom[pl.ds(first_dev + k, 1), :] * scale for k in range(PANEL // width)]
        elim = jnp.broadcast_to(jnp.concatenate(picked, axis=1), (8, PANEL))
        solved = dot(elim, inv_ref[...], NT, precision=HIGHEST)
        part = dot(solved, cross, NT, precision=HIGHEST)
        reduced = mom[pl.ds(own_dev, 1), :] * scale - part[:1]
        red_ref[...] = reduced * (count**0.5)


def gram_schur(count, at, gathered, near, far):
    feat, samp, held, width = gathered.shape
    imps = near.shape[1]
    rows = width * feat // samp
    fixed = lambda i, at_ref: (0, 0)
    return pl.pallas_call(
        lambda *refs: gram_body(count, *refs),
        out_shape=(
            jax.ShapeDtypeStruct((rows, width), f32),
            jax.ShapeDtypeStruct((rows, PANEL), f32),
            jax.ShapeDtypeStruct((1, width), f32),
        ),
        grid_spec=pltpu.PrefetchScalarGridSpec(
            num_scalar_prefetch=1,
            grid=(samp,),
            in_specs=[
                pl.BlockSpec((feat, 1, held, width), lambda i, at_ref: (0, i, 0, 0)),
                pl.BlockSpec((1, imps, width), lambda i, at_ref: (i // 2, 0, 0)),
                pl.BlockSpec((1, imps, width), lambda i, at_ref: (i // 2, 0, 0)),
            ],
            out_specs=[
                pl.BlockSpec((rows, width), fixed),
                pl.BlockSpec((rows, PANEL), fixed),
                pl.BlockSpec((1, width), fixed),
            ],
            scratch_shapes=[
                pltpu.VMEM((width, rows + PANEL), f32),
                pltpu.VMEM((PANEL, rows), f32),
                pltpu.VMEM((PANEL, PANEL), f32),
                pltpu.VMEM((feat, width), f32),
                pltpu.VMEM((PANEL, PANEL), f32),
                pltpu.VMEM((PANEL, 2 * PANEL), f32),
                pltpu.VMEM((128, 256), f32),
            ],
        ),
        compiler_params=pltpu.CompilerParams(vmem_limit_bytes=50 << 20),
        name="gram_schur",
    )(at, gathered, near, far)


def per_device(embeddings, frequencies, phases, treat_freq, treatment, flips, panel):
    imps = embeddings.shape[0]
    width = frequencies.shape[1]
    samp = lax.axis_size(SAMP)
    feat = lax.axis_size(FEAT)
    samp_index = lax.axis_index(SAMP)
    feat_index = lax.axis_index(FEAT)
    count = imps * samp
    rows = width * feat // samp
    piece = imps // feat
    elim = PANEL // width

    project = jnp.dot(embeddings, frequencies, preferred_element_type=f32)
    treated = treatment.astype(f32)
    flipped = flips.astype(f32)
    counter = treated + flipped - 2.0 * treated * flipped
    base = project + phases[None, :]
    observed = cosine(base + treated[:, None] * treat_freq[None, :])
    counterfactual = cosine(base + counter[:, None] * treat_freq[None, :])
    moment_part = jnp.sum(counterfactual - observed, axis=0)
    feature = observed.astype(bf16)

    near = lax.all_gather(feature, "x")
    swapped = lax.ppermute(feature, "zh", [(0, 1), (1, 0)])

    shares = lax.all_to_all(
        feature.reshape(feat, piece, width), FEAT, split_axis=0, concat_axis=0, tiled=True
    )
    swapped, shares = lax.optimization_barrier((swapped, shares))
    far = lax.all_gather(swapped, "x")
    first_dev = panel[0] * elim
    picked = lax.dynamic_slice_in_dim(shares, first_dev, elim, 0)
    high = lax.reduce_precision(moment_part, 8, 7)
    middle = lax.reduce_precision(moment_part - high, 8, 7)
    low = moment_part - high - middle
    moment_rows = jnp.pad(jnp.stack([high, middle, low]), ((0, 13), (0, 0))).astype(bf16)
    held = jnp.concatenate([picked.reshape(elim * piece, width), moment_rows], axis=0)
    send = jnp.concatenate(
        [
            shares.reshape(samp, feat // samp * piece, width),
            jnp.broadcast_to(held[None], (samp,) + held.shape),
        ],
        axis=1,
    )
    share = lax.all_to_all(send, SAMP, split_axis=0, concat_axis=0, tiled=True)
    gathered = lax.all_gather(share, FEAT)

    at = jnp.stack(
        [
            samp_index * rows,
            feat_index * width,
            panel[0] * PANEL,
            lax.axis_index("zh"),
            feat_index,
            first_dev,
        ]
    ).astype(jnp.int32)
    schur, factor, reduced = gram_schur(count, at, gathered, near, far)
    return (schur, factor, reduced[0])


def solution(mesh):
    fine = Mesh(mesh.devices.reshape(4, 2, 4, 4, 2), ("x", "zh", "y", "zl", "core"))
    return jax.shard_map(
        per_device,
        mesh=fine,
        in_specs=(P(SAMP, None), P(None, FEAT), P(FEAT), P(FEAT), P(SAMP), P(SAMP), P()),
        out_specs=(P(SAMP, FEAT), P(SAMP, None), P(FEAT)),
        check_vma=False,
    )
```

time: 323 us -> 331 us (1.025)
  waiting for transfers between devices: 132 us -> 194 us
  blocking collectives: 77.6 us -> 31.9 us
  Pallas kernels: 65.3 us -> 68.7 us
  other arithmetic: 4.98 us -> 1.62 us
    all_gather x1, waiting for transfers between devices: 24.5 us -> 152 us  [per_device(): gathered = lax.all_gather(share, FEAT)]
    ppermute x4 -> x1, waiting for transfers between devices: 91.7 us -> 31.8 us  [per_device(): swapped = lax.ppermute(feature, 'zh', [(0, 1), (1, 0)])]
    all_to_all x1 -> x0, blocking collectives: 45.9 us -> none  [per_device(): lax.all_to_all(partial.reshape(feat, PANEL // feat, PANEL), FEAT, split_a...]
    pallas_call x1, Pallas kernels: 28.1 us -> 68.7 us  [gram_schur(): pl.pallas_call(lambda *refs: gram_body(count, *refs), out_shape=(jax.Shap...]
    pallas_call x1 -> x0, Pallas kernels: 37.2 us -> none  [inverse_factor(): pl.pallas_call(invert_body, out_shape=jax.ShapeDtypeStruct((n, n), f32),...]
    all_to_all x1, waiting for transfers between devices: 16.1 us -> 3.12 us  [per_device(): lax.all_to_all(feature.reshape(feat, piece, width), FEAT, split_axis=0, c...]
    all_gather x0 -> x1, waiting for transfers between devices: none -> 6.15 us  [per_device(): far = lax.all_gather(swapped, 'x')]
    all_to_all x1 -> x0, starting transfers between devices: 3.72 us -> none  [per_device(): lax.all_to_all(jnp.broadcast_to(slab[None], slabs.shape), FEAT, split_axi...]
  transfers between devices with their start and end apart: 8 -> 5, of which waited for: 5 -> 4; matrix products, arithmetic and copies ran while one was open for 2% -> 0% of each run, Pallas kernels for 12% -> 0%
where the time goes in v3:
time: 331 us; the launch traced here: 330 us
  waiting for transfers between devices  194 us (59%)
  Pallas kernels  68.7 us (21%)
  blocking collectives  31.9 us (10%)
  starting transfers between devices  14.6 us (4%)
  between operations  14.5 us (4%)
  matrix products  3.85 us (1%)
    all_gather x1, waiting for transfers between devices, per_device(): gathered = lax.all_gather(share, FEAT)  152 us
    pallas_call x1, Pallas kernels, gram_schur(): pl.pallas_call(lambda *refs: gram_body(count, *refs), out_shape=(jax.Shap...  68.7 us
    all_to_all x1, blocking collectives, per_device(): share = lax.all_to_all(send, SAMP, split_axis=0, concat_axis=0, tiled=True)  31.9 us
    ppermute x1, waiting for transfers between devices, per_device(): swapped = lax.ppermute(feature, 'zh', [(0, 1), (1, 0)])  31.8 us
    all_to_all x1, starting transfers between devices, per_device(): lax.all_to_all(feature.reshape(feat, piece, width), FEAT, split_axis=0, c...  10.2 us
  transfers between devices with their start and end apart: 5, of which 4 were waited for; matrix products, arithmetic and copies ran while one was open for 0% of the time, Pallas kernels for 0%

profile of v3, /device:TPU:1, one launch (start us, length us, event | category | flops | bytes accessed | tf_op | source)
XLA Modules:
  0.0 330.4 jit_solution(203410825453690474)
XLA Ops:
  7.2 0.0 copy-start
  7.2 0.0 all-gather.9.cloned.1.call-start
  7.2 0.8 convert_element_type.12
  8.1 0.7 multiply_subtract_fusion
  8.8 0.0 copy-done
  8.8 3.8 %fusion.16 = (bf16[1024,256]{1,0:T(8,128)(2,1)}, f32[256]{0:T(256)S(1)}) fusion(f32[256]{0:T(256)} %param.10, f32[1024]{0:T(1024)S(1)} %convert_element_type.12, f32[1024]{0:T(1024)S(1)} %multiply_subtract_fusion, f32[256]{0:T(256)} %param.9, bf16[1024,1024]{1,0:T(8,128)(2,1)S(1)} %copy-done, bf16[1024,256]{1,0:T(8,128)(2,1)} %param.8), kind=kOutput, calls=%fused_computation.36 | convolution fusion | flops 547880704 | bytes 3156992 | tf_op jit(solution)/shard_map/dot_general | solution.py:223
  12.6 0.0 all-gather.9.cloned.1.call-update
  12.6 10.2 %all-to-all-start = ((bf16[32,32,256]{2,1,0:T(8,128)(2,1)}), bf16[32,32,256]{2,1,0:T(8,128)(2,1)S(1)}, u32[]{:S(2)}, u32[]{:S(2)}) async-start(bf16[32,32,256]{2,1,0:T(8,128)(2,1)} %bitcast.19), calls=%async_computation | async-start | bytes 1048576 | tf_op jit(solution)/shard_map/all_to_all | solution.py:236
  22.9 0.0 all-gather.11.cloned.1.call-start
  22.9 4.3 %collective-permute-start = (bf16[1024,256]{1,0:T(8,128)(2,1)}, bf16[1024,256]{1,0:T(8,128)(2,1)S(1)}, u32[]{:S(2)}, u32[]{:S(2)}) collective-permute-start(bf16[1024,256]{1,0:T(8,128)(2,1)} %get-tuple-element.13), channel_id=1, source_target_pairs={{0,32},{32,0},{1,33},{33,1},{2,34},{34,2},{3,35},{35,3},{4,36},{36... | collective-permute-start | bytes 1572872 | tf_op jit(solution)/shard_map/ppermute | solution.py:234
  27.2 31.8 %collective-permute-done = bf16[1024,256]{1,0:T(8,128)(2,1)S(1)} collective-permute-done((bf16[1024,256]{1,0:T(8,128)(2,1)}, bf16[1024,256]{1,0:T(8,128)(2,1)S(1)}, u32[]{:S(2)}, u32[]{:S(2)}) %collective-permute-start) | collective-permute-done | bytes 524320 | tf_op jit(solution)/shard_map/ppermute | solution.py:234
  59.0 0.0 copy-start.2
  59.0 3.1 all-to-all-done
  62.1 0.0 copy-done.2
  62.1 0.0 all-gather.11.cloned.1.call-update
  62.2 0.0 all-gather.7.cloned.1.call-start
  63.0 0.1 pad_maximum_fusion
  63.0 31.9 %all_to_all.10 = bf16[8,208,256]{2,1,0:T(8,128)(2,1)} all-to-all(bf16[8,208,256]{2,1,0:T(8,128)(2,1)S(1)} %pad_maximum_fusion), channel_id=1, replica_groups=mesh['x'=4,'zh'=2,'y'=4,'zl'=4,'core'=2] {'x','zh'}, dimensions={0} | all-to-all | bytes 1703936 | tf_op jit(solution)/shard_map/all_to_all | solution.py:255
  94.9 0.0 all-gather.7.cloned.1.call-update
  95.0 0.1 stack.28.refs_0_
  95.1 0.0 all-gather.9.cloned.1.call-done
  95.1 6.2 %all-gather.11.cloned.1.call-done = bf16[4096,256]{1,0:T(8,128)(2,1)} async-done(((bf16[1024,256]{1,0:T(8,128)(2,1)}), bf16[4096,256]{1,0:T(8,128)(2,1)}) %all-gather.11.cloned.1.call-update) | async-done | bytes 2097168 | tf_op jit(solution)/shard_map/all_gather | solution.py:240
  101.2 152.4 %all-gather.7.cloned.1.call-done = bf16[256,208,256]{2,1,0:T(8,128)(2,1)} async-done(((bf16[8,208,256]{2,1,0:T(8,128)(2,1)}), bf16[256,208,256]{2,1,0:T(8,128)(2,1)}) %all-gather.7.cloned.1.call-update) | async-done | bytes 27262992 | tf_op jit(solution)/shard_map/all_gather | solution.py:256
  253.6 0.0 copy-start.1
  253.6 1.6 copy-done.1
  255.2 68.7 %gram_schur.1 = (f32[1024,256]{1,0:T(8,128)}, f32[1024,512]{1,0:T(8,128)}, f32[1,256]{1,0:T(1,128)}) custom-call(s32[6]{0:T(128)S(1)} %stack.28.refs_0_, bf16[32,8,208,256]{3,2,1,0:T(8,128)(2,1)} %bitcast.16, bf16[4,1024,256]{2,1,0:T(8,128)(2,1)S(1)} %bitcast.15, bf16[4,1024,256]{2,1,0:T(8,128)(2,1)} %bitcast.18), custom_call_target="tpu_custom_call" | custom-call | tf_op jit(solution)/shard_map/gram_schur/pallas_call | solution.py:176
  (5 shorter events, 0.1 us)
Async XLA Ops:
  7.2 1.6 copy-start
  7.2 87.9 %all-gather.9.cloned.1.call-start = ((), (), s32[]{:S(2)}) async-start(), calls=%async_computation.3 | async-start | bytes 2621440 | tf_op jit(solution)/shard_map/all_gather | solution.py:233
  12.6 49.5 %all-to-all-start = ((bf16[32,32,256]{2,1,0:T(8,128)(2,1)}), bf16[32,32,256]{2,1,0:T(8,128)(2,1)S(1)}, u32[]{:S(2)}, u32[]{:S(2)}) async-start(bf16[32,32,256]{2,1,0:T(8,128)(2,1)} %bitcast.19), calls=%async_computation | async-start | bytes 1048576 | tf_op jit(solution)/shard_map/all_to_all | solution.py:236
  22.9 78.4 %all-gather.11.cloned.1.call-start = ((), (), s32[]{:S(2)}) async-start(), calls=%async_computation.4 | async-start | bytes 2621440 | tf_op jit(solution)/shard_map/all_gather | solution.py:240
  22.9 36.1 %collective-permute-start = (bf16[1024,256]{1,0:T(8,128)(2,1)}, bf16[1024,256]{1,0:T(8,128)(2,1)S(1)}, u32[]{:S(2)}, u32[]{:S(2)}) collective-permute-start(bf16[1024,256]{1,0:T(8,128)(2,1)} %get-tuple-element.13), channel_id=1, source_target_pairs={{0,32},{32,0},{1,33},{33,1},{2,34},{34,2},{3,35},{35,3},{4,36},{36... | collective-permute-start | bytes 1572872 | tf_op jit(solution)/shard_map/ppermute | solution.py:234
  59.0 3.1 copy-start.2
  62.2 191.5 %all-gather.7.cloned.1.call-start = ((), (), s32[]{:S(2)}) async-start(), calls=%async_computation.2 | async-start | bytes 28114944 | tf_op jit(solution)/shard_map/all_gather | solution.py:256
  253.6 1.6 copy-start.1
Sparse Core Ops, SparseCore 0:
  12.8 37.1 all-gather.8
  62.3 38.8 all-gather.10
  103.1 150.4 all-gather.6

commit v4 on v3

v4 whole, which is shorter than its diff:
```python
import jax
import jax.numpy as jnp
from jax import lax
from jax.experimental import pallas as pl
from jax.experimental.pallas import tpu as pltpu
from jax.sharding import Mesh
from jax.sharding import PartitionSpec as P

PANEL = 512
ridge = 0.1
f32 = jnp.float32
bf16 = jnp.bfloat16
HIGHEST = lax.Precision.HIGHEST

SAMP = ("x", "zh")
FEAT = ("y", "zl", "core")

SINE = (
    -8.885765875337938,
    58.46599556065702,
    -115.4071939365197,
    108.47536728137668,
    -59.39695452559278,
    20.275610646954046,
)


def cosine(x):
    turns = x * 0.15915494309189535
    s = jnp.abs(turns - jnp.round(turns)) - 0.25
    u = s * s
    p = SINE[5]
    for c in SINE[4::-1]:
        p = p * u + c
    return s * p


def dot(left, right, dims, **kw):
    return lax.dot_general(left, right, (dims, ((), ())), preferred_element_type=f32, **kw)


def invert_body(a_ref, out_ref, work, diag):
    n = a_ref.shape[0]
    nb = 128
    work[:, :n] = a_ref[...]
    row = lax.broadcasted_iota(jnp.int32, (n, n), 0)
    col = lax.broadcasted_iota(jnp.int32, (n, n), 1)
    work[:, n:] = (row == col).astype(f32)
    sub = lax.broadcasted_iota(jnp.int32, (8, nb), 0)
    lane = lax.broadcasted_iota(jnp.int32, (8, nb), 1)
    eye = (
        lax.broadcasted_iota(jnp.int32, (nb, nb), 0) == lax.broadcasted_iota(jnp.int32, (nb, nb), 1)
    ).astype(f32)
    for lo in range(0, n, nb):
        hi = lo + nb
        diag[:, :nb] = work[lo:hi, lo:hi]
        diag[:, nb:] = eye
        for q in range(0, nb, 8):
            ra = diag[q : q + 8, :nb]
            rb = diag[q : q + 8, nb:]
            cols = [jnp.broadcast_to(ra[:, q + c : q + c + 1], (8, nb)) for c in range(8)]
            pivots = jnp.ones((8, nb), f32)
            for c in range(8):
                d = jnp.broadcast_to(cols[c][c : c + 1, :], (8, nb))
                pivots = jnp.where(sub == c, d, pivots)
                if c < 7:
                    mult = jnp.where(sub > c, cols[c] / d, 0.0)
                    for e in range(c + 1, 8):
                        cols[e] = cols[e] - mult * jnp.broadcast_to(cols[e][c : c + 1, :], (8, nb))
                    ra = ra - mult * jnp.broadcast_to(ra[c : c + 1, :], (8, nb))
                    rb = rb - mult * jnp.broadcast_to(rb[c : c + 1, :], (8, nb))
            scale = lax.rsqrt(pivots)
            ra = ra * scale
            rb = rb * scale
            diag[q : q + 8, nb:] = rb
            if q + 8 < nb:
                low = jnp.where(lane >= q + 8, ra, 0.0)
                update = dot(low, jnp.concatenate([low, rb], 1), ((0,), (0,)), precision=HIGHEST)
                diag[q + 8 :, :] = diag[q + 8 :, :] - update[q + 8 :, :]
        upper = dot(diag[:, nb:], work[lo:hi, hi : n + hi], ((1,), (0,)), precision=HIGHEST)
        rest = n - hi
        out_ref[lo:hi, :hi] = upper[:, rest:]
        if rest:
            work[hi:, hi : n + hi] = work[hi:, hi : n + hi] - dot(
                upper[:, :rest], upper, ((0,), (0,)), precision=HIGHEST
            )
            out_ref[lo:hi, hi:] = jnp.zeros((nb, rest), f32)


def inverse_factor(pivot):
    n = pivot.shape[0]
    return pl.pallas_call(
        invert_body,
        out_shape=jax.ShapeDtypeStruct((n, n), f32),
        scratch_shapes=[pltpu.VMEM((n, 2 * n), f32), pltpu.VMEM((128, 256), f32)],
        compiler_params=pltpu.CompilerParams(vmem_limit_bytes=16 << 20),
        cost_estimate=pl.CostEstimate(flops=30 * 10**9, bytes_accessed=2 << 20, transcendentals=0),
        name="inverse_factor",
    )(pivot)


def split(a):
    high = a.astype(bf16)
    return high, (a - high.astype(f32)).astype(bf16)


def dot3(left, right, dims):
    lh, ll = left
    rh, rl = right
    return dot(lh, rh, dims) + (dot(lh, rl, dims) + dot(ll, rh, dims))


NN = ((1,), (0,))
NT = ((1,), (1,))


def gram_body(at_ref, all_ref, near_ref, own, panel, pivot):
    step = pl.program_id(0)
    imps = near_ref.shape[1]
    width = near_ref.shape[2]
    piece = imps // all_ref.shape[0]
    rows = panel.shape[1]
    row_blocks = rows // width
    blocks = row_blocks + PANEL // width

    @pl.when(step == 0)
    def _():
        own[...] = jnp.zeros_like(own)
        panel[...] = jnp.zeros_like(panel)
        pivot[...] = jnp.zeros_like(pivot)

    def block(b):
        return all_ref[:, 0, b * piece : (b + 1) * piece, :].reshape(imps, width)

    elim = jnp.concatenate([block(b) for b in range(row_blocks, blocks)], axis=1)
    elim_t = elim.T
    for b in range(row_blocks):
        at = slice(b * width, (b + 1) * width)
        panel[:, at] += dot(elim_t, block(b), NN)
    pivot[...] += dot(elim_t, elim, NN)

    @pl.when(step % 2 == at_ref[3])
    def _():
        mine_t = near_ref[0].T
        for b in range(blocks):
            at = slice(b * width, (b + 1) * width)
            own[:, at] += dot(mine_t, block(b), NN)


def gram_sums(at, gathered, near):
    feat, samp, held, width = gathered.shape
    imps = near.shape[1]
    rows = width * feat // samp
    fixed = lambda i, at_ref: (0, 0)
    shapes = [(width, rows + PANEL), (PANEL, rows), (PANEL, PANEL)]
    return pl.pallas_call(
        gram_body,
        out_shape=[jax.ShapeDtypeStruct(s, f32) for s in shapes],
        grid_spec=pltpu.PrefetchScalarGridSpec(
            num_scalar_prefetch=1,
            grid=(samp,),
            in_specs=[
                pl.BlockSpec((feat, 1, held, width), lambda i, at_ref: (0, i, 0, 0)),
                pl.BlockSpec((1, imps, width), lambda i, at_ref: (i // 2, 0, 0)),
            ],
            out_specs=[pl.BlockSpec(s, fixed) for s in shapes],
        ),
        compiler_params=pltpu.CompilerParams(vmem_limit_bytes=32 << 20),
        cost_estimate=pl.CostEstimate(flops=20 * 10**9, bytes_accessed=30 << 20, transcendentals=0),
        name="gram_sums",
    )(at, gathered, near)


def finish_body(
    count, at_ref, all_ref, far0, far1, far2, far3, near_sum, panel, inv_ref, m_ref, mk_ref,
    schur_ref, factor_ref, red_ref, far_sum, mine_ref,
):
    step = pl.program_id(0)
    imps, width = far0.shape
    piece = imps // all_ref.shape[0]
    rows = panel.shape[1]
    blocks = (rows + PANEL) // width
    for k, ref in enumerate((far0, far1, far2, far3)):

        @pl.when(((step - at_ref[4]) & 3) == k)
        def _():
            mine_ref[...] = ref[...].T

    mine_t = mine_ref[...]
    for b in range(blocks):
        at = slice(b * width, (b + 1) * width)
        part = dot(
            mine_t, all_ref[:, 0, b * piece : (b + 1) * piece, :].reshape(imps, width), NN
        )
        far_sum[:, at] = jnp.where(step == 0, part, far_sum[:, at] + part)

    @pl.when(step == pl.num_programs(0) - 1)
    def _():
        row0, col0, first = at_ref[0], at_ref[1], at_ref[2]
        scale = 1.0 / count

        def diagonal(shape, r0, c0):
            r = r0 + lax.broadcasted_iota(jnp.int32, shape, 0)
            c = c0 + lax.broadcasted_iota(jnp.int32, shape, 1)
            return jnp.where(r == c, ridge, 0.0)

        own = (near_sum[...] + far_sum[...]) * scale
        inv = split(inv_ref[...])
        cross = own[:, rows:] + diagonal((width, PANEL), col0, first)
        cross = dot3(split(cross), inv, NT)
        cross_parts = split(cross)
        for lo in range(0, rows, width):
            at = slice(lo, lo + width)
            cols = panel[:, at].T * scale + diagonal((width, PANEL), row0 + lo, first)
            factor = dot3(split(cols), inv, NT)
            factor_ref[at, :] = factor
            gram = own[:, at].T + diagonal((width, width), row0 + lo, col0)
            schur_ref[at, :] = gram - dot3(split(factor), cross_parts, NT)
        elim = jnp.broadcast_to(mk_ref[...], (8, PANEL))
        solved = dot(elim, inv_ref[...], NT, precision=HIGHEST)
        part = dot(solved, cross, NT, precision=HIGHEST)
        red_ref[...] = (m_ref[...] - part[:1]) * (count**0.5)


def finish(count, at, gathered, far, near_sum, panel, inv, m, mk):
    feat, samp, held, width = gathered.shape
    imps = far[0].shape[0]
    rows = width * feat // samp
    fixed = lambda i, at_ref: (0, 0)
    outs = [(rows, width), (rows, PANEL), (1, width)]
    whole = list(far) + [near_sum, panel, inv, m, mk]
    return pl.pallas_call(
        lambda *refs: finish_body(count, *refs),
        out_shape=[jax.ShapeDtypeStruct(s, f32) for s in outs],
        grid_spec=pltpu.PrefetchScalarGridSpec(
            num_scalar_prefetch=1,
            grid=(len(far),),
            in_specs=[
                pl.BlockSpec(
                    (feat, 1, held, width), lambda i, at_ref: (0, 2 * i + 1 - at_ref[3], 0, 0)
                )
            ]
            + [pl.BlockSpec(a.shape, fixed) for a in whole],
            out_specs=[pl.BlockSpec(s, fixed) for s in outs],
            scratch_shapes=[
                pltpu.VMEM((width, rows + PANEL), f32),
                pltpu.VMEM((width, imps), bf16),
            ],
        ),
        compiler_params=pltpu.CompilerParams(vmem_limit_bytes=44 << 20),
        cost_estimate=pl.CostEstimate(flops=9 * 10**9, bytes_accessed=24 << 20, transcendentals=0),
        name="finish",
    )(at, gathered, *whole)


def per_device(embeddings, frequencies, phases, treat_freq, treatment, flips, panel):
    imps = embeddings.shape[0]
    width = frequencies.shape[1]
    samp = lax.axis_size(SAMP)
    feat = lax.axis_size(FEAT)
    samp_index = lax.axis_index(SAMP)
    feat_index = lax.axis_index(FEAT)
    count = imps * samp
    rows = width * feat // samp
    piece = imps // feat
    elim = PANEL // width

    project = jnp.dot(embeddings, frequencies, preferred_element_type=f32)
    treated = treatment.astype(f32)
    flipped = flips.astype(f32)
    counter = treated + flipped - 2.0 * treated * flipped
    base = project + phases[None, :]
    observed = cosine(base + treated[:, None] * treat_freq[None, :])
    counterfactual = cosine(base + counter[:, None] * treat_freq[None, :])
    moment_part = jnp.sum(counterfactual - observed, axis=0)
    feature = observed.astype(bf16)

    near = lax.all_gather(feature, "x")

    shares = lax.all_to_all(
        feature.reshape(feat, piece, width), FEAT, split_axis=0, concat_axis=0, tiled=True
    )
    first_dev = panel[0] * elim
    picked = lax.dynamic_slice_in_dim(shares, first_dev, elim, 0).reshape(1, elim * piece, width)
    send = jnp.concatenate(
        [
            shares.reshape(samp, feat // samp * piece, width),
            jnp.broadcast_to(picked, (samp, elim * piece, width)),
        ],
        axis=1,
    )
    share = lax.all_to_all(send, SAMP, split_axis=0, concat_axis=0, tiled=True)
    share, near = lax.optimization_barrier((share, near))
    gathered = lax.all_gather(share, FEAT)

    share, moment_part = lax.optimization_barrier((share, moment_part))
    moment = lax.psum(moment_part, SAMP) / count
    moments = lax.all_gather(lax.all_gather(moment, ("zl", "core")), "y").reshape(-1)
    moment_panel = lax.dynamic_slice_in_dim(moments, panel[0] * PANEL, PANEL, 0)

    gathered, feature = lax.optimization_barrier((gathered, feature))
    swapped = lax.ppermute(feature, "zh", [(0, 1), (1, 0)])
    at = jnp.stack(
        [
            samp_index * rows,
            feat_index * width,
            panel[0] * PANEL,
            lax.axis_index("zh"),
            lax.axis_index("x"),
        ]
    ).astype(jnp.int32)
    near_sum, panel_sum, pivot_sum = gram_sums(at, gathered, near)
    swapped, pivot_sum = lax.optimization_barrier((swapped, pivot_sum))
    xs = lax.axis_size("x")
    far = [swapped] + [
        lax.ppermute(swapped, "x", [(i, (i - r) % xs) for i in range(xs)]) for r in range(1, xs)
    ]
    inv = inverse_factor(pivot_sum / count + ridge * jnp.eye(PANEL, dtype=f32))
    schur, factor, reduced = finish(
        count, at, gathered, far, near_sum, panel_sum, inv, moment[None], moment_panel[None]
    )
    return (schur, factor, reduced[0])


def solution(mesh):
    fine = Mesh(mesh.devices.reshape(4, 2, 4, 4, 2), ("x", "zh", "y", "zl", "core"))
    return jax.shard_map(
        per_device,
        mesh=fine,
        in_specs=(P(SAMP, None), P(None, FEAT), P(FEAT), P(FEAT), P(SAMP), P(SAMP), P()),
        out_specs=(P(SAMP, FEAT), P(SAMP, None), P(FEAT)),
        check_vma=False,
    )
```

time: 331 us -> 302 us (0.912)
  waiting for transfers between devices: 194 us -> 109 us
  blocking collectives: 31.9 us -> 76.1 us
  Pallas kernels: 68.7 us -> 74.2 us
  starting transfers between devices: 14.6 us -> 19.7 us
    all_gather x1, waiting for transfers between devices: 152 us -> 93 us  [per_device(): gathered = lax.all_gather(share, FEAT)]
    ppermute x1, waiting for transfers between devices: 31.8 us -> 0.01 us  [per_device(): swapped = lax.ppermute(feature, 'zh', [(0, 1), (1, 0)])]
    all_gather x0 -> x2, blocking collectives: none -> 25.6 us  [the longest x1 16.6 us: per_device(): lax.all_gather(moment, ('zl', 'core'))]
    psum x0 -> x1, blocking collectives: none -> 20.7 us  [per_device(): moment = lax.psum(moment_part, SAMP) / count]
    all_to_all x1, waiting for transfers between devices: 3.12 us -> 16.1 us  [per_device(): lax.all_to_all(feature.reshape(feat, piece, width), FEAT, split_axis=0, c...]
    all_gather x1 -> x0, waiting for transfers between devices: 6.15 us -> none  [per_device(): far = lax.all_gather(swapped, 'x')]
    pallas_call x1 -> x3, Pallas kernels: 68.7 us -> 74.2 us  [the longest x1 37.2 us: inverse_factor(): pl.pallas_call(invert_body, out_shape=jax.ShapeDtypeStruct((n, n), f32),...]
    ppermute x0 -> x3, starting transfers between devices: none -> 4.86 us  [per_device(): lax.ppermute(swapped, 'x', [(i, (i - r) % xs) for i in range(xs)])]
  transfers between devices with their start and end apart: 5 -> 7, of which waited for: 4 -> 2; matrix products, arithmetic and copies ran while one was open for 0% -> 0% of each run, Pallas kernels for 0% -> 20%
where the time goes in v4:
time: 302 us; the launch traced here: 301 us
  waiting for transfers between devices  109 us (36%)
  blocking collectives  76.1 us (25%)
  Pallas kernels  74.2 us (25%)
  starting transfers between devices  19.7 us (7%)
  between operations  14.8 us (5%)
  matrix products  3.84 us (1%)
    all_gather x1, waiting for transfers between devices, per_device(): gathered = lax.all_gather(share, FEAT)  93 us
    pallas_call x1, Pallas kernels, inverse_factor(): pl.pallas_call(invert_body, out_shape=jax.ShapeDtypeStruct((n, n), f32),...  37.2 us
    all_to_all x1, blocking collectives, per_device(): share = lax.all_to_all(send, SAMP, split_axis=0, concat_axis=0, tiled=True)  29.8 us
    pallas_call x1, Pallas kernels, gram_sums(): pl.pallas_call(gram_body, out_shape=[jax.ShapeDtypeStruct(s, f32) for s i...  21.6 us
    psum x1, blocking collectives, per_device(): moment = lax.psum(moment_part, SAMP) / count  20.7 us
    all_gather x1, blocking collectives, per_device(): lax.all_gather(moment, ('zl', 'core'))  16.6 us
    all_to_all x1, waiting for transfers between devices, per_device(): lax.all_to_all(feature.reshape(feat, piece, width), FEAT, split_axis=0, c...  16.1 us
    pallas_call x1, Pallas kernels, finish(): pl.pallas_call(lambda *refs: finish_body(count, *refs), out_shape=[jax.Sh...  15.4 us
  transfers between devices with their start and end apart: 7, of which 2 were waited for; matrix products, arithmetic and copies ran while one was open for 0% of the time, Pallas kernels for 20%

profile of v4, /device:TPU:1, one launch (start us, length us, event | category | flops | bytes accessed | tf_op | source)
XLA Modules:
  0.0 301.4 jit_solution(12690554435894756353)
XLA Ops:
  7.2 0.0 copy-start
  7.2 0.0 all-gather.8.cloned.1.call-start
  7.2 0.8 convert_element_type.10
  8.1 0.7 multiply_subtract_fusion
  8.8 0.0 copy-done
  8.8 3.8 %subtract_reduce_fusion = (f32[256]{0:T(256)S(1)}, bf16[1024,256]{1,0:T(8,128)(2,1)}) fusion(f32[1024]{0:T(1024)S(1)} %multiply_subtract_fusion, f32[256]{0:T(256)} %param.10, f32[1024]{0:T(1024)S(1)} %convert_element_type.10, f32[256]{0:T(256)} %param.9, bf16[1024,1024]{1,0:T(8,128)(2,1)S(1)} %copy-done, bf16[1024,256]{1,0:T(8,128)(2,1)} %param.8), kind=kOutput, calls=%fused_computation.7 | convolution fusion | flops 547880704 | bytes 3156992 | tf_op jit(solution)/shard_map/dot_general | solution.py:268
  12.6 0.0 all-gather.8.cloned.1.call-update
  12.6 10.2 %all-to-all-start = ((bf16[32,32,256]{2,1,0:T(8,128)(2,1)}), bf16[32,32,256]{2,1,0:T(8,128)(2,1)S(1)}, u32[]{:S(2)}, u32[]{:S(2)}) async-start(bf16[32,32,256]{2,1,0:T(8,128)(2,1)} %bitcast.27), calls=%async_computation | async-start | bytes 1048576 | tf_op jit(solution)/shard_map/all_to_all | solution.py:280
  22.9 0.0 all-gather.10.cloned.1.call-start
  23.6 16.1 %all-to-all-done = bf16[32,32,256]{2,1,0:T(8,128)(2,1)S(1)} async-done(((bf16[32,32,256]{2,1,0:T(8,128)(2,1)}), bf16[32,32,256]{2,1,0:T(8,128)(2,1)S(1)}, u32[]{:S(2)}, u32[]{:S(2)}) %all-to-all-start) | async-done | bytes 524320 | tf_op jit(solution)/shard_map/all_to_all | solution.py:280
  39.7 0.0 copy-start.2
  39.7 0.1 pad_maximum_fusion
  39.8 29.8 %all_to_all.10 = bf16[8,192,256]{2,1,0:T(8,128)(2,1)} all-to-all(bf16[8,192,256]{2,1,0:T(8,128)(2,1)S(1)} %pad_maximum_fusion), channel_id=1, replica_groups=mesh['x'=4,'zh'=2,'y'=4,'zl'=4,'core'=2] {'x','zh'}, dimensions={0} | all-to-all | bytes 1572864 | tf_op jit(solution)/shard_map/all_to_all | solution.py:292
  69.5 0.0 all-gather.10.cloned.1.call-update
  69.6 0.1 stack.20.at_ref.refs_0_
  69.7 20.7 %psum.7 = f32[256]{0:T(256)S(1)} all-reduce(f32[256]{0:T(256)S(1)} %get-tuple-element.25), channel_id=1, replica_groups=mesh['x'=4,'zh'=2,'y'=4,'zl'=4,'core'=2] {'x','zh'}, use_global_device_ids=true, to_apply=%region_1.2 | all-reduce | flops 256 | bytes 2048 | tf_op jit(solution)/shard_map/psum | solution.py:297
  90.4 16.6 %all-gather.4 = f32[8,1,256]{2,1,0:T(1,128)S(1)} all-gather(f32[1,1,256]{2,1,0:T(1,128)S(1)} %bitcast.22), channel_id=4, replica_groups=mesh['x'=4,'zh'=2,'y'=4,'zl'=4,'core'=2] {'zl','core'}, dimensions={0}, use_global_device_ids=true | all-gather | bytes 9216 | tf_op jit(solution)/shard_map/all_gather | solution.py:298
  107.0 9.0 %all-gather.3 = f32[32,256]{1,0:T(8,128)S(1)} all-gather(f32[8,256]{1,0:T(8,128)S(1)} %bitcast.31), channel_id=5, replica_groups=mesh['x'=4,'zh'=2,'y'=4,'zl'=4,'core'=2] {'y'}, dimensions={0}, use_global_device_ids=true | all-gather | bytes 40960 | tf_op jit(solution)/shard_map/all_gather | solution.py:298
  116.0 0.1 dynamic_slice.7
  116.1 93.0 %all-gather.10.cloned.1.call-done = bf16[256,192,256]{2,1,0:T(8,128)(2,1)} async-done(((bf16[8,192,256]{2,1,0:T(8,128)(2,1)}), bf16[256,192,256]{2,1,0:T(8,128)(2,1)}) %all-gather.10.cloned.1.call-update) | async-done | bytes 25165840 | tf_op jit(solution)/shard_map/all_gather | solution.py:294
  209.1 4.6 %collective-permute-start = (bf16[1024,256]{1,0:T(8,128)(2,1)S(1)}, bf16[1024,256]{1,0:T(8,128)(2,1)S(1)}, u32[]{:S(2)}, u32[]{:S(2)}) collective-permute-start(bf16[1024,256]{1,0:T(8,128)(2,1)S(1)} %copy-done.2), channel_id=1, source_target_pairs={{0,32},{32,0},{1,33},{33,1},{2,34},{34,2},{3,35},{35,3},{4,36},{36... | collective-permute-start | bytes 1572872 | tf_op jit(solution)/shard_map/ppermute | solution.py:302
  213.7 1.6 copy-done.1
  215.3 21.6 %gram_sums.1 = (f32[256,1536]{1,0:T(8,128)S(1)}, f32[512,1024]{1,0:T(8,128)S(1)}, f32[512,512]{1,0:T(8,128)S(1)}) custom-call(s32[5]{0:T(128)S(1)} %stack.20.at_ref.refs_0_, bf16[32,8,192,256]{3,2,1,0:T(8,128)(2,1)} %bitcast.32, bf16[4,1024,256]{2,1,0:T(8,128)(2,1)S(1)} %bitcast.25), custom_call_target="tpu_custom_call" | custom-call | flops 20000000000 | bytes 31457280 | tf_op jit(solution)/shard_map/gram_sums/pallas_call | solution.py:156
  236.9 0.0 collective-permute-done.refs_2_
  237.0 1.3 collective-permute-start.3
  238.2 2.4 collective-permute-start.2
  240.6 1.2 collective-permute-start.1
  241.8 0.1 select_add_fusion.a_ref
  241.9 37.2 %inverse_factor.1.refs_8_ = f32[512,512]{1,0:T(8,128)S(1)} custom-call(f32[512,512]{1,0:T(8,128)S(1)} %select_add_fusion.a_ref), custom_call_target="tpu_custom_call" | custom-call | flops 30000001024 | bytes 2097152 | tf_op jit(solution)/shard_map/inverse_factor/pallas_call | solution.py:92
  279.2 0.0 collective-permute-done.3.refs_5_
  279.2 0.0 collective-permute-done.2.refs_4_
  279.2 15.4 %finish.1 = (f32[1024,256]{1,0:T(8,128)}, f32[1024,512]{1,0:T(8,128)}, f32[1,256]{1,0:T(1,128)}) custom-call(s32[5]{0:T(128)S(1)} %stack.20.at_ref.refs_0_, bf16[32,8,192,256]{3,2,1,0:T(8,128)(2,1)} %bitcast.33, bf16[1024,256]{1,0:T(8,128)(2,1)S(1)} %collective-permute-done.refs_2_, bf16[1024,256]{1,0:T(8,128)(2,1)S(1)} %collective-permute-done.1.refs_3_, ...), custom_call_target="tpu_custom_call" | custom-call | flops 8999999488 | bytes 25165824 | tf_op jit(solution)/shard_map/finish/pallas_call | solution.py:232
  (9 shorter events, 0.1 us)
Async XLA Ops:
  7.2 1.6 copy-start
  7.2 62.4 %all-gather.8.cloned.1.call-start = ((), (), s32[]{:S(2)}) async-start(), calls=%async_computation.2 | async-start | bytes 2621440 | tf_op jit(solution)/shard_map/all_gather | solution.py:278
  12.6 27.0 %all-to-all-start = ((bf16[32,32,256]{2,1,0:T(8,128)(2,1)}), bf16[32,32,256]{2,1,0:T(8,128)(2,1)S(1)}, u32[]{:S(2)}, u32[]{:S(2)}) async-start(bf16[32,32,256]{2,1,0:T(8,128)(2,1)} %bitcast.27), calls=%async_computation | async-start | bytes 1048576 | tf_op jit(solution)/shard_map/all_to_all | solution.py:280
  22.9 186.3 %all-gather.10.cloned.1.call-start = ((), (), s32[]{:S(2)}) async-start(), calls=%async_computation.3 | async-start | bytes 25952256 | tf_op jit(solution)/shard_map/all_gather | solution.py:294
  39.7 169.5 %copy-start.2 = (bf16[1024,256]{1,0:T(8,128)(2,1)S(1)}, bf16[1024,256]{1,0:T(8,128)(2,1)}, u32[]{:S(2)}) copy-start(bf16[1024,256]{1,0:T(8,128)(2,1)} %get-tuple-element.18) | copy-start | bytes 1572868
  209.1 27.8 %collective-permute-start = (bf16[1024,256]{1,0:T(8,128)(2,1)S(1)}, bf16[1024,256]{1,0:T(8,128)(2,1)S(1)}, u32[]{:S(2)}, u32[]{:S(2)}) collective-permute-start(bf16[1024,256]{1,0:T(8,128)(2,1)S(1)} %copy-done.2), channel_id=1, source_target_pairs={{0,32},{32,0},{1,33},{33,1},{2,34},{34,2},{3,35},{35,3},{4,36},{36... | collective-permute-start | bytes 1572872 | tf_op jit(solution)/shard_map/ppermute | solution.py:302
  213.7 1.6 copy-start.1
  237.0 42.2 %collective-permute-start.3 = (bf16[1024,256]{1,0:T(8,128)(2,1)S(1)}, bf16[1024,256]{1,0:T(8,128)(2,1)S(1)}, u32[]{:S(2)}, u32[]{:S(2)}) collective-permute-start(bf16[1024,256]{1,0:T(8,128)(2,1)S(1)} %collective-permute-done.refs_2_), channel_id=1, source_target_pairs={{0,64},{64,128},{128,192},{192,0},{1,65},{65,129},{129,193},{193,1... | collective-permute-start | bytes 1572872 | tf_op jit(solution)/shard_map/ppermute | solution.py:316
  238.2 41.0 %collective-permute-start.2 = (bf16[1024,256]{1,0:T(8,128)(2,1)S(1)}, bf16[1024,256]{1,0:T(8,128)(2,1)S(1)}, u32[]{:S(2)}, u32[]{:S(2)}) collective-permute-start(bf16[1024,256]{1,0:T(8,128)(2,1)S(1)} %collective-permute-done.refs_2_), channel_id=1, source_target_pairs={{0,128},{64,192},{128,0},{192,64},{1,129},{65,193},{129,1},{193,65... | collective-permute-start | bytes 1572872 | tf_op jit(solution)/shard_map/ppermute | solution.py:316
  240.6 38.6 %collective-permute-start.1 = (bf16[1024,256]{1,0:T(8,128)(2,1)S(1)}, bf16[1024,256]{1,0:T(8,128)(2,1)S(1)}, u32[]{:S(2)}, u32[]{:S(2)}) collective-permute-start(bf16[1024,256]{1,0:T(8,128)(2,1)S(1)} %collective-permute-done.refs_2_), channel_id=1, source_target_pairs={{0,192},{64,0},{128,64},{192,128},{1,193},{65,1},{129,65},{193,129... | collective-permute-start | bytes 1572872 | tf_op jit(solution)/shard_map/ppermute | solution.py:316
Sparse Core Ops, SparseCore 0:
  12.8 37.1 all-gather.7
  69.7 139.4 all-gather.9

commit v5 on v4

--- a/solution.py
+++ b/solution.py
@@ -39,7 +39,22 @@
     return lax.dot_general(left, right, (dims, ((), ())), preferred_element_type=f32, **kw)
 
 
-def invert_body(a_ref, out_ref, work, diag):
+def split(a):
+    high = a.astype(bf16)
+    return high, (a - high.astype(f32)).astype(bf16)
+
+
+def dot3(left, right, dims):
+    lh, ll = left
+    rh, rl = right
+    return dot(lh, rh, dims) + (dot(lh, rl, dims) + dot(ll, rh, dims))
+
+
+NN = ((1,), (0,))
+NT = ((1,), (1,))
+
+
+def eliminate(a_ref, out_ref, work, diag):
     n = a_ref.shape[0]
     nb = 128
     work[:, :n] = a_ref[...]
@@ -55,28 +70,36 @@
         hi = lo + nb
         diag[:, :nb] = work[lo:hi, lo:hi]
         diag[:, nb:] = eye
-        for q in range(0, nb, 8):
-            ra = diag[q : q + 8, :nb]
-            rb = diag[q : q + 8, nb:]
-            cols = [jnp.broadcast_to(ra[:, q + c : q + c + 1], (8, nb)) for c in range(8)]
+
+        def slab(k, carry):
+            q = pl.multiple_of(8 * k, 8)
+            ra = diag[pl.ds(q, 8), :nb]
+            rb = diag[pl.ds(q, 8), nb:]
+            cols = [
+                jnp.broadcast_to(
+                    jnp.sum(jnp.where(lane == q + c, ra, 0.0), axis=1, keepdims=True), (8, nb)
+                )
+                for c in range(8)
+            ]
             pivots = jnp.ones((8, nb), f32)
             for c in range(8):
                 d = jnp.broadcast_to(cols[c][c : c + 1, :], (8, nb))
                 pivots = jnp.where(sub == c, d, pivots)
-                if c < 7:
-                    mult = jnp.where(sub > c, cols[c] / d, 0.0)
-                    for e in range(c + 1, 8):
-                        cols[e] = cols[e] - mult * jnp.broadcast_to(cols[e][c : c + 1, :], (8, nb))
-                    ra = ra - mult * jnp.broadcast_to(ra[c : c + 1, :], (8, nb))
-                    rb = rb - mult * jnp.broadcast_to(rb[c : c + 1, :], (8, nb))
+                mult = jnp.where(sub > c, cols[c] / d, 0.0)
+                for e in range(c + 1, 8):
+                    cols[e] = cols[e] - mult * jnp.broadcast_to(cols[e][c : c + 1, :], (8, nb))
+                ra = ra - mult * jnp.broadcast_to(ra[c : c + 1, :], (8, nb))
+                rb = rb - mult * jnp.broadcast_to(rb[c : c + 1, :], (8, nb))
             scale = lax.rsqrt(pivots)
             ra = ra * scale
             rb = rb * scale
-            diag[q : q + 8, nb:] = rb
-            if q + 8 < nb:
-                low = jnp.where(lane >= q + 8, ra, 0.0)
-                update = dot(low, jnp.concatenate([low, rb], 1), ((0,), (0,)), precision=HIGHEST)
-                diag[q + 8 :, :] = diag[q + 8 :, :] - update[q + 8 :, :]
+            diag[pl.ds(q, 8), nb:] = rb
+            low = jnp.where(lane >= q + 8, ra, 0.0)
+            update = dot(low, jnp.concatenate([low, rb], 1), ((0,), (0,)), precision=HIGHEST)
+            diag[...] = diag[...] - update
+            return carry
+
+        lax.fori_loop(0, nb // 8, slab, 0)
         upper = dot(diag[:, nb:], work[lo:hi, hi : n + hi], ((1,), (0,)), precision=HIGHEST)
         rest = n - hi
         out_ref[lo:hi, :hi] = upper[:, rest:]
@@ -87,31 +110,66 @@
             out_ref[lo:hi, hi:] = jnp.zeros((nb, rest), f32)
 
 
+def inverse_body(a_ref, out_ref, work, diag, s_ref, t_ref):
+    n = a_ref.shape[0]
+    row = lax.broadcasted_iota(jnp.int32, (n, n), 0)
+    col = lax.broadcasted_iota(jnp.int32, (n, n), 1)
+    eye = row == col
+    a = a_ref[...]
+    picked = jnp.where(eye, a, 0.0)
+    scale = lax.rsqrt(jnp.sum(picked, axis=0, keepdims=True))
+    s_ref[...] = a * scale * lax.rsqrt(jnp.sum(picked, axis=1, keepdims=True))
+
+    def lower(e):
+        return jnp.where(row > col, e, jnp.where(eye, 0.5 * e, 0.0))
+
+    one = eye.astype(f32)
+    t_ref[...] = one - lower(s_ref[...] - one)
+    s_high = s_ref[...].astype(bf16)
+    for _ in range(2):
+        t = t_ref[...].astype(bf16)
+        e = dot(dot(t, s_high, NN).astype(bf16), t, NT) - one
+        t_ref[...] = t_ref[...] - dot(lower(e).astype(bf16), t, NN)
+
+    def unsettled(state):
+        step, error = state
+        return jnp.logical_and(step < 8, jnp.logical_not(error <= 1.6e-5))
+
+    def refine(state):
+        t = split(t_ref[...])
+        e = dot3(split(dot3(t, split(s_ref[...]), NN)), t, NT) - one
+        t_ref[...] = t_ref[...] - dot3(split(lower(e)), t, NN)
+        return state[0] + 1, jnp.sum(e * e)
+
+    _, error = lax.while_loop(unsettled, refine, (jnp.int32(0), jnp.float32(1.0)))
+    t = t_ref[...]
+    smallest = jnp.min(jnp.where(eye, t, 1.0))
+    good = jnp.logical_and(error <= 1.6e-5, smallest > 0.0)
+
+    @pl.when(good)
+    def _():
+        out_ref[...] = t_ref[...] * scale
+
+    @pl.when(jnp.logical_not(good))
+    def _():
+        eliminate(a_ref, out_ref, work, diag)
+
+
 def inverse_factor(pivot):
     n = pivot.shape[0]
     return pl.pallas_call(
-        invert_body,
+        inverse_body,
         out_shape=jax.ShapeDtypeStruct((n, n), f32),
-        scratch_shapes=[pltpu.VMEM((n, 2 * n), f32), pltpu.VMEM((128, 256), f32)],
-        compiler_params=pltpu.CompilerParams(vmem_limit_bytes=16 << 20),
+        scratch_shapes=[
+            pltpu.VMEM((n, 2 * n), f32),
+            pltpu.VMEM((128, 256), f32),
+            pltpu.VMEM((n, n), f32),
+            pltpu.VMEM((n, n), f32),
+        ],
+        compiler_params=pltpu.CompilerParams(vmem_limit_bytes=32 << 20),
         cost_estimate=pl.CostEstimate(flops=30 * 10**9, bytes_accessed=2 << 20, transcendentals=0),
         name="inverse_factor",
     )(pivot)
-
-
-def split(a):
-    high = a.astype(bf16)
-    return high, (a - high.astype(f32)).astype(bf16)
-
-
-def dot3(left, right, dims):
-    lh, ll = left
-    rh, rl = right
-    return dot(lh, rh, dims) + (dot(lh, rl, dims) + dot(ll, rh, dims))
-
-
-NN = ((1,), (0,))
-NT = ((1,), (1,))
 
 
 def gram_body(at_ref, all_ref, near_ref, own, panel, pivot):

time: 302 us -> 322 us (1.066)
  Pallas kernels: 74.2 us -> 94 us
    pallas_call x1, Pallas kernels: 37.2 us -> 57 us  [inverse_factor(): pl.pallas_call(inverse_body, out_shape=jax.ShapeDtypeStruct((n, n), f32),...]
  transfers between devices with their start and end apart: 7 -> 7, of which waited for: 2 -> 2; matrix products, arithmetic and copies ran while one was open for 0% -> 0% of each run, Pallas kernels for 20% -> 24%
where the time goes in v5:
time: 322 us; the launch traced here: 321 us
  waiting for transfers between devices  109 us (34%)
  Pallas kernels  94 us (29%)
  blocking collectives  76.1 us (24%)
  starting transfers between devices  19.7 us (6%)
  between operations  14.8 us (5%)
  matrix products  3.84 us (1%)
    all_gather x1, waiting for transfers between devices, per_device(): gathered = lax.all_gather(share, FEAT)  93 us
    pallas_call x1, Pallas kernels, inverse_factor(): pl.pallas_call(inverse_body, out_shape=jax.ShapeDtypeStruct((n, n), f32),...  57 us
    all_to_all x1, blocking collectives, per_device(): share = lax.all_to_all(send, SAMP, split_axis=0, concat_axis=0, tiled=True)  29.8 us
    pallas_call x1, Pallas kernels, gram_sums(): pl.pallas_call(gram_body, out_shape=[jax.ShapeDtypeStruct(s, f32) for s i...  21.6 us
    psum x1, blocking collectives, per_device(): moment = lax.psum(moment_part, SAMP) / count  20.7 us
    all_gather x1, blocking collectives, per_device(): lax.all_gather(moment, ('zl', 'core'))  16.6 us
    all_to_all x1, waiting for transfers between devices, per_device(): lax.all_to_all(feature.reshape(feat, piece, width), FEAT, split_axis=0, c...  16.1 us
    pallas_call x1, Pallas kernels, finish(): pl.pallas_call(lambda *refs: finish_body(count, *refs), out_shape=[jax.Sh...  15.4 us
  transfers between devices with their start and end apart: 7, of which 2 were waited for; matrix products, arithmetic and copies ran while one was open for 0% of the time, Pallas kernels for 24%

profile of v5, /device:TPU:1, one launch (start us, length us, event | category | flops | bytes accessed | tf_op | source)
XLA Modules:
  0.0 321.2 jit_solution(9341327487535861369)
XLA Ops:
  7.2 0.0 copy-start
  7.2 0.0 all-gather.8.cloned.1.call-start
  7.2 0.8 convert_element_type.10
  8.1 0.7 multiply_subtract_fusion
  8.8 0.0 copy-done
  8.8 3.8 %subtract_reduce_fusion = (f32[256]{0:T(256)S(1)}, bf16[1024,256]{1,0:T(8,128)(2,1)}) fusion(f32[1024]{0:T(1024)S(1)} %multiply_subtract_fusion, f32[256]{0:T(256)} %param.10, f32[1024]{0:T(1024)S(1)} %convert_element_type.10, f32[256]{0:T(256)} %param.9, bf16[1024,1024]{1,0:T(8,128)(2,1)S(1)} %copy-done, bf16[1024,256]{1,0:T(8,128)(2,1)} %param.8), kind=kOutput, calls=%fused_computation.7 | convolution fusion | flops 547880704 | bytes 3156992 | tf_op jit(solution)/shard_map/dot_general | solution.py:326
  12.6 0.0 all-gather.8.cloned.1.call-update
  12.6 10.2 %all-to-all-start = ((bf16[32,32,256]{2,1,0:T(8,128)(2,1)}), bf16[32,32,256]{2,1,0:T(8,128)(2,1)S(1)}, u32[]{:S(2)}, u32[]{:S(2)}) async-start(bf16[32,32,256]{2,1,0:T(8,128)(2,1)} %bitcast.27), calls=%async_computation | async-start | bytes 1048576 | tf_op jit(solution)/shard_map/all_to_all | solution.py:338
  22.9 0.0 all-gather.10.cloned.1.call-start
  23.6 16.1 %all-to-all-done = bf16[32,32,256]{2,1,0:T(8,128)(2,1)S(1)} async-done(((bf16[32,32,256]{2,1,0:T(8,128)(2,1)}), bf16[32,32,256]{2,1,0:T(8,128)(2,1)S(1)}, u32[]{:S(2)}, u32[]{:S(2)}) %all-to-all-start) | async-done | bytes 524320 | tf_op jit(solution)/shard_map/all_to_all | solution.py:338
  39.7 0.0 copy-start.2
  39.7 0.1 pad_maximum_fusion
  39.8 29.8 %all_to_all.10 = bf16[8,192,256]{2,1,0:T(8,128)(2,1)} all-to-all(bf16[8,192,256]{2,1,0:T(8,128)(2,1)S(1)} %pad_maximum_fusion), channel_id=1, replica_groups=mesh['x'=4,'zh'=2,'y'=4,'zl'=4,'core'=2] {'x','zh'}, dimensions={0} | all-to-all | bytes 1572864 | tf_op jit(solution)/shard_map/all_to_all | solution.py:350
  69.5 0.0 all-gather.10.cloned.1.call-update
  69.6 0.1 stack.20.at_ref.refs_0_
  69.7 20.7 %psum.7 = f32[256]{0:T(256)S(1)} all-reduce(f32[256]{0:T(256)S(1)} %get-tuple-element.25), channel_id=1, replica_groups=mesh['x'=4,'zh'=2,'y'=4,'zl'=4,'core'=2] {'x','zh'}, use_global_device_ids=true, to_apply=%region_1.2 | all-reduce | flops 256 | bytes 2048 | tf_op jit(solution)/shard_map/psum | solution.py:355
  90.4 16.6 %all-gather.4 = f32[8,1,256]{2,1,0:T(1,128)S(1)} all-gather(f32[1,1,256]{2,1,0:T(1,128)S(1)} %bitcast.22), channel_id=4, replica_groups=mesh['x'=4,'zh'=2,'y'=4,'zl'=4,'core'=2] {'zl','core'}, dimensions={0}, use_global_device_ids=true | all-gather | bytes 9216 | tf_op jit(solution)/shard_map/all_gather | solution.py:356
  107.0 9.0 %all-gather.3 = f32[32,256]{1,0:T(8,128)S(1)} all-gather(f32[8,256]{1,0:T(8,128)S(1)} %bitcast.31), channel_id=5, replica_groups=mesh['x'=4,'zh'=2,'y'=4,'zl'=4,'core'=2] {'y'}, dimensions={0}, use_global_device_ids=true | all-gather | bytes 40960 | tf_op jit(solution)/shard_map/all_gather | solution.py:356
  116.0 0.1 dynamic_slice.7
  116.1 93.0 %all-gather.10.cloned.1.call-done = bf16[256,192,256]{2,1,0:T(8,128)(2,1)} async-done(((bf16[8,192,256]{2,1,0:T(8,128)(2,1)}), bf16[256,192,256]{2,1,0:T(8,128)(2,1)}) %all-gather.10.cloned.1.call-update) | async-done | bytes 25165840 | tf_op jit(solution)/shard_map/all_gather | solution.py:352
  209.1 4.6 %collective-permute-start = (bf16[1024,256]{1,0:T(8,128)(2,1)S(1)}, bf16[1024,256]{1,0:T(8,128)(2,1)S(1)}, u32[]{:S(2)}, u32[]{:S(2)}) collective-permute-start(bf16[1024,256]{1,0:T(8,128)(2,1)S(1)} %copy-done.2), channel_id=1, source_target_pairs={{0,32},{32,0},{1,33},{33,1},{2,34},{34,2},{3,35},{35,3},{4,36},{36... | collective-permute-start | bytes 1572872 | tf_op jit(solution)/shard_map/ppermute | solution.py:360
  213.7 1.6 copy-done.1
  215.3 21.6 %gram_sums.1 = (f32[256,1536]{1,0:T(8,128)S(1)}, f32[512,1024]{1,0:T(8,128)S(1)}, f32[512,512]{1,0:T(8,128)S(1)}) custom-call(s32[5]{0:T(128)S(1)} %stack.20.at_ref.refs_0_, bf16[32,8,192,256]{3,2,1,0:T(8,128)(2,1)} %bitcast.32, bf16[4,1024,256]{2,1,0:T(8,128)(2,1)S(1)} %bitcast.25), custom_call_target="tpu_custom_call" | custom-call | flops 20000000000 | bytes 31457280 | tf_op jit(solution)/shard_map/gram_sums/pallas_call | solution.py:214
  236.9 0.0 collective-permute-done.refs_2_
  237.0 1.3 collective-permute-start.3
  238.2 2.4 collective-permute-start.2
  240.6 1.2 collective-permute-start.1
  241.8 0.1 select_add_fusion.a_ref
  241.9 57.0 %inverse_factor.1.refs_8_ = f32[512,512]{1,0:T(8,128)S(1)} custom-call(f32[512,512]{1,0:T(8,128)S(1)} %select_add_fusion.a_ref), custom_call_target="tpu_custom_call" | custom-call | flops 30000001024 | bytes 2097152 | tf_op jit(solution)/shard_map/inverse_factor/pallas_call | solution.py:160
  299.0 0.0 collective-permute-done.3.refs_5_
  299.0 0.0 collective-permute-done.1.refs_3_
  299.0 15.4 %finish.1 = (f32[1024,256]{1,0:T(8,128)}, f32[1024,512]{1,0:T(8,128)}, f32[1,256]{1,0:T(1,128)}) custom-call(s32[5]{0:T(128)S(1)} %stack.20.at_ref.refs_0_, bf16[32,8,192,256]{3,2,1,0:T(8,128)(2,1)} %bitcast.33, bf16[1024,256]{1,0:T(8,128)(2,1)S(1)} %collective-permute-done.refs_2_, bf16[1024,256]{1,0:T(8,128)(2,1)S(1)} %collective-permute-done.1.refs_3_, ...), custom_call_target="tpu_custom_call" | custom-call | flops 8999999488 | bytes 25165824 | tf_op jit(solution)/shard_map/finish/pallas_call | solution.py:290
  (9 shorter events, 0.1 us)
Async XLA Ops:
  7.2 1.6 copy-start
  7.2 62.4 %all-gather.8.cloned.1.call-start = ((), (), s32[]{:S(2)}) async-start(), calls=%async_computation.2 | async-start | bytes 2621440 | tf_op jit(solution)/shard_map/all_gather | solution.py:336
  12.6 27.0 %all-to-all-start = ((bf16[32,32,256]{2,1,0:T(8,128)(2,1)}), bf16[32,32,256]{2,1,0:T(8,128)(2,1)S(1)}, u32[]{:S(2)}, u32[]{:S(2)}) async-start(bf16[32,32,256]{2,1,0:T(8,128)(2,1)} %bitcast.27), calls=%async_computation | async-start | bytes 1048576 | tf_op jit(solution)/shard_map/all_to_all | solution.py:338
  22.9 186.3 %all-gather.10.cloned.1.call-start = ((), (), s32[]{:S(2)}) async-start(), calls=%async_computation.3 | async-start | bytes 25952256 | tf_op jit(solution)/shard_map/all_gather | solution.py:352
  39.7 169.5 %copy-start.2 = (bf16[1024,256]{1,0:T(8,128)(2,1)S(1)}, bf16[1024,256]{1,0:T(8,128)(2,1)}, u32[]{:S(2)}) copy-start(bf16[1024,256]{1,0:T(8,128)(2,1)} %get-tuple-element.18) | copy-start | bytes 1572868
  209.1 27.8 %collective-permute-start = (bf16[1024,256]{1,0:T(8,128)(2,1)S(1)}, bf16[1024,256]{1,0:T(8,128)(2,1)S(1)}, u32[]{:S(2)}, u32[]{:S(2)}) collective-permute-start(bf16[1024,256]{1,0:T(8,128)(2,1)S(1)} %copy-done.2), channel_id=1, source_target_pairs={{0,32},{32,0},{1,33},{33,1},{2,34},{34,2},{3,35},{35,3},{4,36},{36... | collective-permute-start | bytes 1572872 | tf_op jit(solution)/shard_map/ppermute | solution.py:360
  213.7 1.6 copy-start.1
  237.0 62.0 %collective-permute-start.3 = (bf16[1024,256]{1,0:T(8,128)(2,1)S(1)}, bf16[1024,256]{1,0:T(8,128)(2,1)S(1)}, u32[]{:S(2)}, u32[]{:S(2)}) collective-permute-start(bf16[1024,256]{1,0:T(8,128)(2,1)S(1)} %collective-permute-done.refs_2_), channel_id=1, source_target_pairs={{0,64},{64,128},{128,192},{192,0},{1,65},{65,129},{129,193},{193,1... | collective-permute-start | bytes 1572872 | tf_op jit(solution)/shard_map/ppermute | solution.py:374
  238.2 60.7 %collective-permute-start.2 = (bf16[1024,256]{1,0:T(8,128)(2,1)S(1)}, bf16[1024,256]{1,0:T(8,128)(2,1)S(1)}, u32[]{:S(2)}, u32[]{:S(2)}) collective-permute-start(bf16[1024,256]{1,0:T(8,128)(2,1)S(1)} %collective-permute-done.refs_2_), channel_id=1, source_target_pairs={{0,128},{64,192},{128,0},{192,64},{1,129},{65,193},{129,1},{193,65... | collective-permute-start | bytes 1572872 | tf_op jit(solution)/shard_map/ppermute | solution.py:374
  240.6 58.3 %collective-permute-start.1 = (bf16[1024,256]{1,0:T(8,128)(2,1)S(1)}, bf16[1024,256]{1,0:T(8,128)(2,1)S(1)}, u32[]{:S(2)}, u32[]{:S(2)}) collective-permute-start(bf16[1024,256]{1,0:T(8,128)(2,1)S(1)} %collective-permute-done.refs_2_), channel_id=1, source_target_pairs={{0,192},{64,0},{128,64},{192,128},{1,193},{65,1},{129,65},{193,129... | collective-permute-start | bytes 1572872 | tf_op jit(solution)/shard_map/ppermute | solution.py:374
Sparse Core Ops, SparseCore 0:
  12.8 37.1 all-gather.7
  69.7 139.4 all-gather.9

commit v6 on v3

--- a/solution.py
+++ b/solution.py
@@ -50,13 +50,14 @@
     return dot(lh, rh, dims) + (dot(lh, rl, dims) + dot(ll, rh, dims))
 
 
+NN = ((1,), (0,))
 NT = ((1,), (1,))
 
 
-def invert(a, out_ref, work, diag):
-    n = a.shape[0]
+def invert_body(a_ref, out_ref, work, diag):
+    n = a_ref.shape[0]
     nb = 128
-    work[:, :n] = a
+    work[:, :n] = a_ref[...]
     row = lax.broadcasted_iota(jnp.int32, (n, n), 0)
     col = lax.broadcasted_iota(jnp.int32, (n, n), 1)
     work[:, n:] = (row == col).astype(f32)
@@ -69,28 +70,36 @@
         hi = lo + nb
         diag[:, :nb] = work[lo:hi, lo:hi]
         diag[:, nb:] = eye
-        for q in range(0, nb, 8):
-            ra = diag[q : q + 8, :nb]
-            rb = diag[q : q + 8, nb:]
-            cols = [jnp.broadcast_to(ra[:, q + c : q + c + 1], (8, nb)) for c in range(8)]
+
+        def slab(k, carry):
+            q = pl.multiple_of(8 * k, 8)
+            ra = diag[pl.ds(q, 8), :nb]
+            rb = diag[pl.ds(q, 8), nb:]
+            cols = [
+                jnp.broadcast_to(
+                    jnp.sum(jnp.where(lane == q + c, ra, 0.0), axis=1, keepdims=True), (8, nb)
+                )
+                for c in range(8)
+            ]
             pivots = jnp.ones((8, nb), f32)
             for c in range(8):
                 d = jnp.broadcast_to(cols[c][c : c + 1, :], (8, nb))
                 pivots = jnp.where(sub == c, d, pivots)
-                if c < 7:
-                    mult = jnp.where(sub > c, cols[c] / d, 0.0)
-                    for e in range(c + 1, 8):
-                        cols[e] = cols[e] - mult * jnp.broadcast_to(cols[e][c : c + 1, :], (8, nb))
-                    ra = ra - mult * jnp.broadcast_to(ra[c : c + 1, :], (8, nb))
-                    rb = rb - mult * jnp.broadcast_to(rb[c : c + 1, :], (8, nb))
+                mult = jnp.where(sub > c, cols[c] / d, 0.0)
+                for e in range(c + 1, 8):
+                    cols[e] = cols[e] - mult * jnp.broadcast_to(cols[e][c : c + 1, :], (8, nb))
+                ra = ra - mult * jnp.broadcast_to(ra[c : c + 1, :], (8, nb))
+                rb = rb - mult * jnp.broadcast_to(rb[c : c + 1, :], (8, nb))
             scale = lax.rsqrt(pivots)
             ra = ra * scale
             rb = rb * scale
-            diag[q : q + 8, nb:] = rb
-            if q + 8 < nb:
-                low = jnp.where(lane >= q + 8, ra, 0.0)
-                update = dot(low, jnp.concatenate([low, rb], 1), ((0,), (0,)), precision=HIGHEST)
-                diag[q + 8 :, :] = diag[q + 8 :, :] - update[q + 8 :, :]
+            diag[pl.ds(q, 8), nb:] = rb
+            low = jnp.where(lane >= q + 8, ra, 0.0)
+            update = dot(low, jnp.concatenate([low, rb], 1), ((0,), (0,)), precision=HIGHEST)
+            diag[...] = diag[...] - update
+            return carry
+
+        lax.fori_loop(0, nb // 8, slab, 0)
         upper = dot(diag[:, nb:], work[lo:hi, hi : n + hi], ((1,), (0,)), precision=HIGHEST)
         rest = n - hi
         out_ref[lo:hi, :hi] = upper[:, rest:]
@@ -101,9 +110,21 @@
             out_ref[lo:hi, hi:] = jnp.zeros((nb, rest), f32)
 
 
+def inverse_factor(pivot):
+    n = pivot.shape[0]
+    return pl.pallas_call(
+        invert_body,
+        out_shape=jax.ShapeDtypeStruct((n, n), f32),
+        scratch_shapes=[pltpu.VMEM((n, 2 * n), f32), pltpu.VMEM((128, 256), f32)],
+        compiler_params=pltpu.CompilerParams(vmem_limit_bytes=16 << 20),
+        cost_estimate=pl.CostEstimate(flops=30 * 10**9, bytes_accessed=2 << 20, transcendentals=0),
+        name="inverse_factor",
+    )(pivot)
+
+
 def gram_body(
-    count, at_ref, all_ref, near_ref, far_ref, schur_ref, factor_ref, red_ref,
-    own, panel, pivot, mom, inv_ref, work, diag
+    count, at_ref, all_ref, near_ref, far0, far1, far2, far3, inv_ref, mom,
+    schur_ref, factor_ref, red_ref, own, panel, mine_ref,
 ):
     step = pl.program_id(0)
     imps = near_ref.shape[1]
@@ -118,23 +139,29 @@
     def _():
         own[...] = jnp.zeros_like(own)
         panel[...] = jnp.zeros_like(panel)
-        pivot[...] = jnp.zeros_like(pivot)
-        mom[...] = jnp.zeros_like(mom)
-
-    mine = jnp.where(step % 2 == at_ref[3], near_ref[0], far_ref[0])
+
+    near_step = step % 2 == at_ref[3]
+
+    @pl.when(near_step)
+    def _():
+        mine_ref[...] = near_ref[0].T
+
+    for k, ref in enumerate((far0, far1, far2, far3)):
+
+        @pl.when(jnp.logical_not(near_step) & (((step // 2 - at_ref[6]) & 3) == k))
+        def _():
+            mine_ref[...] = ref[...].T
+
     block = [
         all_ref[:, 0, b * piece : (b + 1) * piece, :].reshape(imps, width) for b in range(blocks)
     ]
-    mine_t = mine.T
-    elim = jnp.concatenate(block[row_blocks:], axis=1)
-    elim_t = elim.T
+    mine_t = mine_ref[...]
+    elim_t = jnp.concatenate(block[row_blocks:], axis=1).T
     for b in range(blocks):
         at = slice(b * width, (b + 1) * width)
         own[:, at] += dot(mine_t, block[b], ((1,), (0,)))
         if b < row_blocks:
             panel[:, at] += dot(elim_t, block[b], ((1,), (0,)))
-    pivot[...] += dot(elim_t, elim, ((1,), (0,)))
-    mom[...] += jnp.sum(all_ref[:, 0, blocks * piece :, :].astype(f32), axis=1)
 
     @pl.when(step == pl.num_programs(0) - 1)
     def _():
@@ -146,7 +173,6 @@
             c = c0 + lax.broadcasted_iota(jnp.int32, shape, 1)
             return jnp.where(r == c, ridge, 0.0)
 
-        invert(pivot[...] * scale + diagonal((PANEL, PANEL), 0, 0), inv_ref, work, diag)
         inv = split(inv_ref[...])
         cross = own[:, rows:] * scale + diagonal((width, PANEL), col0, first)
         cross = dot3(split(cross), inv, NT)
@@ -160,19 +186,20 @@
             schur_ref[at, :] = gram - dot3(split(factor), cross_parts, NT)
         own_dev = at_ref[4]
         first_dev = at_ref[5]
-        picked = [mom[pl.ds(first_dev + k, 1), :] * scale for k in range(PANEL // width)]
+        picked = [mom[pl.ds(first_dev + k, 1), :] for k in range(PANEL // width)]
         elim = jnp.broadcast_to(jnp.concatenate(picked, axis=1), (8, PANEL))
         solved = dot(elim, inv_ref[...], NT, precision=HIGHEST)
         part = dot(solved, cross, NT, precision=HIGHEST)
-        reduced = mom[pl.ds(own_dev, 1), :] * scale - part[:1]
+        reduced = mom[pl.ds(own_dev, 1), :] - part[:1]
         red_ref[...] = reduced * (count**0.5)
 
 
-def gram_schur(count, at, gathered, near, far):
+def gram_schur(count, at, gathered, near, far, inv, moments):
     feat, samp, held, width = gathered.shape
     imps = near.shape[1]
     rows = width * feat // samp
     fixed = lambda i, at_ref: (0, 0)
+    whole = list(far) + [inv, moments]
     return pl.pallas_call(
         lambda *refs: gram_body(count, *refs),
         out_shape=(
@@ -186,8 +213,8 @@
             in_specs=[
                 pl.BlockSpec((feat, 1, held, width), lambda i, at_ref: (0, i, 0, 0)),
                 pl.BlockSpec((1, imps, width), lambda i, at_ref: (i // 2, 0, 0)),
-                pl.BlockSpec((1, imps, width), lambda i, at_ref: (i // 2, 0, 0)),
-            ],
+            ]
+            + [pl.BlockSpec(a.shape, fixed) for a in whole],
             out_specs=[
                 pl.BlockSpec((rows, width), fixed),
                 pl.BlockSpec((rows, PANEL), fixed),
@@ -196,16 +223,13 @@
             scratch_shapes=[
                 pltpu.VMEM((width, rows + PANEL), f32),
                 pltpu.VMEM((PANEL, rows), f32),
-                pltpu.VMEM((PANEL, PANEL), f32),
-                pltpu.VMEM((feat, width), f32),
-                pltpu.VMEM((PANEL, PANEL), f32),
-                pltpu.VMEM((PANEL, 2 * PANEL), f32),
-                pltpu.VMEM((128, 256), f32),
+                pltpu.VMEM((width, imps), bf16),
             ],
         ),
         compiler_params=pltpu.CompilerParams(vmem_limit_bytes=50 << 20),
+        cost_estimate=pl.CostEstimate(flops=20 * 10**9, bytes_accessed=30 << 20, transcendentals=0),
         name="gram_schur",
-    )(at, gathered, near, far)
+    )(at, gathered, near, *whole)
 
 
 def per_device(embeddings, frequencies, phases, treat_freq, treatment, flips, panel):
@@ -231,29 +255,54 @@
     feature = observed.astype(bf16)
 
     near = lax.all_gather(feature, "x")
-    swapped = lax.ppermute(feature, "zh", [(0, 1), (1, 0)])
 
     shares = lax.all_to_all(
         feature.reshape(feat, piece, width), FEAT, split_axis=0, concat_axis=0, tiled=True
     )
-    swapped, shares = lax.optimization_barrier((swapped, shares))
-    far = lax.all_gather(swapped, "x")
     first_dev = panel[0] * elim
-    picked = lax.dynamic_slice_in_dim(shares, first_dev, elim, 0)
-    high = lax.reduce_precision(moment_part, 8, 7)
-    middle = lax.reduce_precision(moment_part - high, 8, 7)
-    low = moment_part - high - middle
-    moment_rows = jnp.pad(jnp.stack([high, middle, low]), ((0, 13), (0, 0))).astype(bf16)
-    held = jnp.concatenate([picked.reshape(elim * piece, width), moment_rows], axis=0)
+    picked = lax.dynamic_slice_in_dim(shares, first_dev, elim, 0).reshape(1, elim * piece, width)
     send = jnp.concatenate(
         [
             shares.reshape(samp, feat // samp * piece, width),
-            jnp.broadcast_to(held[None], (samp,) + held.shape),
+            jnp.broadcast_to(picked, (samp, elim * piece, width)),
         ],
         axis=1,
     )
     share = lax.all_to_all(send, SAMP, split_axis=0, concat_axis=0, tiled=True)
+    share, near = lax.optimization_barrier((share, near))
     gathered = lax.all_gather(share, FEAT)
+
+    share, feature, moment_part = lax.optimization_barrier((share, feature, moment_part))
+    swapped = lax.ppermute(feature, "zh", [(0, 1), (1, 0)])
+    skip = feat // samp * piece
+    mine = jnp.concatenate(
+        [
+            share[:, skip + k * piece : skip + (k + 1) * piece, :].reshape(samp * piece, width)
+            for k in range(elim)
+        ],
+        axis=1,
+    )
+    part_rows = PANEL // samp
+    left = lax.dynamic_slice_in_dim(mine, samp_index * part_rows, part_rows, 1)
+    partial = dot(left, mine, ((0,), (0,))).reshape(feat, part_rows // feat * PANEL)
+    slabs = lax.all_to_all(partial, FEAT, split_axis=0, concat_axis=0, tiled=True)
+    held = jnp.concatenate([jnp.sum(slabs, axis=0), moment_part])[None]
+    held = lax.all_gather(held, ("zl", "core"), axis=0, tiled=True)
+    held = lax.all_gather(held, "y", axis=0, tiled=True)
+    other = lax.ppermute(held, "zh", [(0, 1), (1, 0)])
+    lower = lax.axis_index("zh") == 0
+    pair = jnp.stack([jnp.where(lower, held, other), jnp.where(lower, other, held)])
+    xs = lax.axis_size("x")
+    table = lax.all_to_all(
+        jnp.broadcast_to(pair[None], (xs,) + pair.shape), "x", split_axis=0, concat_axis=0, tiled=True
+    )
+    far = [swapped] + [
+        lax.ppermute(swapped, "x", [(i, (i - r) % xs) for i in range(xs)]) for r in range(1, xs)
+    ]
+    cut = part_rows // feat * PANEL
+    pivot = table[..., :cut].reshape(PANEL, PANEL) / count
+    moments = jnp.sum(table[..., cut:].reshape(samp, feat, width), axis=0) / count
+    inv = inverse_factor(pivot + ridge * jnp.eye(PANEL, dtype=f32))
 
     at = jnp.stack(
         [
@@ -263,9 +312,10 @@
             lax.axis_index("zh"),
             feat_index,
             first_dev,
+            lax.axis_index("x"),
         ]
     ).astype(jnp.int32)
-    schur, factor, reduced = gram_schur(count, at, gathered, near, far)
+    schur, factor, reduced = gram_schur(count, at, gathered, near, far, inv, moments)
     return (schur, factor, reduced[0])
 
 

time: 331 us -> 278 us (0.84)
  waiting for transfers between devices: 194 us -> 93.5 us
  blocking collectives: 31.9 us -> 69 us
  Pallas kernels: 68.7 us -> 62.8 us
  local copies, waits for them, and re-layouts: 1.73 us -> 6.98 us
  starting transfers between devices: 14.6 us -> 19.5 us
  other arithmetic: 1.62 us -> 6.5 us
    all_gather x1, waiting for transfers between devices: 152 us -> 24 us  [per_device(): gathered = lax.all_gather(share, FEAT)]
    pallas_call x1, Pallas kernels: 68.7 us -> 29.3 us  [gram_schur(): pl.pallas_call(lambda *refs: gram_body(count, *refs), out_shape=(jax.Shap...]
    pallas_call x0 -> x1, Pallas kernels: none -> 33.6 us  [inverse_factor(): pl.pallas_call(invert_body, out_shape=jax.ShapeDtypeStruct((n, n), f32),...]
    all_gather x0 -> x2, blocking collectives: none -> 22 us  [the longest x1 12.8 us: per_device(): held = lax.all_gather(held, ('zl', 'core'), axis=0, tiled=True)]
    all_to_all x0 -> x1, blocking collectives: none -> 17.3 us  [per_device(): lax.all_to_all(partial, FEAT, split_axis=0, concat_axis=0, tiled=True)]
    ppermute x0 -> x4, waiting for transfers between devices: none -> 15.3 us  [the longest x1 15.3 us: per_device(): other = lax.ppermute(held, 'zh', [(0, 1), (1, 0)])]
    all_to_all x1, waiting for transfers between devices: 3.12 us -> 16.1 us  [per_device(): lax.all_to_all(feature.reshape(feat, piece, width), FEAT, split_axis=0, c...]
    ppermute x1, waiting for transfers between devices: 31.8 us -> 38.1 us  [per_device(): swapped = lax.ppermute(feature, 'zh', [(0, 1), (1, 0)])]
  transfers between devices with their start and end apart: 5 -> 9, of which waited for: 4 -> 4; matrix products, arithmetic and copies ran while one was open for 0% -> 4% of each run, Pallas kernels for 0% -> 12%
where the time goes in v6:
time: 278 us; the launch traced here: 277 us
  waiting for transfers between devices  93.5 us (34%)
  blocking collectives  69 us (25%)
  Pallas kernels  62.8 us (23%)
  starting transfers between devices  19.5 us (7%)
  between operations  14.9 us (5%)
  local copies, waits for them, and re-layouts  6.98 us (3%)
  other arithmetic  6.5 us (2%)
  matrix products  4.14 us (1%)
    ppermute x1, waiting for transfers between devices, per_device(): swapped = lax.ppermute(feature, 'zh', [(0, 1), (1, 0)])  38.1 us
    pallas_call x1, Pallas kernels, inverse_factor(): pl.pallas_call(invert_body, out_shape=jax.ShapeDtypeStruct((n, n), f32),...  33.6 us
    all_to_all x1, blocking collectives, per_device(): share = lax.all_to_all(send, SAMP, split_axis=0, concat_axis=0, tiled=True)  29.6 us
    pallas_call x1, Pallas kernels, gram_schur(): pl.pallas_call(lambda *refs: gram_body(count, *refs), out_shape=(jax.Shap...  29.3 us
    all_gather x1, waiting for transfers between devices, per_device(): gathered = lax.all_gather(share, FEAT)  24 us
    all_to_all x1, blocking collectives, per_device(): lax.all_to_all(partial, FEAT, split_axis=0, concat_axis=0, tiled=True)  17.3 us
    all_to_all x1, waiting for transfers between devices, per_device(): lax.all_to_all(feature.reshape(feat, piece, width), FEAT, split_axis=0, c...  16.1 us
    ppermute x1, waiting for transfers between devices, per_device(): other = lax.ppermute(held, 'zh', [(0, 1), (1, 0)])  15.3 us
  transfers between devices with their start and end apart: 9, of which 4 were waited for; matrix products, arithmetic and copies ran while one was open for 4% of the time, Pallas kernels for 12%

profile of v6, /device:TPU:1, one launch (start us, length us, event | category | flops | bytes accessed | tf_op | source)
XLA Modules:
  0.0 277.3 jit_solution(13452804986152156898)
XLA Ops:
  7.2 0.8 convert_element_type.10
  8.1 0.7 multiply_subtract_fusion
  8.8 3.9 %subtract_reduce_fusion = (f32[256]{0:T(256)S(1)}, bf16[1024,256]{1,0:T(8,128)(2,1)}) fusion(f32[1024]{0:T(1024)S(1)} %multiply_subtract_fusion, f32[256]{0:T(256)} %param.10, f32[1024]{0:T(1024)S(1)} %convert_element_type.10, f32[256]{0:T(256)} %param.9, bf16[1024,1024]{1,0:T(8,128)(2,1)S(1)} %copy-done, bf16[1024,256]{1,0:T(8,128)(2,1)} %param.8), kind=kOutput, calls=%fused_computation.10 | convolution fusion | flops 547880704 | bytes 3156992 | tf_op jit(solution)/shard_map/dot_general | solution.py:247
  12.7 10.2 %all-to-all-start = ((bf16[32,32,256]{2,1,0:T(8,128)(2,1)}), bf16[32,32,256]{2,1,0:T(8,128)(2,1)S(1)}, u32[]{:S(2)}, u32[]{:S(2)}) async-start(bf16[32,32,256]{2,1,0:T(8,128)(2,1)} %bitcast.26), calls=%async_computation | async-start | bytes 1048576 | tf_op jit(solution)/shard_map/all_to_all | solution.py:259
  23.6 16.1 %all-to-all-done = bf16[32,32,256]{2,1,0:T(8,128)(2,1)S(1)} async-done(((bf16[32,32,256]{2,1,0:T(8,128)(2,1)}), bf16[32,32,256]{2,1,0:T(8,128)(2,1)S(1)}, u32[]{:S(2)}, u32[]{:S(2)}) %all-to-all-start) | async-done | bytes 524320 | tf_op jit(solution)/shard_map/all_to_all | solution.py:259
  39.7 0.1 pad_maximum_fusion
  39.8 29.6 %all_to_all.25 = bf16[8,192,256]{2,1,0:T(8,128)(2,1)} all-to-all(bf16[8,192,256]{2,1,0:T(8,128)(2,1)S(1)} %pad_maximum_fusion), channel_id=1, replica_groups=mesh['x'=4,'zh'=2,'y'=4,'zl'=4,'core'=2] {'x','zh'}, dimensions={0} | all-to-all | bytes 1572864 | tf_op jit(solution)/shard_map/all_to_all | solution.py:271
  69.4 1.0 fusion.16
  70.4 0.3 fusion.10
  70.7 0.1 all_to_all.20
  70.9 17.3 %all_to_all.26 = f32[32,1,1024]{2,1,0:T(1,128)S(1)} all-to-all(f32[32,1,1024]{2,1,0:T(1,128)S(1)} %all_to_all.20), channel_id=1, replica_groups=mesh['x'=4,'zh'=2,'y'=4,'zl'=4,'core'=2] {'y','zl','core'}, dimensions={0} | all-to-all | bytes 262144 | tf_op jit(solution)/shard_map/all_to_all | solution.py:288
  88.2 0.1 reduce_sum.28
  88.3 12.8 %all-gather.3 = f32[8,1,1280]{2,1,0:T(1,128)S(1)} all-gather(f32[1,1,1280]{2,1,0:T(1,128)S(1)} %reshape.46), channel_id=4, replica_groups=mesh['x'=4,'zh'=2,'y'=4,'zl'=4,'core'=2] {'zl','core'}, dimensions={0}, use_global_device_ids=true | all-gather | bytes 46080 | tf_op jit(solution)/shard_map/all_gather | solution.py:290
  101.1 9.2 %all_gather.23 = f32[32,1280]{1,0:T(8,128)S(1)} all-gather(f32[8,1280]{1,0:T(8,128)S(1)} %bitcast.29), channel_id=1, replica_groups=mesh['x'=4,'zh'=2,'y'=4,'zl'=4,'core'=2] {'y'}, dimensions={0}, use_global_device_ids=true | all-gather | bytes 204800 | tf_op jit(solution)/shard_map/all_gather | solution.py:291
  110.4 15.3 %collective-permute-done.4 = f32[32,1280]{1,0:T(8,128)S(1)} collective-permute-done((f32[32,1280]{1,0:T(8,128)S(1)}, f32[32,1280]{1,0:T(8,128)S(1)}, u32[]{:S(2)}, u32[]{:S(2)}) %collective-permute-start.4) | collective-permute-done | bytes 163872 | tf_op jit(solution)/shard_map/ppermute | solution.py:292
  125.8 1.2 broadcast_in_dim.11
  126.9 4.3 %all-to-all-start.3 = ((f32[4,2,32,1280]{3,2,1,0:T(8,128)}), f32[4,2,32,1280]{3,2,1,0:T(8,128)}, u32[]{:S(2)}, u32[]{:S(2)}) async-start(f32[4,2,32,1280]{3,2,1,0:T(8,128)} %broadcast_in_dim.11), calls=%async_computation.3 | async-start | bytes 2621440 | tf_op jit(solution)/shard_map/all_to_all | solution.py:296
  131.3 0.1 collective-permute-start
  131.4 0.1 stack.34.refs_0_
  131.5 38.1 %collective-permute-done.refs_3_ = bf16[1024,256]{1,0:T(8,128)(2,1)S(1)} collective-permute-done((bf16[1024,256]{1,0:T(8,128)(2,1)S(1)}, bf16[1024,256]{1,0:T(8,128)(2,1)S(1)}, u32[]{:S(2)}, u32[]{:S(2)}) %collective-permute-start) | collective-permute-done | bytes 524320 | tf_op jit(solution)/shard_map/ppermute | solution.py:276
  169.6 1.2 collective-permute-start.3
  170.7 2.4 collective-permute-start.2
  173.1 1.2 collective-permute-start.1
  174.3 2.3 slice_multiply_fusion
  176.6 2.4 div.16
  179.0 1.4 select_add_fusion.a_ref
  180.4 33.6 %inverse_factor.1.refs_7_ = f32[512,512]{1,0:T(8,128)S(1)} custom-call(f32[512,512]{1,0:T(8,128)S(1)} %select_add_fusion.a_ref), custom_call_target="tpu_custom_call" | custom-call | flops 30000001024 | bytes 2097152 | tf_op jit(solution)/shard_map/inverse_factor/pallas_call | solution.py:115
  214.0 1.0 copy-done.1
  214.9 1.0 slice_reduce_fusion
  216.0 24.0 %all-gather.9.cloned.1.call-done = bf16[256,192,256]{2,1,0:T(8,128)(2,1)} async-done(((bf16[8,192,256]{2,1,0:T(8,128)(2,1)}), bf16[256,192,256]{2,1,0:T(8,128)(2,1)}) %all-gather.9.cloned.1.call-update) | async-done | bytes 25165840 | tf_op jit(solution)/shard_map/all_gather | solution.py:273
  240.0 1.2 copy-done.2
  241.2 29.3 %gram_schur.1 = (f32[1024,256]{1,0:T(8,128)}, f32[1024,512]{1,0:T(8,128)}, f32[1,256]{1,0:T(1,128)}) custom-call(s32[7]{0:T(128)S(1)} %stack.34.refs_0_, bf16[32,8,192,256]{3,2,1,0:T(8,128)(2,1)} %bitcast.31, bf16[4,1024,256]{2,1,0:T(8,128)(2,1)} %bitcast.32, bf16[1024,256]{1,0:T(8,128)(2,1)S(1)} %collective-permute-done.refs_3_, ...), custom_call_target="tpu_custom_call" | custom-call | flops 20000000000 | bytes 31457280 | tf_op jit(solution)/shard_map/gram_schur/pallas_call | solution.py:203
  (24 shorter events, 0.3 us)
Async XLA Ops:
  7.2 1.6 copy-start
  7.2 62.2 %all-gather.7.cloned.1.call-start = ((), (), s32[]{:S(2)}) async-start(), calls=%async_computation.4 | async-start | bytes 2621440 | tf_op jit(solution)/shard_map/all_gather | solution.py:257
  12.7 27.0 %all-to-all-start = ((bf16[32,32,256]{2,1,0:T(8,128)(2,1)}), bf16[32,32,256]{2,1,0:T(8,128)(2,1)S(1)}, u32[]{:S(2)}, u32[]{:S(2)}) async-start(bf16[32,32,256]{2,1,0:T(8,128)(2,1)} %bitcast.26), calls=%async_computation | async-start | bytes 1048576 | tf_op jit(solution)/shard_map/all_to_all | solution.py:259
  22.9 217.1 %all-gather.9.cloned.1.call-start = ((), (), s32[]{:S(2)}) async-start(), calls=%async_computation.5 | async-start | bytes 25952256 | tf_op jit(solution)/shard_map/all_gather | solution.py:273
  110.4 15.3 %collective-permute-start.4 = (f32[32,1280]{1,0:T(8,128)S(1)}, f32[32,1280]{1,0:T(8,128)S(1)}, u32[]{:S(2)}, u32[]{:S(2)}) collective-permute-start(f32[32,1280]{1,0:T(8,128)S(1)} %all_gather.23), channel_id=1, source_target_pairs={{0,32},{32,0},{1,33},{33,1},{2,34},{34,2},{3,35},{35,3},{4,36},{36... | collective-permute-start | bytes 491528 | tf_op jit(solution)/shard_map/ppermute | solution.py:292
  125.8 5.5 %copy-start.3 = (bf16[1024,256]{1,0:T(8,128)(2,1)S(1)}, bf16[1024,256]{1,0:T(8,128)(2,1)}, u32[]{:S(2)}) copy-start(bf16[1024,256]{1,0:T(8,128)(2,1)} %get-tuple-element.13) | copy-start | bytes 1572868
  126.9 47.4 %all-to-all-start.3 = ((f32[4,2,32,1280]{3,2,1,0:T(8,128)}), f32[4,2,32,1280]{3,2,1,0:T(8,128)}, u32[]{:S(2)}, u32[]{:S(2)}) async-start(f32[4,2,32,1280]{3,2,1,0:T(8,128)} %broadcast_in_dim.11), calls=%async_computation.3 | async-start | bytes 2621440 | tf_op jit(solution)/shard_map/all_to_all | solution.py:296
  131.3 38.3 %collective-permute-start = (bf16[1024,256]{1,0:T(8,128)(2,1)S(1)}, bf16[1024,256]{1,0:T(8,128)(2,1)S(1)}, u32[]{:S(2)}, u32[]{:S(2)}) collective-permute-start(bf16[1024,256]{1,0:T(8,128)(2,1)S(1)} %copy-done.3), channel_id=1, source_target_pairs={{0,32},{32,0},{1,33},{33,1},{2,34},{34,2},{3,35},{35,3},{4,36},{36... | collective-permute-start | bytes 1572872 | tf_op jit(solution)/shard_map/ppermute | solution.py:276
  169.6 46.4 %collective-permute-start.3 = (bf16[1024,256]{1,0:T(8,128)(2,1)S(1)}, bf16[1024,256]{1,0:T(8,128)(2,1)S(1)}, u32[]{:S(2)}, u32[]{:S(2)}) collective-permute-start(bf16[1024,256]{1,0:T(8,128)(2,1)S(1)} %collective-permute-done.refs_3_), channel_id=1, source_target_pairs={{0,64},{64,128},{128,192},{192,0},{1,65},{65,129},{129,193},{193,1... | collective-permute-start | bytes 1572872 | tf_op jit(solution)/shard_map/ppermute | solution.py:300
  170.7 45.2 %collective-permute-start.2 = (bf16[1024,256]{1,0:T(8,128)(2,1)S(1)}, bf16[1024,256]{1,0:T(8,128)(2,1)}, u32[]{:S(2)}, u32[]{:S(2)}) collective-permute-start(bf16[1024,256]{1,0:T(8,128)(2,1)S(1)} %collective-permute-done.refs_3_), channel_id=1, source_target_pairs={{0,128},{64,192},{128,0},{192,64},{1,129},{65,193},{129,1},{193,65... | collective-permute-start | bytes 1572872 | tf_op jit(solution)/shard_map/ppermute | solution.py:300
  173.1 42.9 %collective-permute-start.1 = (bf16[1024,256]{1,0:T(8,128)(2,1)S(1)}, bf16[1024,256]{1,0:T(8,128)(2,1)}, u32[]{:S(2)}, u32[]{:S(2)}) collective-permute-start(bf16[1024,256]{1,0:T(8,128)(2,1)S(1)} %collective-permute-done.refs_3_), channel_id=1, source_target_pairs={{0,192},{64,0},{128,64},{192,128},{1,193},{65,1},{129,65},{193,129... | collective-permute-start | bytes 1572872 | tf_op jit(solution)/shard_map/ppermute | solution.py:300
  214.0 1.0 copy-start.1
  240.0 1.2 copy-start.2
Sparse Core Ops, SparseCore 0:
  12.8 37.1 all-gather.6
  69.5 170.3 all-gather.8

commit v7 on v6

--- a/solution.py
+++ b/solution.py
@@ -14,6 +14,7 @@
 
 SAMP = ("x", "zh")
 FEAT = ("y", "zl", "core")
+ZED = ("zh", "zl")
 
 SINE = (
     -8.885765875337938,
@@ -273,7 +274,12 @@
     gathered = lax.all_gather(share, FEAT)
 
     share, feature, moment_part = lax.optimization_barrier((share, feature, moment_part))
-    swapped = lax.ppermute(feature, "zh", [(0, 1), (1, 0)])
+    half = imps // 2
+    zs = lax.axis_size(ZED)
+    upward = [(i, (i + zs // 4) % zs) for i in range(zs)]
+    downward = [(i, (i - zs // 4) % zs) for i in range(zs)]
+    first = lax.ppermute(feature[:half], ZED, upward)
+    second = lax.ppermute(feature[half:], ZED, downward)
     skip = feat // samp * piece
     mine = jnp.concatenate(
         [
@@ -287,18 +293,23 @@
     partial = dot(left, mine, ((0,), (0,))).reshape(feat, part_rows // feat * PANEL)
     slabs = lax.all_to_all(partial, FEAT, split_axis=0, concat_axis=0, tiled=True)
     held = jnp.concatenate([jnp.sum(slabs, axis=0), moment_part])[None]
+    held, first, second = lax.optimization_barrier((held, first, second))
+    first = lax.ppermute(first, ZED, upward)
+    second = lax.ppermute(second, ZED, downward)
     held = lax.all_gather(held, ("zl", "core"), axis=0, tiled=True)
     held = lax.all_gather(held, "y", axis=0, tiled=True)
+    held, first, second = lax.optimization_barrier((held, first, second))
+    swapped = jnp.concatenate([first, second], axis=0)
+    xs = lax.axis_size("x")
+    far = [swapped] + [
+        lax.ppermute(swapped, "x", [(i, (i - r) % xs) for i in range(xs)]) for r in range(1, xs)
+    ]
     other = lax.ppermute(held, "zh", [(0, 1), (1, 0)])
     lower = lax.axis_index("zh") == 0
     pair = jnp.stack([jnp.where(lower, held, other), jnp.where(lower, other, held)])
-    xs = lax.axis_size("x")
     table = lax.all_to_all(
         jnp.broadcast_to(pair[None], (xs,) + pair.shape), "x", split_axis=0, concat_axis=0, tiled=True
     )
-    far = [swapped] + [
-        lax.ppermute(swapped, "x", [(i, (i - r) % xs) for i in range(xs)]) for r in range(1, xs)
-    ]
     cut = part_rows // feat * PANEL
     pivot = table[..., :cut].reshape(PANEL, PANEL) / count
     moments = jnp.sum(table[..., cut:].reshape(samp, feat, width), axis=0) / count

time: 278 us -> 278 us (level)
  starting transfers between devices: 19.5 us -> 35.2 us
  waiting for transfers between devices: 93.5 us -> 78.1 us
    ppermute x1 -> x4, waiting for transfers between devices: 38.1 us -> 6.12 us  [the longest x1 6.12 us: per_device(): second = lax.ppermute(feature[half:], ZED, downward)]
    all_to_all x1 -> x0, blocking collectives: 17.3 us -> none  [per_device(): lax.all_to_all(partial, FEAT, split_axis=0, concat_axis=0, tiled=True)]
    all_gather x1, blocking collectives: 12.8 us -> 29.3 us  [per_device(): held = lax.all_gather(held, ('zl', 'core'), axis=0, tiled=True)]
    all_to_all x0 -> x1, waiting for transfers between devices: none -> 14.2 us  [per_device(): lax.all_to_all(partial, FEAT, split_axis=0, concat_axis=0, tiled=True)]
    all_to_all x1, waiting for transfers between devices: 0.01 us -> 8.71 us  [per_device(): lax.all_to_all(jnp.broadcast_to(pair[None], (xs,) + pair.shape), 'x', spl...]
    all_to_all x0 -> x1, starting transfers between devices: none -> 6.95 us  [per_device(): lax.all_to_all(partial, FEAT, split_axis=0, concat_axis=0, tiled=True)]
    ppermute x1 -> x4, starting transfers between devices: 0.09 us -> 6.03 us  [the longest x1 2.11 us: per_device(): second = lax.ppermute(second, ZED, downward)]
    all_gather x1, waiting for transfers between devices: 24 us -> 19.9 us  [per_device(): gathered = lax.all_gather(share, FEAT)]
  transfers between devices with their start and end apart: 9 -> 13, of which waited for: 4 -> 6; matrix products, arithmetic and copies ran while one was open for 4% -> 4% of each run, Pallas kernels for 12% -> 12%
where the time goes in v7:
time: 278 us; the launch traced here: 277 us
  waiting for transfers between devices  78.1 us (28%)
  blocking collectives  68.2 us (25%)
  Pallas kernels  62.9 us (23%)
  starting transfers between devices  35.2 us (13%)
  between operations  14.9 us (5%)
  local copies, waits for them, and re-layouts  7.72 us (3%)
  other arithmetic  6.42 us (2%)
  matrix products  4.14 us (1%)
    pallas_call x1, Pallas kernels, inverse_factor(): pl.pallas_call(invert_body, out_shape=jax.ShapeDtypeStruct((n, n), f32),...  33.6 us
    all_to_all x1, blocking collectives, per_device(): share = lax.all_to_all(send, SAMP, split_axis=0, concat_axis=0, tiled=True)  29.8 us
    all_gather x1, blocking collectives, per_device(): held = lax.all_gather(held, ('zl', 'core'), axis=0, tiled=True)  29.3 us
    pallas_call x1, Pallas kernels, gram_schur(): pl.pallas_call(lambda *refs: gram_body(count, *refs), out_shape=(jax.Shap...  29.3 us
    all_gather x1, waiting for transfers between devices, per_device(): gathered = lax.all_gather(share, FEAT)  19.9 us
    all_to_all x1, waiting for transfers between devices, per_device(): lax.all_to_all(feature.reshape(feat, piece, width), FEAT, split_axis=0, c...  16.1 us
    all_to_all x1, waiting for transfers between devices, per_device(): lax.all_to_all(partial, FEAT, split_axis=0, concat_axis=0, tiled=True)  14.2 us
    ppermute x1, waiting for transfers between devices, per_device(): other = lax.ppermute(held, 'zh', [(0, 1), (1, 0)])  13 us
  transfers between devices with their start and end apart: 13, of which 6 were waited for; matrix products, arithmetic and copies ran while one was open for 4% of the time, Pallas kernels for 12%

profile of v7, /device:TPU:1, one launch (start us, length us, event | category | flops | bytes accessed | tf_op | source)
XLA Modules:
  0.0 277.5 jit_solution(18087171583355645582)
XLA Ops:
  7.2 0.8 convert_element_type.10
  8.8 3.9 %subtract_reduce_fusion = (f32[256]{0:T(256)S(1)}, bf16[1024,256]{1,0:T(8,128)(2,1)}) fusion(f32[1024]{0:T(1024)S(1)} %multiply_subtract_fusion, f32[256]{0:T(256)} %param.10, f32[1024]{0:T(1024)S(1)} %convert_element_type.10, f32[256]{0:T(256)} %param.9, bf16[1024,1024]{1,0:T(8,128)(2,1)S(1)} %copy-done, bf16[1024,256]{1,0:T(8,128)(2,1)} %param.8), kind=kOutput, calls=%fused_computation.10 | convolution fusion | flops 547880704 | bytes 3156992 | tf_op jit(solution)/shard_map/dot_general | solution.py:248
  12.7 10.2 %all-to-all-start = ((bf16[32,32,256]{2,1,0:T(8,128)(2,1)}), bf16[32,32,256]{2,1,0:T(8,128)(2,1)S(1)}, u32[]{:S(2)}, u32[]{:S(2)}) async-start(bf16[32,32,256]{2,1,0:T(8,128)(2,1)} %bitcast.26), calls=%async_computation | async-start | bytes 1048576 | tf_op jit(solution)/shard_map/all_to_all | solution.py:260
  23.6 16.1 %all-to-all-done = bf16[32,32,256]{2,1,0:T(8,128)(2,1)S(1)} async-done(((bf16[32,32,256]{2,1,0:T(8,128)(2,1)}), bf16[32,32,256]{2,1,0:T(8,128)(2,1)S(1)}, u32[]{:S(2)}, u32[]{:S(2)}) %all-to-all-start) | async-done | bytes 524320 | tf_op jit(solution)/shard_map/all_to_all | solution.py:260
  39.8 29.8 %all_to_all.25 = bf16[8,192,256]{2,1,0:T(8,128)(2,1)} all-to-all(bf16[8,192,256]{2,1,0:T(8,128)(2,1)S(1)} %pad_maximum_fusion), channel_id=1, replica_groups=mesh['x'=4,'zh'=2,'y'=4,'zl'=4,'core'=2] {'x','zh'}, dimensions={0} | all-to-all | bytes 1572864 | tf_op jit(solution)/shard_map/all_to_all | solution.py:272
  69.6 1.0 fusion.16
  71.7 6.9 %all-to-all-start.2 = ((f32[32,1,1024]{2,1,0:T(1,128)}), f32[32,1,1024]{2,1,0:T(1,128)S(1)}, u32[]{:S(2)}, u32[]{:S(2)}) async-start(f32[32,1,1024]{2,1,0:T(1,128)} %all_to_all.20), calls=%async_computation.2 | async-start | bytes 262144 | tf_op jit(solution)/shard_map/all_to_all | solution.py:294
  78.7 0.8 collective-permute-start.1
  79.5 1.6 collective-permute-start
  81.1 14.2 %all-to-all-done.2 = f32[32,1,1024]{2,1,0:T(1,128)S(1)} async-done(((f32[32,1,1024]{2,1,0:T(1,128)}), f32[32,1,1024]{2,1,0:T(1,128)S(1)}, u32[]{:S(2)}, u32[]{:S(2)}) %all-to-all-start.2) | async-done | bytes 131104 | tf_op jit(solution)/shard_map/all_to_all | solution.py:294
  95.5 6.1 %collective-permute-done.1 = bf16[512,256]{1,0:T(8,128)(2,1)S(1)} collective-permute-done((bf16[512,256]{1,0:T(8,128)(2,1)S(1)}, bf16[512,256]{1,0:T(8,128)(2,1)S(1)}, u32[]{:S(2)}, u32[]{:S(2)}) %collective-permute-start.1) | collective-permute-done | bytes 262176 | tf_op jit(solution)/shard_map/ppermute | solution.py:282
  101.6 1.5 collective-permute-start.2
  103.1 2.1 collective-permute-start.3
  105.2 29.3 %all-gather.2 = f32[8,1,1280]{2,1,0:T(1,128)S(1)} all-gather(f32[1,1,1280]{2,1,0:T(1,128)S(1)} %bitcast.32), channel_id=1, replica_groups=mesh['x'=4,'zh'=2,'y'=4,'zl'=4,'core'=2] {'zl','core'}, dimensions={0}, use_global_device_ids=true | all-gather | bytes 46080 | tf_op jit(solution)/shard_map/all_gather | solution.py:299
  134.5 9.2 %all_gather.23 = f32[32,1280]{1,0:T(8,128)S(1)} all-gather(f32[8,1280]{1,0:T(8,128)S(1)} %bitcast.30), channel_id=1, replica_groups=mesh['x'=4,'zh'=2,'y'=4,'zl'=4,'core'=2] {'y'}, dimensions={0}, use_global_device_ids=true | all-gather | bytes 204800 | tf_op jit(solution)/shard_map/all_gather | solution.py:300
  143.6 2.6 collective-permute-start.7
  146.2 13.0 %collective-permute-done.7 = f32[32,1280]{1,0:T(8,128)S(1)} collective-permute-done((f32[32,1280]{1,0:T(8,128)S(1)}, f32[32,1280]{1,0:T(8,128)S(1)}, u32[]{:S(2)}, u32[]{:S(2)}) %collective-permute-start.7) | collective-permute-done | bytes 163872 | tf_op jit(solution)/shard_map/ppermute | solution.py:307
  159.2 1.2 broadcast_in_dim.11
  160.4 4.3 %all-to-all-start.3 = ((f32[4,2,32,1280]{3,2,1,0:T(8,128)}), f32[4,2,32,1280]{3,2,1,0:T(8,128)}, u32[]{:S(2)}, u32[]{:S(2)}) async-start(f32[4,2,32,1280]{3,2,1,0:T(8,128)} %broadcast_in_dim.11), calls=%async_computation.3 | async-start | bytes 2621440 | tf_op jit(solution)/shard_map/all_to_all | solution.py:310
  164.8 1.5 collective-permute-start.6
  166.3 2.4 collective-permute-start.5
  168.7 1.2 collective-permute-start.4
  169.9 8.7 %all-to-all-done.3 = f32[4,2,32,1280]{3,2,1,0:T(8,128)} async-done(((f32[4,2,32,1280]{3,2,1,0:T(8,128)}), f32[4,2,32,1280]{3,2,1,0:T(8,128)}, u32[]{:S(2)}, u32[]{:S(2)}) %all-to-all-start.3) | async-done | bytes 1310752 | tf_op jit(solution)/shard_map/all_to_all | solution.py:310
  178.6 2.3 slice_multiply_fusion
  180.9 2.4 div.16
  183.3 1.4 select_add_fusion.a_ref
  184.7 33.6 %inverse_factor.1.refs_7_ = f32[512,512]{1,0:T(8,128)S(1)} custom-call(f32[512,512]{1,0:T(8,128)S(1)} %select_add_fusion.a_ref), custom_call_target="tpu_custom_call" | custom-call | flops 30000001024 | bytes 2097152 | tf_op jit(solution)/shard_map/inverse_factor/pallas_call | solution.py:116
  218.2 1.0 copy-done.1
  219.2 1.0 slice_reduce_fusion
  220.2 19.9 %all-gather.8.cloned.1.call-done = bf16[256,192,256]{2,1,0:T(8,128)(2,1)} async-done(((bf16[8,192,256]{2,1,0:T(8,128)(2,1)}), bf16[256,192,256]{2,1,0:T(8,128)(2,1)}) %all-gather.8.cloned.1.call-update) | async-done | bytes 25165840 | tf_op jit(solution)/shard_map/all_gather | solution.py:274
  240.1 1.2 copy-done.2
  241.4 29.3 %gram_schur.1 = (f32[1024,256]{1,0:T(8,128)}, f32[1024,512]{1,0:T(8,128)}, f32[1,256]{1,0:T(1,128)}) custom-call(s32[7]{0:T(128)S(1)} %stack.34.refs_0_, bf16[32,8,192,256]{3,2,1,0:T(8,128)(2,1)} %bitcast.33, bf16[4,1024,256]{2,1,0:T(8,128)(2,1)} %bitcast.34, bf16[1024,256]{1,0:T(8,128)(2,1)S(1)} %constant_dynamic-update-slice_fusion.refs_3_, ...), custom_call_target="tpu_custom_call" | custom-call | flops 20000000000 | bytes 31457280 | tf_op jit(solution)/shard_map/gram_schur/pallas_call | solution.py:204
  (34 shorter events, 2.4 us)
Async XLA Ops:
  7.2 1.6 copy-start
  7.2 62.4 %all-gather.6.cloned.1.call-start = ((), (), s32[]{:S(2)}) async-start(), calls=%async_computation.4 | async-start | bytes 2621440 | tf_op jit(solution)/shard_map/all_gather | solution.py:258
  12.7 27.0 %all-to-all-start = ((bf16[32,32,256]{2,1,0:T(8,128)(2,1)}), bf16[32,32,256]{2,1,0:T(8,128)(2,1)S(1)}, u32[]{:S(2)}, u32[]{:S(2)}) async-start(bf16[32,32,256]{2,1,0:T(8,128)(2,1)} %bitcast.26), calls=%async_computation | async-start | bytes 1048576 | tf_op jit(solution)/shard_map/all_to_all | solution.py:260
  22.9 217.3 %all-gather.8.cloned.1.call-start = ((), (), s32[]{:S(2)}) async-start(), calls=%async_computation.5 | async-start | bytes 25952256 | tf_op jit(solution)/shard_map/all_gather | solution.py:274
  39.8 38.9 %copy-start.3 = (bf16[1024,256]{1,0:T(8,128)(2,1)S(1)}, bf16[1024,256]{1,0:T(8,128)(2,1)}, u32[]{:S(2)}) copy-start(bf16[1024,256]{1,0:T(8,128)(2,1)} %get-tuple-element.21) | copy-start | bytes 1572868
  71.7 23.7 %all-to-all-start.2 = ((f32[32,1,1024]{2,1,0:T(1,128)}), f32[32,1,1024]{2,1,0:T(1,128)S(1)}, u32[]{:S(2)}, u32[]{:S(2)}) async-start(f32[32,1,1024]{2,1,0:T(1,128)} %all_to_all.20), calls=%async_computation.2 | async-start | bytes 262144 | tf_op jit(solution)/shard_map/all_to_all | solution.py:294
  78.7 22.9 %collective-permute-start.1 = (bf16[512,256]{1,0:T(8,128)(2,1)S(1)}, bf16[512,256]{1,0:T(8,128)(2,1)S(1)}, u32[]{:S(2)}, u32[]{:S(2)}) collective-permute-start(bf16[512,256]{1,0:T(8,128)(2,1)S(1)} %get-tuple-element.35), channel_id=1, source_target_pairs={{0,36},{2,38},{4,0},{6,2},{32,4},{34,6},{36,32},{38,34},{1,37},{3,... | collective-permute-start | bytes 786440 | tf_op jit(solution)/shard_map/ppermute | solution.py:282
  79.5 22.1 %collective-permute-start = (bf16[512,256]{1,0:T(8,128)(2,1)S(1)}, bf16[512,256]{1,0:T(8,128)(2,1)S(1)}, u32[]{:S(2)}, u32[]{:S(2)}) collective-permute-start(bf16[512,256]{1,0:T(8,128)(2,1)S(1)} %get-tuple-element.36), channel_id=1, source_target_pairs={{0,4},{2,6},{4,32},{6,34},{32,36},{34,38},{36,0},{38,2},{1,5},{3,7... | collective-permute-start | bytes 786440 | tf_op jit(solution)/shard_map/ppermute | solution.py:281
  101.6 42.0 %collective-permute-start.2 = (bf16[512,256]{1,0:T(8,128)(2,1)S(1)}, bf16[512,256]{1,0:T(8,128)(2,1)S(1)}, u32[]{:S(2)}, u32[]{:S(2)}) collective-permute-start(bf16[512,256]{1,0:T(8,128)(2,1)S(1)} %collective-permute-done), channel_id=1, source_target_pairs={{0,4},{2,6},{4,32},{6,34},{32,36},{34,38},{36,0},{38,2},{1,5},{3,7... | collective-permute-start | bytes 786440 | tf_op jit(solution)/shard_map/ppermute | solution.py:297
  103.1 40.6 %collective-permute-start.3 = (bf16[512,256]{1,0:T(8,128)(2,1)S(1)}, bf16[512,256]{1,0:T(8,128)(2,1)S(1)}, u32[]{:S(2)}, u32[]{:S(2)}) collective-permute-start(bf16[512,256]{1,0:T(8,128)(2,1)S(1)} %collective-permute-done.1), channel_id=1, source_target_pairs={{0,36},{2,38},{4,0},{6,2},{32,4},{34,6},{36,32},{38,34},{1,37},{3,... | collective-permute-start | bytes 786440 | tf_op jit(solution)/shard_map/ppermute | solution.py:298
  143.6 15.5 %collective-permute-start.7 = (f32[32,1280]{1,0:T(8,128)S(1)}, f32[32,1280]{1,0:T(8,128)S(1)}, u32[]{:S(2)}, u32[]{:S(2)}) collective-permute-start(f32[32,1280]{1,0:T(8,128)S(1)} %all_gather.23), channel_id=1, source_target_pairs={{0,32},{32,0},{1,33},{33,1},{2,34},{34,2},{3,35},{35,3},{4,36},{36... | collective-permute-start | bytes 491528 | tf_op jit(solution)/shard_map/ppermute | solution.py:307
  160.4 18.2 %all-to-all-start.3 = ((f32[4,2,32,1280]{3,2,1,0:T(8,128)}), f32[4,2,32,1280]{3,2,1,0:T(8,128)}, u32[]{:S(2)}, u32[]{:S(2)}) async-start(f32[4,2,32,1280]{3,2,1,0:T(8,128)} %broadcast_in_dim.11), calls=%async_computation.3 | async-start | bytes 2621440 | tf_op jit(solution)/shard_map/all_to_all | solution.py:310
  164.8 55.4 %collective-permute-start.6 = (bf16[1024,256]{1,0:T(8,128)(2,1)S(1)}, bf16[1024,256]{1,0:T(8,128)(2,1)S(1)}, u32[]{:S(2)}, u32[]{:S(2)}) collective-permute-start(bf16[1024,256]{1,0:T(8,128)(2,1)S(1)} %constant_dynamic-update-slice_fusion.refs_3_), channel_id=1, source_target_pairs={{0,64},{64,128},{128,192},{192,0},{1,65},{65,129},{129,193},{193,1... | collective-permute-start | bytes 1572872 | tf_op jit(solution)/shard_map/ppermute | solution.py:305
  166.3 53.9 %collective-permute-start.5 = (bf16[1024,256]{1,0:T(8,128)(2,1)S(1)}, bf16[1024,256]{1,0:T(8,128)(2,1)}, u32[]{:S(2)}, u32[]{:S(2)}) collective-permute-start(bf16[1024,256]{1,0:T(8,128)(2,1)S(1)} %constant_dynamic-update-slice_fusion.refs_3_), channel_id=1, source_target_pairs={{0,128},{64,192},{128,0},{192,64},{1,129},{65,193},{129,1},{193,65... | collective-permute-start | bytes 1572872 | tf_op jit(solution)/shard_map/ppermute | solution.py:305
  168.7 51.5 %collective-permute-start.4 = (bf16[1024,256]{1,0:T(8,128)(2,1)S(1)}, bf16[1024,256]{1,0:T(8,128)(2,1)}, u32[]{:S(2)}, u32[]{:S(2)}) collective-permute-start(bf16[1024,256]{1,0:T(8,128)(2,1)S(1)} %constant_dynamic-update-slice_fusion.refs_3_), channel_id=1, source_target_pairs={{0,192},{64,0},{128,64},{192,128},{1,193},{65,1},{129,65},{193,129... | collective-permute-start | bytes 1572872 | tf_op jit(solution)/shard_map/ppermute | solution.py:305
  218.2 1.0 copy-start.1
  240.1 1.2 copy-start.2
Sparse Core Ops, SparseCore 0:
  12.8 37.1 all-gather.5
  69.7 170.3 all-gather.7

commit v8 on v6

--- a/solution.py
+++ b/solution.py
@@ -37,17 +37,6 @@
 
 def dot(left, right, dims, **kw):
     return lax.dot_general(left, right, (dims, ((), ())), preferred_element_type=f32, **kw)
-
-
-def split(a):
-    high = a.astype(bf16)
-    return high, (a - high.astype(f32)).astype(bf16)
-
-
-def dot3(left, right, dims):
-    lh, ll = left
-    rh, rl = right
-    return dot(lh, rh, dims) + (dot(lh, rl, dims) + dot(ll, rh, dims))
 
 
 NN = ((1,), (0,))
@@ -140,28 +129,29 @@
         own[...] = jnp.zeros_like(own)
         panel[...] = jnp.zeros_like(panel)
 
-    near_step = step % 2 == at_ref[3]
-
-    @pl.when(near_step)
-    def _():
-        mine_ref[...] = near_ref[0].T
-
+    zh = at_ref[3]
+    mine_ref[zh] = near_ref[0].T
     for k, ref in enumerate((far0, far1, far2, far3)):
 
-        @pl.when(jnp.logical_not(near_step) & (((step // 2 - at_ref[6]) & 3) == k))
+        @pl.when(((step - at_ref[6]) & 3) == k)
         def _():
-            mine_ref[...] = ref[...].T
-
-    block = [
-        all_ref[:, 0, b * piece : (b + 1) * piece, :].reshape(imps, width) for b in range(blocks)
+            mine_ref[1 - zh] = ref[...].T
+
+    def block(half, b):
+        return all_ref[:, half, b * piece : (b + 1) * piece, :].reshape(imps, width)
+
+    elim = [
+        jnp.concatenate([block(half, b) for b in range(row_blocks, blocks)], axis=1)
+        for half in range(2)
     ]
-    mine_t = mine_ref[...]
-    elim_t = jnp.concatenate(block[row_blocks:], axis=1).T
-    for b in range(blocks):
+    left = [jnp.concatenate([mine_ref[half], elim[half].T], axis=0) for half in range(2)]
+    both = jnp.concatenate(left, axis=1)
+    for b in range(row_blocks):
         at = slice(b * width, (b + 1) * width)
-        own[:, at] += dot(mine_t, block[b], ((1,), (0,)))
-        if b < row_blocks:
-            panel[:, at] += dot(elim_t, block[b], ((1,), (0,)))
+        sums = dot(both, jnp.concatenate([block(0, b), block(1, b)], axis=0), NN)
+        own[:, at] += sums[:width]
+        panel[:, at] += sums[width:]
+    own[:, rows:] += dot(mine_ref[0], elim[0], NN) + dot(mine_ref[1], elim[1], NN)
 
     @pl.when(step == pl.num_programs(0) - 1)
     def _():
@@ -173,24 +163,35 @@
             c = c0 + lax.broadcasted_iota(jnp.int32, shape, 1)
             return jnp.where(r == c, ridge, 0.0)
 
-        inv = split(inv_ref[...])
+        inv = inv_ref[...].T
+        part = PANEL // 2
+
+        def solve(a):
+            return jnp.concatenate(
+                [
+                    dot(a[:, :part], inv[:part, :part], NN, precision=HIGHEST),
+                    dot(a, inv[:, part:], NN, precision=HIGHEST),
+                ],
+                axis=1,
+            )
+
         cross = own[:, rows:] * scale + diagonal((width, PANEL), col0, first)
-        cross = dot3(split(cross), inv, NT)
-        cross_parts = split(cross)
+        cross = solve(cross)
+        cross_t = cross.T
         for lo in range(0, rows, width):
             at = slice(lo, lo + width)
             cols = panel[:, at].T * scale + diagonal((width, PANEL), row0 + lo, first)
-            factor = dot3(split(cols), inv, NT)
+            factor = solve(cols)
             factor_ref[at, :] = factor
             gram = own[:, at].T * scale + diagonal((width, width), row0 + lo, col0)
-            schur_ref[at, :] = gram - dot3(split(factor), cross_parts, NT)
+            schur_ref[at, :] = gram - dot(factor, cross_t, NN, precision=HIGHEST)
         own_dev = at_ref[4]
         first_dev = at_ref[5]
         picked = [mom[pl.ds(first_dev + k, 1), :] for k in range(PANEL // width)]
         elim = jnp.broadcast_to(jnp.concatenate(picked, axis=1), (8, PANEL))
         solved = dot(elim, inv_ref[...], NT, precision=HIGHEST)
-        part = dot(solved, cross, NT, precision=HIGHEST)
-        reduced = mom[pl.ds(own_dev, 1), :] - part[:1]
+        taken = dot(solved, cross, NT, precision=HIGHEST)
+        reduced = mom[pl.ds(own_dev, 1), :] - taken[:1]
         red_ref[...] = reduced * (count**0.5)
 
 
@@ -209,10 +210,10 @@
         ),
         grid_spec=pltpu.PrefetchScalarGridSpec(
             num_scalar_prefetch=1,
-            grid=(samp,),
+            grid=(samp // 2,),
             in_specs=[
-                pl.BlockSpec((feat, 1, held, width), lambda i, at_ref: (0, i, 0, 0)),
-                pl.BlockSpec((1, imps, width), lambda i, at_ref: (i // 2, 0, 0)),
+                pl.BlockSpec((feat, 2, held, width), lambda i, at_ref: (0, i, 0, 0)),
+                pl.BlockSpec((1, imps, width), lambda i, at_ref: (i, 0, 0)),
             ]
             + [pl.BlockSpec(a.shape, fixed) for a in whole],
             out_specs=[
@@ -223,7 +224,7 @@
             scratch_shapes=[
                 pltpu.VMEM((width, rows + PANEL), f32),
                 pltpu.VMEM((PANEL, rows), f32),
-                pltpu.VMEM((width, imps), bf16),
+                pltpu.VMEM((2, width, imps), bf16),
             ],
         ),
         compiler_params=pltpu.CompilerParams(vmem_limit_bytes=50 << 20),

time: 278 us -> 280 us (level)
  no operation moved by 1% of the time
where the time goes in v8:
time: 280 us; the launch traced here: 279 us
  waiting for transfers between devices  93.5 us (33%)
  blocking collectives  69 us (25%)
  Pallas kernels  64.6 us (23%)
  starting transfers between devices  19.5 us (7%)
  between operations  14.9 us (5%)
  local copies, waits for them, and re-layouts  6.98 us (2%)
  other arithmetic  6.49 us (2%)
  matrix products  4.14 us (1%)
    ppermute x1, waiting for transfers between devices, per_device(): swapped = lax.ppermute(feature, 'zh', [(0, 1), (1, 0)])  38.1 us
    pallas_call x1, Pallas kernels, inverse_factor(): pl.pallas_call(invert_body, out_shape=jax.ShapeDtypeStruct((n, n), f32),...  33.6 us
    pallas_call x1, Pallas kernels, gram_schur(): pl.pallas_call(lambda *refs: gram_body(count, *refs), out_shape=(jax.Shap...  31 us
    all_to_all x1, blocking collectives, per_device(): share = lax.all_to_all(send, SAMP, split_axis=0, concat_axis=0, tiled=True)  29.6 us
    all_gather x1, waiting for transfers between devices, per_device(): gathered = lax.all_gather(share, FEAT)  24 us
    all_to_all x1, blocking collectives, per_device(): lax.all_to_all(partial, FEAT, split_axis=0, concat_axis=0, tiled=True)  17.3 us
    all_to_all x1, waiting for transfers between devices, per_device(): lax.all_to_all(feature.reshape(feat, piece, width), FEAT, split_axis=0, c...  16.1 us
    ppermute x1, waiting for transfers between devices, per_device(): other = lax.ppermute(held, 'zh', [(0, 1), (1, 0)])  15.3 us
  transfers between devices with their start and end apart: 9, of which 4 were waited for; matrix products, arithmetic and copies ran while one was open for 4% of the time, Pallas kernels for 12%

profile of v8, /device:TPU:1, one launch (start us, length us, event | category | flops | bytes accessed | tf_op | source)
XLA Modules:
  0.0 279.1 jit_solution(7762034451396816173)
XLA Ops:
  7.2 0.8 convert_element_type.10
  8.1 0.7 multiply_subtract_fusion
  8.8 3.9 %subtract_reduce_fusion = (f32[256]{0:T(256)S(1)}, bf16[1024,256]{1,0:T(8,128)(2,1)}) fusion(f32[1024]{0:T(1024)S(1)} %multiply_subtract_fusion, f32[256]{0:T(256)} %param.10, f32[1024]{0:T(1024)S(1)} %convert_element_type.10, f32[256]{0:T(256)} %param.9, bf16[1024,1024]{1,0:T(8,128)(2,1)S(1)} %copy-done, bf16[1024,256]{1,0:T(8,128)(2,1)} %param.8), kind=kOutput, calls=%fused_computation.10 | convolution fusion | flops 547880704 | bytes 3156992 | tf_op jit(solution)/shard_map/dot_general | solution.py:248
  12.7 10.2 %all-to-all-start = ((bf16[32,32,256]{2,1,0:T(8,128)(2,1)}), bf16[32,32,256]{2,1,0:T(8,128)(2,1)S(1)}, u32[]{:S(2)}, u32[]{:S(2)}) async-start(bf16[32,32,256]{2,1,0:T(8,128)(2,1)} %bitcast.26), calls=%async_computation | async-start | bytes 1048576 | tf_op jit(solution)/shard_map/all_to_all | solution.py:260
  23.6 16.1 %all-to-all-done = bf16[32,32,256]{2,1,0:T(8,128)(2,1)S(1)} async-done(((bf16[32,32,256]{2,1,0:T(8,128)(2,1)}), bf16[32,32,256]{2,1,0:T(8,128)(2,1)S(1)}, u32[]{:S(2)}, u32[]{:S(2)}) %all-to-all-start) | async-done | bytes 524320 | tf_op jit(solution)/shard_map/all_to_all | solution.py:260
  39.7 0.1 pad_maximum_fusion
  39.8 29.6 %all_to_all.25 = bf16[8,192,256]{2,1,0:T(8,128)(2,1)} all-to-all(bf16[8,192,256]{2,1,0:T(8,128)(2,1)S(1)} %pad_maximum_fusion), channel_id=1, replica_groups=mesh['x'=4,'zh'=2,'y'=4,'zl'=4,'core'=2] {'x','zh'}, dimensions={0} | all-to-all | bytes 1572864 | tf_op jit(solution)/shard_map/all_to_all | solution.py:272
  69.4 1.0 fusion.16
  70.4 0.3 fusion.10
  70.7 0.1 all_to_all.20
  70.9 17.3 %all_to_all.26 = f32[32,1,1024]{2,1,0:T(1,128)S(1)} all-to-all(f32[32,1,1024]{2,1,0:T(1,128)S(1)} %all_to_all.20), channel_id=1, replica_groups=mesh['x'=4,'zh'=2,'y'=4,'zl'=4,'core'=2] {'y','zl','core'}, dimensions={0} | all-to-all | bytes 262144 | tf_op jit(solution)/shard_map/all_to_all | solution.py:289
  88.2 0.1 reduce_sum.28
  88.3 12.8 %all-gather.3 = f32[8,1,1280]{2,1,0:T(1,128)S(1)} all-gather(f32[1,1,1280]{2,1,0:T(1,128)S(1)} %reshape.46), channel_id=4, replica_groups=mesh['x'=4,'zh'=2,'y'=4,'zl'=4,'core'=2] {'zl','core'}, dimensions={0}, use_global_device_ids=true | all-gather | bytes 46080 | tf_op jit(solution)/shard_map/all_gather | solution.py:291
  101.1 9.2 %all_gather.23 = f32[32,1280]{1,0:T(8,128)S(1)} all-gather(f32[8,1280]{1,0:T(8,128)S(1)} %bitcast.29), channel_id=1, replica_groups=mesh['x'=4,'zh'=2,'y'=4,'zl'=4,'core'=2] {'y'}, dimensions={0}, use_global_device_ids=true | all-gather | bytes 204800 | tf_op jit(solution)/shard_map/all_gather | solution.py:292
  110.4 15.3 %collective-permute-done.4 = f32[32,1280]{1,0:T(8,128)S(1)} collective-permute-done((f32[32,1280]{1,0:T(8,128)S(1)}, f32[32,1280]{1,0:T(8,128)S(1)}, u32[]{:S(2)}, u32[]{:S(2)}) %collective-permute-start.4) | collective-permute-done | bytes 163872 | tf_op jit(solution)/shard_map/ppermute | solution.py:293
  125.8 1.2 broadcast_in_dim.11
  126.9 4.3 %all-to-all-start.3 = ((f32[4,2,32,1280]{3,2,1,0:T(8,128)}), f32[4,2,32,1280]{3,2,1,0:T(8,128)}, u32[]{:S(2)}, u32[]{:S(2)}) async-start(f32[4,2,32,1280]{3,2,1,0:T(8,128)} %broadcast_in_dim.11), calls=%async_computation.3 | async-start | bytes 2621440 | tf_op jit(solution)/shard_map/all_to_all | solution.py:297
  131.3 0.1 collective-permute-start
  131.4 0.1 stack.34.refs_0_
  131.5 38.1 %collective-permute-done.refs_3_ = bf16[1024,256]{1,0:T(8,128)(2,1)S(1)} collective-permute-done((bf16[1024,256]{1,0:T(8,128)(2,1)S(1)}, bf16[1024,256]{1,0:T(8,128)(2,1)S(1)}, u32[]{:S(2)}, u32[]{:S(2)}) %collective-permute-start) | collective-permute-done | bytes 524320 | tf_op jit(solution)/shard_map/ppermute | solution.py:277
  169.6 1.2 collective-permute-start.3
  170.7 2.4 collective-permute-start.2
  173.1 1.2 collective-permute-start.1
  174.3 2.3 slice_multiply_fusion
  176.6 2.4 div.16
  179.0 1.4 select_add_fusion.a_ref
  180.4 33.6 %inverse_factor.1.refs_7_ = f32[512,512]{1,0:T(8,128)S(1)} custom-call(f32[512,512]{1,0:T(8,128)S(1)} %select_add_fusion.a_ref), custom_call_target="tpu_custom_call" | custom-call | flops 30000001024 | bytes 2097152 | tf_op jit(solution)/shard_map/inverse_factor/pallas_call | solution.py:104
  214.0 1.0 copy-done.1
  214.9 1.0 slice_reduce_fusion
  216.0 24.0 %all-gather.9.cloned.1.call-done = bf16[256,192,256]{2,1,0:T(8,128)(2,1)} async-done(((bf16[8,192,256]{2,1,0:T(8,128)(2,1)}), bf16[256,192,256]{2,1,0:T(8,128)(2,1)}) %all-gather.9.cloned.1.call-update) | async-done | bytes 25165840 | tf_op jit(solution)/shard_map/all_gather | solution.py:274
  240.0 1.2 copy-done.2
  241.2 31.0 %gram_schur.1 = (f32[1024,256]{1,0:T(8,128)}, f32[1024,512]{1,0:T(8,128)}, f32[1,256]{1,0:T(1,128)}) custom-call(s32[7]{0:T(128)S(1)} %stack.34.refs_0_, bf16[32,8,192,256]{3,2,1,0:T(8,128)(2,1)} %bitcast.31, bf16[4,1024,256]{2,1,0:T(8,128)(2,1)} %bitcast.32, bf16[1024,256]{1,0:T(8,128)(2,1)S(1)} %collective-permute-done.refs_3_, ...), custom_call_target="tpu_custom_call" | custom-call | flops 20000000000 | bytes 31457280 | tf_op jit(solution)/shard_map/gram_schur/pallas_call | solution.py:204
  (24 shorter events, 0.3 us)
Async XLA Ops:
  7.2 1.6 copy-start
  7.2 62.2 %all-gather.7.cloned.1.call-start = ((), (), s32[]{:S(2)}) async-start(), calls=%async_computation.4 | async-start | bytes 2621440 | tf_op jit(solution)/shard_map/all_gather | solution.py:258
  12.7 27.0 %all-to-all-start = ((bf16[32,32,256]{2,1,0:T(8,128)(2,1)}), bf16[32,32,256]{2,1,0:T(8,128)(2,1)S(1)}, u32[]{:S(2)}, u32[]{:S(2)}) async-start(bf16[32,32,256]{2,1,0:T(8,128)(2,1)} %bitcast.26), calls=%async_computation | async-start | bytes 1048576 | tf_op jit(solution)/shard_map/all_to_all | solution.py:260
  22.9 217.1 %all-gather.9.cloned.1.call-start = ((), (), s32[]{:S(2)}) async-start(), calls=%async_computation.5 | async-start | bytes 25952256 | tf_op jit(solution)/shard_map/all_gather | solution.py:274
  110.4 15.3 %collective-permute-start.4 = (f32[32,1280]{1,0:T(8,128)S(1)}, f32[32,1280]{1,0:T(8,128)S(1)}, u32[]{:S(2)}, u32[]{:S(2)}) collective-permute-start(f32[32,1280]{1,0:T(8,128)S(1)} %all_gather.23), channel_id=1, source_target_pairs={{0,32},{32,0},{1,33},{33,1},{2,34},{34,2},{3,35},{35,3},{4,36},{36... | collective-permute-start | bytes 491528 | tf_op jit(solution)/shard_map/ppermute | solution.py:293
  125.8 5.5 %copy-start.3 = (bf16[1024,256]{1,0:T(8,128)(2,1)S(1)}, bf16[1024,256]{1,0:T(8,128)(2,1)}, u32[]{:S(2)}) copy-start(bf16[1024,256]{1,0:T(8,128)(2,1)} %get-tuple-element.13) | copy-start | bytes 1572868
  126.9 47.4 %all-to-all-start.3 = ((f32[4,2,32,1280]{3,2,1,0:T(8,128)}), f32[4,2,32,1280]{3,2,1,0:T(8,128)}, u32[]{:S(2)}, u32[]{:S(2)}) async-start(f32[4,2,32,1280]{3,2,1,0:T(8,128)} %broadcast_in_dim.11), calls=%async_computation.3 | async-start | bytes 2621440 | tf_op jit(solution)/shard_map/all_to_all | solution.py:297
  131.3 38.3 %collective-permute-start = (bf16[1024,256]{1,0:T(8,128)(2,1)S(1)}, bf16[1024,256]{1,0:T(8,128)(2,1)S(1)}, u32[]{:S(2)}, u32[]{:S(2)}) collective-permute-start(bf16[1024,256]{1,0:T(8,128)(2,1)S(1)} %copy-done.3), channel_id=1, source_target_pairs={{0,32},{32,0},{1,33},{33,1},{2,34},{34,2},{3,35},{35,3},{4,36},{36... | collective-permute-start | bytes 1572872 | tf_op jit(solution)/shard_map/ppermute | solution.py:277
  169.6 46.4 %collective-permute-start.3 = (bf16[1024,256]{1,0:T(8,128)(2,1)S(1)}, bf16[1024,256]{1,0:T(8,128)(2,1)S(1)}, u32[]{:S(2)}, u32[]{:S(2)}) collective-permute-start(bf16[1024,256]{1,0:T(8,128)(2,1)S(1)} %collective-permute-done.refs_3_), channel_id=1, source_target_pairs={{0,64},{64,128},{128,192},{192,0},{1,65},{65,129},{129,193},{193,1... | collective-permute-start | bytes 1572872 | tf_op jit(solution)/shard_map/ppermute | solution.py:301
  170.7 45.2 %collective-permute-start.2 = (bf16[1024,256]{1,0:T(8,128)(2,1)S(1)}, bf16[1024,256]{1,0:T(8,128)(2,1)}, u32[]{:S(2)}, u32[]{:S(2)}) collective-permute-start(bf16[1024,256]{1,0:T(8,128)(2,1)S(1)} %collective-permute-done.refs_3_), channel_id=1, source_target_pairs={{0,128},{64,192},{128,0},{192,64},{1,129},{65,193},{129,1},{193,65... | collective-permute-start | bytes 1572872 | tf_op jit(solution)/shard_map/ppermute | solution.py:301
  173.1 42.8 %collective-permute-start.1 = (bf16[1024,256]{1,0:T(8,128)(2,1)S(1)}, bf16[1024,256]{1,0:T(8,128)(2,1)}, u32[]{:S(2)}, u32[]{:S(2)}) collective-permute-start(bf16[1024,256]{1,0:T(8,128)(2,1)S(1)} %collective-permute-done.refs_3_), channel_id=1, source_target_pairs={{0,192},{64,0},{128,64},{192,128},{1,193},{65,1},{129,65},{193,129... | collective-permute-start | bytes 1572872 | tf_op jit(solution)/shard_map/ppermute | solution.py:301
  214.0 1.0 copy-start.1
  240.0 1.2 copy-start.2
Sparse Core Ops, SparseCore 0:
  12.8 37.1 all-gather.6
  69.5 170.3 all-gather.8

commit v9 on v8

--- a/solution.py
+++ b/solution.py
@@ -283,26 +283,25 @@
         ],
         axis=1,
     )
-    part_rows = PANEL // samp
-    left = lax.dynamic_slice_in_dim(mine, samp_index * part_rows, part_rows, 1)
+    xs = lax.axis_size("x")
+    part_rows = PANEL // xs
+    left = lax.dynamic_slice_in_dim(mine, lax.axis_index("x") * part_rows, part_rows, 1)
     partial = dot(left, mine, ((0,), (0,))).reshape(feat, part_rows // feat * PANEL)
     slabs = lax.all_to_all(partial, FEAT, split_axis=0, concat_axis=0, tiled=True)
     held = jnp.concatenate([jnp.sum(slabs, axis=0), moment_part])[None]
     held = lax.all_gather(held, ("zl", "core"), axis=0, tiled=True)
     held = lax.all_gather(held, "y", axis=0, tiled=True)
-    other = lax.ppermute(held, "zh", [(0, 1), (1, 0)])
-    lower = lax.axis_index("zh") == 0
-    pair = jnp.stack([jnp.where(lower, held, other), jnp.where(lower, other, held)])
-    xs = lax.axis_size("x")
+    cut = part_rows // feat * PANEL
+    other = lax.ppermute(held[:, cut:], "zh", [(0, 1), (1, 0)])
+    held = jnp.concatenate([held[:, :cut], held[:, cut:] + other], axis=1)
     table = lax.all_to_all(
-        jnp.broadcast_to(pair[None], (xs,) + pair.shape), "x", split_axis=0, concat_axis=0, tiled=True
+        jnp.broadcast_to(held[None], (xs,) + held.shape), "x", split_axis=0, concat_axis=0, tiled=True
     )
     far = [swapped] + [
         lax.ppermute(swapped, "x", [(i, (i - r) % xs) for i in range(xs)]) for r in range(1, xs)
     ]
-    cut = part_rows // feat * PANEL
     pivot = table[..., :cut].reshape(PANEL, PANEL) / count
-    moments = jnp.sum(table[..., cut:].reshape(samp, feat, width), axis=0) / count
+    moments = jnp.sum(table[..., cut:].reshape(xs, feat, width), axis=0) / count
     inv = inverse_factor(pivot + ridge * jnp.eye(PANEL, dtype=f32))
 
     at = jnp.stack(

time: 280 us -> 277 us (0.989)
  waiting for transfers between devices: 93.5 us -> 85.5 us
  blocking collectives: 69 us -> 73.6 us
    ppermute x1, waiting for transfers between devices: 15.3 us -> 7.68 us  [per_device(): other = lax.ppermute(held[:, cut:], 'zh', [(0, 1), (1, 0)])]
    all_to_all x1, blocking collectives: 17.3 us -> 21.6 us  [per_device(): lax.all_to_all(partial, FEAT, split_axis=0, concat_axis=0, tiled=True)]
where the time goes in v9:
time: 277 us; the launch traced here: 276 us
  waiting for transfers between devices  85.5 us (31%)
  blocking collectives  73.6 us (27%)
  Pallas kernels  64.6 us (23%)
  starting transfers between devices  19.4 us (7%)
  between operations  14.9 us (5%)
  local copies, waits for them, and re-layouts  7.25 us (3%)
  other arithmetic  6.45 us (2%)
  matrix products  4.08 us (1%)
    ppermute x1, waiting for transfers between devices, per_device(): swapped = lax.ppermute(feature, 'zh', [(0, 1), (1, 0)])  38.3 us
    pallas_call x1, Pallas kernels, inverse_factor(): pl.pallas_call(invert_body, out_shape=jax.ShapeDtypeStruct((n, n), f32),...  33.6 us
    pallas_call x1, Pallas kernels, gram_schur(): pl.pallas_call(lambda *refs: gram_body(count, *refs), out_shape=(jax.Shap...  31 us
    all_to_all x1, blocking collectives, per_device(): share = lax.all_to_all(send, SAMP, split_axis=0, concat_axis=0, tiled=True)  29.6 us
    all_gather x1, waiting for transfers between devices, per_device(): gathered = lax.all_gather(share, FEAT)  23.4 us
    all_to_all x1, blocking collectives, per_device(): lax.all_to_all(partial, FEAT, split_axis=0, concat_axis=0, tiled=True)  21.6 us
    all_to_all x1, waiting for transfers between devices, per_device(): lax.all_to_all(feature.reshape(feat, piece, width), FEAT, split_axis=0, c...  16.1 us
    all_gather x1, blocking collectives, per_device(): held = lax.all_gather(held, ('zl', 'core'), axis=0, tiled=True)  11.9 us
  transfers between devices with their start and end apart: 9, of which 4 were waited for; matrix products, arithmetic and copies ran while one was open for 4% of the time, Pallas kernels for 12%

profile of v9, /device:TPU:1, one launch (start us, length us, event | category | flops | bytes accessed | tf_op | source)
XLA Modules:
  0.0 275.8 jit_solution(12620190162590626893)
XLA Ops:
  7.2 0.8 convert_element_type.10
  8.1 0.7 multiply_subtract_fusion
  8.8 3.9 %subtract_reduce_fusion = (f32[256]{0:T(256)S(1)}, bf16[1024,256]{1,0:T(8,128)(2,1)}) fusion(f32[1024]{0:T(1024)S(1)} %multiply_subtract_fusion, f32[256]{0:T(256)} %param.10, f32[1024]{0:T(1024)S(1)} %convert_element_type.10, f32[256]{0:T(256)} %param.9, bf16[1024,1024]{1,0:T(8,128)(2,1)S(1)} %copy-done, bf16[1024,256]{1,0:T(8,128)(2,1)} %param.8), kind=kOutput, calls=%fused_computation.10 | convolution fusion | flops 547880704 | bytes 3156992 | tf_op jit(solution)/shard_map/dot_general | solution.py:248
  12.7 10.2 %all-to-all-start = ((bf16[32,32,256]{2,1,0:T(8,128)(2,1)}), bf16[32,32,256]{2,1,0:T(8,128)(2,1)S(1)}, u32[]{:S(2)}, u32[]{:S(2)}) async-start(bf16[32,32,256]{2,1,0:T(8,128)(2,1)} %bitcast.20), calls=%async_computation | async-start | bytes 1048576 | tf_op jit(solution)/shard_map/all_to_all | solution.py:260
  23.6 16.1 %all-to-all-done = bf16[32,32,256]{2,1,0:T(8,128)(2,1)S(1)} async-done(((bf16[32,32,256]{2,1,0:T(8,128)(2,1)}), bf16[32,32,256]{2,1,0:T(8,128)(2,1)S(1)}, u32[]{:S(2)}, u32[]{:S(2)}) %all-to-all-start) | async-done | bytes 524320 | tf_op jit(solution)/shard_map/all_to_all | solution.py:260
  39.7 0.1 pad_maximum_fusion
  39.8 29.6 %all_to_all.25 = bf16[8,192,256]{2,1,0:T(8,128)(2,1)} all-to-all(bf16[8,192,256]{2,1,0:T(8,128)(2,1)S(1)} %pad_maximum_fusion), channel_id=1, replica_groups=mesh['x'=4,'zh'=2,'y'=4,'zl'=4,'core'=2] {'x','zh'}, dimensions={0} | all-to-all | bytes 1572864 | tf_op jit(solution)/shard_map/all_to_all | solution.py:272
  69.4 1.0 fusion.16
  70.4 0.2 fusion.10
  70.7 0.3 all_to_all.20
  71.0 21.6 %all_to_all.26 = f32[32,1,2048]{2,1,0:T(1,128)S(1)} all-to-all(f32[32,1,2048]{2,1,0:T(1,128)S(1)} %all_to_all.20), channel_id=1, replica_groups=mesh['x'=4,'zh'=2,'y'=4,'zl'=4,'core'=2] {'y','zl','core'}, dimensions={0} | all-to-all | bytes 524288 | tf_op jit(solution)/shard_map/all_to_all | solution.py:290
  92.5 0.2 reduce_sum.28
  92.7 11.9 %all-gather.3 = f32[8,1,2304]{2,1,0:T(1,128)S(1)} all-gather(f32[1,1,2304]{2,1,0:T(1,128)S(1)} %reshape.45), channel_id=4, replica_groups=mesh['x'=4,'zh'=2,'y'=4,'zl'=4,'core'=2] {'zl','core'}, dimensions={0}, use_global_device_ids=true | all-gather | bytes 82944 | tf_op jit(solution)/shard_map/all_gather | solution.py:292
  104.7 10.5 %all_gather.23 = f32[32,2304]{1,0:T(8,128)S(1)} all-gather(f32[8,2304]{1,0:T(8,128)S(1)} %bitcast.23), channel_id=1, replica_groups=mesh['x'=4,'zh'=2,'y'=4,'zl'=4,'core'=2] {'y'}, dimensions={0}, use_global_device_ids=true | all-gather | bytes 368640 | tf_op jit(solution)/shard_map/all_gather | solution.py:293
  115.2 7.7 %collective-permute-done.4 = f32[32,256]{1,0:T(8,128)S(1)} collective-permute-done((f32[32,256]{1,0:T(8,128)S(1)}, f32[32,256]{1,0:T(8,128)S(1)}, u32[]{:S(2)}, u32[]{:S(2)}) %collective-permute-start.4) | collective-permute-done | bytes 32800 | tf_op jit(solution)/shard_map/ppermute | solution.py:295
  122.9 1.1 broadcast_in_dim.11
  124.0 4.3 %all-to-all-start.3 = ((f32[4,32,2304]{2,1,0:T(8,128)}), f32[4,32,2304]{2,1,0:T(8,128)}, u32[]{:S(2)}, u32[]{:S(2)}) async-start(f32[4,32,2304]{2,1,0:T(8,128)} %broadcast_in_dim.11), calls=%async_computation.3 | async-start | bytes 2359296 | tf_op jit(solution)/shard_map/all_to_all | solution.py:297
  128.3 0.1 collective-permute-start
  128.4 0.1 stack.25.refs_0_
  128.5 38.3 %collective-permute-done.refs_3_ = bf16[1024,256]{1,0:T(8,128)(2,1)S(1)} collective-permute-done((bf16[1024,256]{1,0:T(8,128)(2,1)S(1)}, bf16[1024,256]{1,0:T(8,128)(2,1)S(1)}, u32[]{:S(2)}, u32[]{:S(2)}) %collective-permute-start) | collective-permute-done | bytes 524320 | tf_op jit(solution)/shard_map/ppermute | solution.py:277
  166.8 1.2 collective-permute-start.3
  168.0 2.4 collective-permute-start.2
  170.4 1.2 collective-permute-start.1
  171.6 2.4 slice_multiply_fusion
  174.0 2.5 div.16
  176.5 1.3 select_add_fusion.a_ref
  177.8 33.6 %inverse_factor.1.refs_7_ = f32[512,512]{1,0:T(8,128)S(1)} custom-call(f32[512,512]{1,0:T(8,128)S(1)} %select_add_fusion.a_ref), custom_call_target="tpu_custom_call" | custom-call | flops 30000001024 | bytes 2097152 | tf_op jit(solution)/shard_map/inverse_factor/pallas_call | solution.py:104
  211.4 1.0 copy-done.1
  212.4 0.9 slice_reduce_fusion
  213.3 23.4 %all-gather.9.cloned.1.call-done = bf16[256,192,256]{2,1,0:T(8,128)(2,1)} async-done(((bf16[8,192,256]{2,1,0:T(8,128)(2,1)}), bf16[256,192,256]{2,1,0:T(8,128)(2,1)}) %all-gather.9.cloned.1.call-update) | async-done | bytes 25165840 | tf_op jit(solution)/shard_map/all_gather | solution.py:274
  236.7 1.2 copy-done.2
  238.0 31.0 %gram_schur.1 = (f32[1024,256]{1,0:T(8,128)}, f32[1024,512]{1,0:T(8,128)}, f32[1,256]{1,0:T(1,128)}) custom-call(s32[7]{0:T(128)S(1)} %stack.25.refs_0_, bf16[32,8,192,256]{3,2,1,0:T(8,128)(2,1)} %bitcast.25, bf16[4,1024,256]{2,1,0:T(8,128)(2,1)} %bitcast.26, bf16[1024,256]{1,0:T(8,128)(2,1)S(1)} %collective-permute-done.refs_3_, ...), custom_call_target="tpu_custom_call" | custom-call | flops 20000000000 | bytes 31457280 | tf_op jit(solution)/shard_map/gram_schur/pallas_call | solution.py:204
  (26 shorter events, 0.2 us)
Async XLA Ops:
  7.2 1.6 copy-start
  7.2 62.2 %all-gather.7.cloned.1.call-start = ((), (), s32[]{:S(2)}) async-start(), calls=%async_computation.4 | async-start | bytes 2621440 | tf_op jit(solution)/shard_map/all_gather | solution.py:258
  12.7 27.0 %all-to-all-start = ((bf16[32,32,256]{2,1,0:T(8,128)(2,1)}), bf16[32,32,256]{2,1,0:T(8,128)(2,1)S(1)}, u32[]{:S(2)}, u32[]{:S(2)}) async-start(bf16[32,32,256]{2,1,0:T(8,128)(2,1)} %bitcast.20), calls=%async_computation | async-start | bytes 1048576 | tf_op jit(solution)/shard_map/all_to_all | solution.py:260
  22.9 213.9 %all-gather.9.cloned.1.call-start = ((), (), s32[]{:S(2)}) async-start(), calls=%async_computation.5 | async-start | bytes 25952256 | tf_op jit(solution)/shard_map/all_gather | solution.py:274
  115.2 7.7 %collective-permute-start.4 = (f32[32,256]{1,0:T(8,128)S(1)}, f32[32,256]{1,0:T(8,128)S(1)}, u32[]{:S(2)}, u32[]{:S(2)}) collective-permute-start(f32[32,256]{1,0:T(8,128)S(1)} %slice.26), channel_id=1, source_target_pairs={{0,32},{32,0},{1,33},{33,1},{2,34},{34,2},{3,35},{35,3},{4,36},{36... | collective-permute-start | bytes 98312 | tf_op jit(solution)/shard_map/ppermute | solution.py:295
  122.9 5.4 %copy-start.3 = (bf16[1024,256]{1,0:T(8,128)(2,1)S(1)}, bf16[1024,256]{1,0:T(8,128)(2,1)}, u32[]{:S(2)}) copy-start(bf16[1024,256]{1,0:T(8,128)(2,1)} %get-tuple-element.13) | copy-start | bytes 1572868
  124.0 47.6 %all-to-all-start.3 = ((f32[4,32,2304]{2,1,0:T(8,128)}), f32[4,32,2304]{2,1,0:T(8,128)}, u32[]{:S(2)}, u32[]{:S(2)}) async-start(f32[4,32,2304]{2,1,0:T(8,128)} %broadcast_in_dim.11), calls=%async_computation.3 | async-start | bytes 2359296 | tf_op jit(solution)/shard_map/all_to_all | solution.py:297
  128.3 38.5 %collective-permute-start = (bf16[1024,256]{1,0:T(8,128)(2,1)S(1)}, bf16[1024,256]{1,0:T(8,128)(2,1)S(1)}, u32[]{:S(2)}, u32[]{:S(2)}) collective-permute-start(bf16[1024,256]{1,0:T(8,128)(2,1)S(1)} %copy-done.3), channel_id=1, source_target_pairs={{0,32},{32,0},{1,33},{33,1},{2,34},{34,2},{3,35},{35,3},{4,36},{36... | collective-permute-start | bytes 1572872 | tf_op jit(solution)/shard_map/ppermute | solution.py:277
  166.8 46.5 %collective-permute-start.3 = (bf16[1024,256]{1,0:T(8,128)(2,1)S(1)}, bf16[1024,256]{1,0:T(8,128)(2,1)S(1)}, u32[]{:S(2)}, u32[]{:S(2)}) collective-permute-start(bf16[1024,256]{1,0:T(8,128)(2,1)S(1)} %collective-permute-done.refs_3_), channel_id=1, source_target_pairs={{0,64},{64,128},{128,192},{192,0},{1,65},{65,129},{129,193},{193,1... | collective-permute-start | bytes 1572872 | tf_op jit(solution)/shard_map/ppermute | solution.py:301
  168.0 45.3 %collective-permute-start.2 = (bf16[1024,256]{1,0:T(8,128)(2,1)S(1)}, bf16[1024,256]{1,0:T(8,128)(2,1)}, u32[]{:S(2)}, u32[]{:S(2)}) collective-permute-start(bf16[1024,256]{1,0:T(8,128)(2,1)S(1)} %collective-permute-done.refs_3_), channel_id=1, source_target_pairs={{0,128},{64,192},{128,0},{192,64},{1,129},{65,193},{129,1},{193,65... | collective-permute-start | bytes 1572872 | tf_op jit(solution)/shard_map/ppermute | solution.py:301
  170.4 42.9 %collective-permute-start.1 = (bf16[1024,256]{1,0:T(8,128)(2,1)S(1)}, bf16[1024,256]{1,0:T(8,128)(2,1)}, u32[]{:S(2)}, u32[]{:S(2)}) collective-permute-start(bf16[1024,256]{1,0:T(8,128)(2,1)S(1)} %collective-permute-done.refs_3_), channel_id=1, source_target_pairs={{0,192},{64,0},{128,64},{192,128},{1,193},{65,1},{129,65},{193,129... | collective-permute-start | bytes 1572872 | tf_op jit(solution)/shard_map/ppermute | solution.py:301
  211.4 1.0 copy-start.1
  236.7 1.2 copy-start.2
Sparse Core Ops, SparseCore 0:
  12.8 37.1 all-gather.6
  69.5 167.1 all-gather.8
